TPU v7x, 128 devices: a whole 4x4x4 slice. The times are simulated.
128 devices in a mesh: gx: 4 (over y), gy: 32 (over z, x, core).
Axes of the slice: x: 4, y: 4, z: 4, core: 2. Of those that a mesh axis runs over, the one named last changes fastest.
Arguments:
- populations: float32 [19, 128, 256, 256], P(None, 'gx', 'gy'), may hold values from 0.02 to 0.08
- mass: float32 [256, 4096], P('gx', 'gy'), may hold values from 0.2 to 1
- modulus: float32 [256, 4096], P('gx', 'gy'), may hold values from 0.1 to 0.5
- cell_live: int32 [256, 4096], P('gx', 'gy'), may hold values 0 or 1
- stiff_ref: float32 [12, 12], replicated, as said below
- rec_block: int32 [524288], P(('gx', 'gy')), may hold values from 0 to 255
- rec_owner: int32 [524288, 1], P(('gx', 'gy')), may hold values from 0 to 127; in each aligned block of 4096 rows (0 to 4095, 4096 to 8191, ...) at most 64 rows name the same one
- rec_node: int32 [524288], P(('gx', 'gy')), may hold values from 0 to 8191
- rbf_weight: float32 [524288, 256], P(('gx', 'gy')), may hold values from 0 to 2
Outputs:
- populations_next: float32 [19, 128, 256, 256], P(None, 'gx', 'gy')
- displacement: float32 [3, 256, 4096], P(None, 'gx', 'gy')
Inputs may be any that keep to these rules, and one draw needn't show every extreme that they name: `rec_owner`: in the records of one device no owner is named more than 64 times, and every owner is named by some record. `stiff_ref`: symmetric with a positive diagonal that exceeds the sum of magnitudes of each row's other entries.
All inputs are finite; a program needn't handle non-finite values. No bound on the sum of `cell_live` on one device may be relied on, other than what follows from the above.
Results may differ from a plain program's by a relative error of at most 0.0003.
Values sent between devices are 32-bit elements; how exact they have to be, the bound alone decides.
No kernel may reach another device: no remote copies, remote signals or barrier semaphores. Data moves between devices by JAX's collectives and lax.ppermute only.
A program may use at most 128 MiB of HBM per device.

v0:
```python
import jax
import jax.numpy as jnp
from jax import lax
from jax.experimental import pallas as pl
from jax.experimental.pallas import tpu as pltpu
from jax.sharding import PartitionSpec as P

F32 = jnp.float32
BF16 = jnp.bfloat16
ALL = ("gx", "gy")
VMEM_LIMIT = 48 * 1024 * 1024

DIRS = (
    (0, 0, 0),
    (1, 0, 0),
    (-1, 0, 0),
    (0, 1, 0),
    (0, -1, 0),
    (0, 0, 1),
    (0, 0, -1),
    (1, 1, 0),
    (-1, -1, 0),
    (1, -1, 0),
    (-1, 1, 0),
    (1, 0, 1),
    (-1, 0, -1),
    (1, 0, -1),
    (-1, 0, 1),
    (0, 1, 1),
    (0, -1, -1),
    (0, 1, -1),
    (0, -1, 1),
)
WEIGHTS = (1.0 / 3.0,) + (1.0 / 18.0,) * 6 + (1.0 / 36.0,) * 12
RATE = 1.25
COUPLING = 0.1
XP = tuple(q for q in range(19) if DIRS[q][0] == 1)
XM = tuple(q for q in range(19) if DIRS[q][0] == -1)
YP = tuple(q for q in range(19) if DIRS[q][1] == 1)
YM = tuple(q for q in range(19) if DIRS[q][1] == -1)

R = 4096
NB = 256
NK = 256
ND = 128
CAP = 64
NU, NV = 64, 128
RB = 512
EU, EV = 72, 256


def iota(shape, dim):
    return lax.broadcasted_iota(jnp.int32, shape, dim)


def halves(x):
    high = x.astype(BF16).astype(F32)
    return high, x - high


def combine(fields, direction):
    total = None
    for axis in range(3):
        if direction[axis] != 0:
            term = fields[axis] if direction[axis] == 1 else -fields[axis]
            total = term if total is None else total + term
    return total


def dot_t(a, b):
    return lax.dot_general(a, b, (((1,), (1,)), ((), ())), preferred_element_type=F32)


def dot(a, b):
    return lax.dot_general(a, b, (((1,), (0,)), ((), ())), preferred_element_type=F32)


def load_kernel(pop_ref, w_ref, blk_ref, own_ref, node_ref, send_ref, rank_ref, m_ref, tri_ref, carry_ref):
    step = pl.program_id(0)

    @pl.when(step == 0)
    def _():
        def rows_of(i, _):
            rows = pl.ds(pl.multiple_of(i * 16, 16), 16)
            pops = [pop_ref[q, rows, :] for q in range(1, 19)]
            for axis in range(3):
                total = None
                for q in range(1, 19):
                    if DIRS[q][axis] != 0:
                        term = pops[q - 1] if DIRS[q][axis] == 1 else -pops[q - 1]
                        total = term if total is None else total + term
                high = total.astype(BF16)
                low = (total - high.astype(F32)).astype(BF16)
                at = pl.ds(pl.multiple_of(axis * NB + i * 16, 16), 16)
                m_ref[at, 0:NK] = high
                m_ref[at, NK : 2 * NK] = low
                m_ref[at, 2 * NK : 3 * NK] = high
            return 0

        lax.fori_loop(0, NB // 16, rows_of, 0)
        before = (iota((256, 256), 0) < iota((256, 256), 1)).astype(F32)
        tri_ref[:, 0:256] = before.astype(BF16)
        tri_ref[:, 256:512] = jnp.ones((256, 256), BF16)
        carry_ref[...] = jnp.zeros_like(carry_ref)
        send_ref[...] = jnp.zeros_like(send_ref)

    w = w_ref[...]
    w_high = w.astype(BF16)
    w_low = (w - w_high.astype(F32)).astype(BF16)
    w_all = jnp.concatenate([w_high, w_high, w_low], axis=1)
    at_block = iota((NB, RB), 0) == blk_ref[...]
    values = []
    for axis in range(3):
        product = dot_t(m_ref[axis * NB : (axis + 1) * NB, :], w_all)
        values.append(jnp.sum(jnp.where(at_block, product, 0.0), axis=0, keepdims=True))
    values.append(node_ref[...].astype(F32))

    named = iota((ND, RB), 0) == own_ref[...]
    named_bf = jnp.where(named, 1.0, 0.0).astype(BF16)
    ranks = []
    for part in range(RB // 256):
        cols = slice(part * 256, (part + 1) * 256)
        counts = dot(named_bf[:, cols], tri_ref[...])
        upto = counts[:, 0:256] + carry_ref[...]
        ranks.append(jnp.sum(jnp.where(named[:, cols], upto, 0.0), axis=0, keepdims=True))
        carry_ref[...] += counts[:, 256:512]
    rank = jnp.concatenate(ranks, axis=1).astype(jnp.int32)
    rank_ref[...] = rank
    in_slot = iota((CAP, RB), 0) == rank
    highs, lows = [], []
    for value in values:
        high, low = halves(value)
        highs.append(jnp.where(in_slot, high, 0.0).astype(BF16))
        lows.append(jnp.where(in_slot, low, 0.0).astype(BF16))
    packed = jnp.concatenate([jnp.concatenate(highs, axis=0), jnp.concatenate(lows, axis=0)], axis=1)
    send_ref[...] += dot_t(jnp.concatenate([named_bf, named_bf], axis=1), packed)


def loads_to_send(pops, weights, block_row, owner_row, node_row):
    row_spec = pl.BlockSpec((1, RB), lambda i: (0, i))
    return pl.pallas_call(
        load_kernel,
        grid=(R // RB,),
        in_specs=[
            pl.BlockSpec((19, NB, NK), lambda i: (0, 0, 0)),
            pl.BlockSpec((RB, NK), lambda i: (i, 0)),
            row_spec,
            row_spec,
            row_spec,
        ],
        out_specs=[pl.BlockSpec((ND, 4 * CAP), lambda i: (0, 0)), row_spec],
        out_shape=[
            jax.ShapeDtypeStruct((ND, 4 * CAP), F32),
            jax.ShapeDtypeStruct((1, R), jnp.int32),
        ],
        scratch_shapes=[
            pltpu.VMEM((3 * NB, 3 * NK), BF16),
            pltpu.VMEM((256, 512), BF16),
            pltpu.VMEM((ND, 256), F32),
        ],
        compiler_params=pltpu.CompilerParams(vmem_limit_bytes=VMEM_LIMIT),
        name="loads",
    )(pops, weights, block_row, owner_row, node_row)


def collide_kernel(pop_ref, read_ref, xp_ref, xm_ref, yp_ref, ym_ref):
    def line(x, _):
        rows = pl.ds(pl.multiple_of(x * 8, 8), 8)
        pops = [pop_ref[q, rows, :] for q in range(19)]
        density = pops[0]
        for q in range(1, 19):
            density = density + pops[q]
        inverse = 1.0 / density
        velocity = []
        for axis in range(3):
            total = None
            for q in range(1, 19):
                if DIRS[q][axis] != 0:
                    term = pops[q] if DIRS[q][axis] == 1 else -pops[q]
                    total = term if total is None else total + term
            velocity.append(total * inverse)
        squared = velocity[0] * velocity[0] + velocity[1] * velocity[1] + velocity[2] * velocity[2]
        base = 1.0 - 1.5 * squared
        for q in range(19):
            cx, cy, cz = DIRS[q]
            along = combine(velocity, DIRS[q])
            bracket = base if along is None else base + along * (3.0 + 4.5 * along)
            relaxed = pops[q] - RATE * (pops[q] - (WEIGHTS[q] * density) * bracket)
            if cz != 0:
                relaxed = pltpu.roll(relaxed, 1 if cz == 1 else NK - 1, 1)
            if cy != 0:
                relaxed = pltpu.roll(relaxed, 1 if cy == 1 else 7, 0)
            if cy == 1:
                yp_ref[YP.index(q), pl.ds(lax.rem(x + cx + 32, 32), 1), :] = relaxed[0:1, :]
            if cy == -1:
                ym_ref[YM.index(q), pl.ds(lax.rem(x + cx + 32, 32), 1), :] = relaxed[7:8, :]
            to = pl.ds(pl.multiple_of(lax.rem(x + cx + 32, 32) * 8, 8), 8)
            read_ref[q, to, :] = relaxed
        return 0

    lax.fori_loop(0, 32, line, 0)
    for i, q in enumerate(XP):
        xp_ref[i] = read_ref[q, 0:8, :]
    for i, q in enumerate(XM):
        xm_ref[i] = read_ref[q, NB - 8 : NB, :]


def collide_and_run(pops):
    return pl.pallas_call(
        collide_kernel,
        out_shape=[
            jax.ShapeDtypeStruct((19, NB, NK), F32),
            jax.ShapeDtypeStruct((5, 8, NK), F32),
            jax.ShapeDtypeStruct((5, 8, NK), F32),
            jax.ShapeDtypeStruct((5, 32, NK), F32),
            jax.ShapeDtypeStruct((5, 32, NK), F32),
        ],
        compiler_params=pltpu.CompilerParams(vmem_limit_bytes=VMEM_LIMIT),
        name="collide",
    )(pops)


def node_rows(recv_t):
    node = recv_t[3 * CAP : 4 * CAP, :].astype(jnp.int32)
    return node >> 7, node & 127


def force_kernel(recv_ref, mass_ref, mod_ref, live_ref, f_ref, low_ref, high_ref, u_ref, v_ref, hl_ref):
    recv_t = recv_ref[...].T
    u_ref[...], v_ref[...] = node_rows(recv_t)
    high, low = halves(recv_t[0 : 3 * CAP, :])
    hl_ref[0 : 3 * CAP, :] = high
    hl_ref[3 * CAP : 6 * CAP, :] = low
    u_of = iota((NU, ND), 0)
    v_of = iota((NV, ND), 0)

    def chunk(i, acc):
        at = pl.multiple_of(i * 8, 8)
        u8 = u_ref[pl.ds(at, 8), :]
        v8 = v_ref[pl.ds(at, 8), :]
        vals = [hl_ref[pl.ds(pl.multiple_of(part * CAP + at, 8), 8), :] for part in range(6)]
        lhs, rhs = [], []
        for r in range(8):
            here = u_of == u8[r : r + 1, :]
            lhs.append(
                jnp.concatenate(
                    [jnp.where(here, vals[part][r : r + 1, :], 0.0).astype(BF16) for part in range(6)], axis=0
                )
            )
            rhs.append(jnp.where(v_of == v8[r : r + 1, :], 1.0, 0.0).astype(BF16))
        return acc + dot_t(jnp.concatenate(lhs, axis=1), jnp.concatenate(rhs, axis=1))

    acc = lax.fori_loop(0, CAP // 8, chunk, jnp.zeros((6 * NU, NV), F32))
    fields = [acc[c * NU : (c + 1) * NU, :] + acc[(3 + c) * NU : (4 + c) * NU, :] for c in range(3)]
    for c in range(3):
        f_ref[c] = fields[c]
    fields = fields + [mass_ref[...], mod_ref[...], live_ref[...].astype(F32)]
    low_ref[...] = jnp.zeros_like(low_ref)
    high_ref[...] = jnp.zeros_like(high_ref)
    for i, field in enumerate(fields):
        low_ref[i : i + 1, :] = field[NU - 1 : NU, :]
        high_ref[2 * i : 2 * i + 2, :] = field[0:2, :]


def force_of(recv, mass, modulus, live):
    return pl.pallas_call(
        force_kernel,
        out_shape=[
            jax.ShapeDtypeStruct((3, NU, NV), F32),
            jax.ShapeDtypeStruct((8, 128), F32),
            jax.ShapeDtypeStruct((16, 128), F32),
        ],
        scratch_shapes=[
            pltpu.VMEM((CAP, ND), jnp.int32),
            pltpu.VMEM((CAP, ND), jnp.int32),
            pltpu.VMEM((6 * CAP, ND), F32),
        ],
        compiler_params=pltpu.CompilerParams(vmem_limit_bytes=VMEM_LIMIT),
        name="force",
    )(recv, mass, modulus, live)


def rim_tile(i, low_ref, high_ref):
    sub = iota((8, 128), 0)
    tile = jnp.where(sub == 0, high_ref[2 * i : 2 * i + 1, :], 0.0)
    tile = jnp.where(sub == 1, high_ref[2 * i + 1 : 2 * i + 2, :], tile)
    return jnp.where(sub == 7, low_ref[i : i + 1, :], tile)


def rim_kernel(f_ref, mass_ref, mod_ref, live_ref, low_ref, high_ref, to_low_ref, to_high_ref):
    fields = [f_ref[0], f_ref[1], f_ref[2], mass_ref[...], mod_ref[...], live_ref[...].astype(F32)]
    to_low_ref[...] = jnp.zeros_like(to_low_ref)
    to_high_ref[...] = jnp.zeros_like(to_high_ref)
    for i, field in enumerate(fields):
        whole = jnp.concatenate(
            [field, rim_tile(i, low_ref, high_ref), jnp.zeros((128 - EU, 128), F32)], axis=0
        )
        turned = whole.T
        to_low_ref[i : i + 1, :] = turned[127:128, :]
        to_high_ref[2 * i : 2 * i + 2, :] = turned[0:2, :]


def rim_columns(force, mass, modulus, live, low, high):
    return pl.pallas_call(
        rim_kernel,
        out_shape=[jax.ShapeDtypeStruct((8, 128), F32), jax.ShapeDtypeStruct((16, 128), F32)],
        name="rim",
    )(force, mass, modulus, live, low, high)


def shell_kernel(
    stiff_ref, f_ref, mass_ref, mod_ref, live_ref, ulow_ref, uhigh_ref, vlow_ref, vhigh_ref, recv_ref,
    y_ref, ret_ref,
    e_ref, c_ref, g_ref, y_ext_ref, fy_ref, u_ref, v_ref, rt_ref,
):
    fields = [f_ref[0], f_ref[1], f_ref[2], mass_ref[...], mod_ref[...], live_ref[...].astype(F32)]
    sub = iota((8, 128), 0)
    for i, field in enumerate(fields):
        e_ref[i, 0:NU, 0:NV] = field
        e_ref[i, NU:EU, 0:NV] = rim_tile(i, ulow_ref, uhigh_ref)
        first = jnp.where(sub == 0, vhigh_ref[2 * i : 2 * i + 1, :], 0.0)
        first = jnp.where(sub == 1, vhigh_ref[2 * i + 1 : 2 * i + 2, :], first)
        last = jnp.where(sub == 7, vlow_ref[i : i + 1, :], 0.0)
        side = jnp.concatenate([first, jnp.zeros((112, 128), F32), last], axis=0).T
        e_ref[i, :, NV:EV] = side[0:EU, :]

    def up(x):
        return pltpu.roll(x, EU - 1, 0)

    def right(x):
        return pltpu.roll(x, EV - 1, 1)

    def down(x):
        return pltpu.roll(x, 1, 0)

    def left(x):
        return pltpu.roll(x, 1, 1)

    mod = e_ref[4]
    mod = mod + up(mod)
    e_ref[5] = e_ref[5] * (mod + right(mod)) * 0.25
    for c in range(3):
        field = e_ref[c]
        moved = up(field)
        c_ref[c] = field
        c_ref[3 + c] = moved
        c_ref[6 + c] = right(field)
        c_ref[9 + c] = right(moved)

    def cells(t, _):
        rows = pl.ds(pl.multiple_of(t * 8, 8), 8)
        corner = [c_ref[k, rows, :] for k in range(12)]
        scale = e_ref[5, rows, :]
        for k in range(12):
            total = stiff_ref[k, 0] * corner[0]
            for m in range(1, 12):
                total = total + stiff_ref[k, m] * corner[m]
            g_ref[k, rows, :] = scale * total
        return 0

    lax.fori_loop(0, EU // 8, cells, 0)
    mass = e_ref[3]
    for c in range(3):
        spread = g_ref[c] + down(g_ref[3 + c])
        beside = g_ref[6 + c] + down(g_ref[9 + c])
        y_ext_ref[c] = mass * e_ref[c] + spread + left(beside)
        y_ref[c] = y_ext_ref[c, 0:NU, 0:NV]
    for c in range(3):
        field = y_ext_ref[c]
        moved = up(field)
        c_ref[c] = field
        c_ref[3 + c] = moved
        c_ref[6 + c] = right(field)
        c_ref[9 + c] = right(moved)

    def energy(t, sums):
        rows = pl.ds(pl.multiple_of(t * 8, 8), 8)
        corner = [c_ref[k, rows, 0:NV] for k in range(12)]
        total = None
        for k in range(12):
            inner = stiff_ref[k, 0] * corner[0]
            for m in range(1, 12):
                inner = inner + stiff_ref[k, m] * corner[m]
            total = corner[k] * inner if total is None else total + corner[k] * inner
        m3 = e_ref[5, rows, 0:NV] * total
        m0, m1, m2 = None, None, None
        for c in range(3):
            f = e_ref[c, rows, 0:NV]
            y = corner[c]
            m0 = f * f if m0 is None else m0 + f * f
            m1 = f * y if m1 is None else m1 + f * y
            m2 = y * y if m2 is None else m2 + y * y
        m3 = m3 + e_ref[3, rows, 0:NV] * m2
        return tuple(s + m for s, m in zip(sums, (m0, m1, m2, m3)))

    zero = jnp.zeros((8, NV), F32)
    sums = lax.fori_loop(0, NU // 8, energy, (zero, zero, zero, zero))
    lane = iota((1, 128), 1)
    moments = jnp.zeros((1, 128), F32)
    for i in range(4):
        whole = jnp.sum(jnp.sum(sums[i], axis=0, keepdims=True), axis=1, keepdims=True)
        moments = jnp.where(lane == i, whole, moments)

    for c in range(3):
        for part, field in ((c, f_ref[c]), (3 + c, y_ref[c])):
            high = field.astype(BF16)
            fy_ref[part * NU : (part + 1) * NU, 0:NV] = high
            fy_ref[part * NU : (part + 1) * NU, NV : 2 * NV] = (field - high.astype(F32)).astype(BF16)
    u_ref[...], v_ref[...] = node_rows(recv_ref[...].T)
    u_of = iota((NU, ND), 0)
    v_of = iota((NV, ND), 0)

    def chunk(i, _):
        at = pl.multiple_of(i * 8, 8)
        u8 = u_ref[pl.ds(at, 8), :]
        v8 = v_ref[pl.ds(at, 8), :]
        rhs = jnp.concatenate(
            [jnp.where(v_of == v8[r : r + 1, :], 1.0, 0.0).astype(BF16) for r in range(8)], axis=1
        )
        picked = dot(fy_ref[...], jnp.concatenate([rhs, rhs], axis=0))
        tiles = [jnp.zeros((8, ND), F32) for _ in range(6)]
        for r in range(8):
            here = u_of == u8[r : r + 1, :]
            for part in range(6):
                block = picked[part * NU : (part + 1) * NU, r * ND : (r + 1) * ND]
                row = jnp.sum(jnp.where(here, block, 0.0), axis=0, keepdims=True)
                tiles[part] = jnp.where(sub == r, row, tiles[part])
        for part in range(6):
            rt_ref[pl.ds(pl.multiple_of(part * CAP + at, 8), 8), :] = tiles[part]
        return 0

    lax.fori_loop(0, CAP // 8, chunk, 0)
    ret_ref[:, 0 : 6 * CAP] = rt_ref[...].T
    ret_ref[:, 6 * CAP : 8 * CAP] = jnp.broadcast_to(moments, (ND, 128))


def shell_of(stiff, force, mass, modulus, live, ulow, uhigh, vlow, vhigh, recv):
    vmem = pl.BlockSpec(memory_space=pltpu.VMEM)
    return pl.pallas_call(
        shell_kernel,
        in_specs=[pl.BlockSpec(memory_space=pltpu.SMEM)] + [vmem] * 9,
        out_specs=[vmem, vmem],
        out_shape=[
            jax.ShapeDtypeStruct((3, NU, NV), F32),
            jax.ShapeDtypeStruct((ND, 8 * CAP), F32),
        ],
        scratch_shapes=[
            pltpu.VMEM((6, EU, EV), F32),
            pltpu.VMEM((12, EU, EV), F32),
            pltpu.VMEM((12, EU, EV), F32),
            pltpu.VMEM((3, EU, EV), F32),
            pltpu.VMEM((6 * NU, 2 * NV), BF16),
            pltpu.VMEM((CAP, ND), jnp.int32),
            pltpu.VMEM((CAP, ND), jnp.int32),
            pltpu.VMEM((6 * CAP, ND), F32),
        ],
        compiler_params=pltpu.CompilerParams(vmem_limit_bytes=VMEM_LIMIT),
        name="shell",
    )(stiff, force, mass, modulus, live, ulow, uhigh, vlow, vhigh, recv)


RSTEPS = R // RB
XS = 4
OSTEPS = 32 // XS


def next_kernel(
    pq_ref, back_ref, w_ref, blk_ref, own_ref, rank_ref, f_ref, y_ref, read_ref, xp_ref, xm_ref, yp_ref, ym_ref,
    next_ref, disp_ref,
    x_ref, force_ref,
):
    step = pl.program_id(0)

    @pl.when(step == 0)
    def _():
        p = pq_ref[0]
        q = pq_ref[1]
        back = p * back_ref[:, 0 : 3 * CAP] + q * back_ref[:, 3 * CAP : 6 * CAP]
        turned = back.T * COUPLING
        high = turned.astype(BF16)
        x_ref[:, 0:ND] = high
        x_ref[:, ND : 2 * ND] = (turned - high.astype(F32)).astype(BF16)
        disp_ref[...] = p * f_ref[...] + q * y_ref[...]
        force_ref[...] = jnp.zeros_like(force_ref)

    @pl.when(step < RSTEPS)
    def _():
        named = jnp.where(iota((ND, RB), 0) == own_ref[...], 1.0, 0.0).astype(BF16)
        picked = dot(x_ref[...], jnp.concatenate([named, named], axis=0))
        in_slot = iota((CAP, RB), 0) == rank_ref[...]
        at_block = iota((NB, RB), 0) == blk_ref[...]
        w = w_ref[...]
        w_high = w.astype(BF16)
        w_low = (w - w_high.astype(F32)).astype(BF16)
        w_all = jnp.concatenate([w_high, w_high, w_low], axis=0)
        for c in range(3):
            moved = jnp.sum(
                jnp.where(in_slot, picked[c * CAP : (c + 1) * CAP, :], 0.0), axis=0, keepdims=True
            )
            high, low = halves(moved)
            high = jnp.where(at_block, high, 0.0).astype(BF16)
            low = jnp.where(at_block, low, 0.0).astype(BF16)
            force_ref[c * NB : (c + 1) * NB, :] += dot(jnp.concatenate([high, low, high], axis=1), w_all)

    @pl.when(step >= RSTEPS)
    def _():
        slab = step - RSTEPS
        sub = iota((8, NK), 0)
        for xx in range(XS):
            x = slab * XS + xx
            forcing = [
                force_ref[pl.ds(pl.multiple_of(c * NB + x * 8, 8), 8), :] for c in range(3)
            ]
            for q in range(19):
                cx, cy, _ = DIRS[q]
                value = read_ref[q, xx * 8 : (xx + 1) * 8, :]
                if cx == 1 and xx == 0:
                    value = jnp.where(x == 0, xp_ref[XP.index(q)], value)
                if cx == -1 and xx == XS - 1:
                    value = jnp.where(x == 31, xm_ref[XM.index(q)], value)
                if cy == 1:
                    value = jnp.where(sub == 0, yp_ref[YP.index(q), pl.ds(x, 1), :], value)
                if cy == -1:
                    value = jnp.where(sub == 7, ym_ref[YM.index(q), pl.ds(x, 1), :], value)
                along = combine(forcing, DIRS[q])
                if along is not None:
                    value = value + (3.0 * WEIGHTS[q]) * along
                next_ref[q, xx * 8 : (xx + 1) * 8, :] = value


def outputs_of(pq, back, weights, block_row, owner_row, rank_row, force, image, read, xp, xm, yp, ym):
    def record(i):
        return jnp.minimum(i, RSTEPS - 1)

    def slab(i):
        return jnp.maximum(i - RSTEPS, 0)

    row_spec = pl.BlockSpec((1, RB), lambda i: (0, record(i)))
    patch = pl.BlockSpec((3, NU, NV), lambda i: (0, 0, 0))
    lines = pl.BlockSpec((19, XS * 8, NK), lambda i: (0, slab(i), 0))
    x_face = pl.BlockSpec((5, 8, NK), lambda i: (0, 0, 0))
    y_face = pl.BlockSpec((5, 32, NK), lambda i: (0, 0, 0))
    return pl.pallas_call(
        next_kernel,
        grid=(RSTEPS + OSTEPS,),
        in_specs=[
            pl.BlockSpec(memory_space=pltpu.SMEM),
            pl.BlockSpec((ND, 8 * CAP), lambda i: (0, 0)),
            pl.BlockSpec((RB, NK), lambda i: (record(i), 0)),
            row_spec,
            row_spec,
            row_spec,
            patch,
            patch,
            lines,
            x_face,
            x_face,
            y_face,
            y_face,
        ],
        out_specs=[lines, patch],
        out_shape=[
            jax.ShapeDtypeStruct((19, NB, NK), F32),
            jax.ShapeDtypeStruct((3, NU, NV), F32),
        ],
        scratch_shapes=[
            pltpu.VMEM((3 * CAP, 2 * ND), BF16),
            pltpu.VMEM((3 * NB, NK), F32),
        ],
        compiler_params=pltpu.CompilerParams(vmem_limit_bytes=VMEM_LIMIT),
        name="outputs",
    )(pq, back, weights, block_row, owner_row, rank_row, force, image, read, xp, xm, yp, ym)


def pass_on(x, axis, shift):
    count = lax.axis_size(axis)
    return lax.ppermute(x, axis, [(i, (i + shift) % count) for i in range(count)])


def padded(field):
    for axis, dim in (("gx", 1), ("gy", 2)):
        size = field.shape[dim]
        head = lax.slice_in_dim(field, 0, 1, axis=dim)
        tail = lax.slice_in_dim(field, size - 1, size, axis=dim)
        field = jnp.concatenate([pass_on(tail, axis, 1), field, pass_on(head, axis, -1)], axis=dim)
    return field


def operate(field, mass, modulus, live, stiff):
    static = padded(jnp.stack([modulus, live.astype(F32)]))
    wide = padded(field)

    def corners(a):
        return a[..., :-1, :-1], a[..., 1:, :-1], a[..., :-1, 1:], a[..., 1:, 1:]

    c0, c1, c2, c3 = corners(static[0])
    scale = static[1, :-1, :-1] * (c0 + c1 + c2 + c3) * 0.25
    vector = jnp.concatenate(corners(wide), axis=0)
    result = scale[None] * jnp.einsum("kl,lab->kab", stiff, vector, precision=lax.Precision.HIGHEST)
    return (
        mass[None] * field
        + result[0:3, 1:, 1:]
        + result[3:6, :-1, 1:]
        + result[6:9, 1:, :-1]
        + result[9:12, :-1, :-1]
    )


def per_device(populations, mass, modulus, live, stiff, rec_block, rec_owner, rec_node, weights):
    pops = populations.reshape(19, NB, NK)
    block_row = rec_block.reshape(1, R)
    owner_row = rec_owner.reshape(1, R)
    node_row = rec_node.reshape(1, R)

    send, rank_row = loads_to_send(pops, weights, block_row, owner_row, node_row)
    recv = lax.all_to_all(send, ALL, 0, 0, tiled=True)

    read, xp, xm, yp, ym = collide_and_run(pops)
    xp = pass_on(xp, "gx", 1)
    xm = pass_on(xm, "gx", -1)
    yp = yp.at[YP.index(7), 0].set(xp[XP.index(7), 0]).at[YP.index(10), 31].set(xm[XM.index(10), 0])
    ym = ym.at[YM.index(9), 0].set(xp[XP.index(9), 7]).at[YM.index(8), 31].set(xm[XM.index(8), 7])
    yp = pass_on(yp, "gy", 1)
    ym = pass_on(ym, "gy", -1)

    force, low, high = force_of(recv, mass, modulus, live)
    ulow = pass_on(low, "gx", 1)
    uhigh = pass_on(high, "gx", -1)
    low, high = rim_columns(force, mass, modulus, live, ulow, uhigh)
    vlow = pass_on(low, "gy", 1)
    vhigh = pass_on(high, "gy", -1)
    image, ret = shell_of(stiff, force, mass, modulus, live, ulow, uhigh, vlow, vhigh, recv)
    back = lax.all_to_all(ret, ALL, 0, 0, tiled=True)

    moments = jnp.sum(back[:, 6 * CAP : 6 * CAP + 4], axis=0)
    m0, m1, m2, m3 = moments[0], moments[1], moments[2], moments[3]
    first = m0 / m1
    left_over = first * first * m2 - m0
    ratio = left_over / m0
    gain = 1.0 + ratio
    curve = gain * gain * m1 - 2.0 * gain * first * m2 + first * first * m3
    sound = (
        (left_over > 1e-3 * m0)
        & (curve > 1e-2 * gain * gain * m1)
        & (curve < 1e30)
        & (m1 > 1e-30)
        & (m0 > 1e-30)
    )

    def quick(_):
        return ratio, left_over / curve

    def careful(operands):
        force, image, mass, modulus, live, stiff = operands
        residual = force - first * image
        norm = lax.psum(jnp.sum(residual * residual), ALL)
        ratio = norm / m0
        direction = residual + ratio * force
        along = operate(direction, mass, modulus, live, stiff)
        return ratio, norm / lax.psum(jnp.sum(direction * along), ALL)

    ratio, second = lax.cond(sound, quick, careful, (force, image, mass, modulus, live, stiff))
    pq = jnp.stack([first + second * (1.0 + ratio), -(first * second)])

    populations_next, displacement = outputs_of(
        pq, back, weights, block_row, owner_row, rank_row, force, image, read, xp, xm, yp, ym
    )
    return populations_next.reshape(19, 32, 8, NK), displacement


def solution(mesh):
    return jax.shard_map(
        per_device,
        mesh=mesh,
        in_specs=(
            P(None, "gx", "gy", None),
            P("gx", "gy"),
            P("gx", "gy"),
            P("gx", "gy"),
            P(),
            P(ALL),
            P(ALL, None),
            P(ALL),
            P(ALL, None),
        ),
        out_specs=(P(None, "gx", "gy", None), P(None, "gx", "gy")),
        check_vma=False,
    )
```

profile of v0, /device:TPU:1, one launch (start us, length us, event | category | flops | bytes accessed | tf_op | source)
XLA Modules:
  0.0 120.1 jit_solution(11029844571902022567)
XLA Ops:
  0.6 0.0 copy-start
  0.6 2.2 %copy-done = f32[4096,256]{1,0:T(8,128)S(1)} copy-done((f32[4096,256]{1,0:T(8,128)S(1)}, f32[4096,256]{1,0:T(8,128)}, u32[]{:S(2)}) %copy-start) | copy-done | bytes 4194328
  2.8 0.7 copy-done.3
  3.5 0.7 copy-done.5
  4.3 0.7 copy-done.9
  5.0 14.0 %loads.1 = (f32[128,256]{1,0:T(8,128)S(1)}, s32[1,4096]{1,0:T(1,128)S(1)}) custom-call(f32[19,256,256]{2,1,0:T(8,128)} %bitcast.44, f32[4096,256]{1,0:T(8,128)S(1)} %copy-done, s32[1,4096]{1,0:T(1,128)S(1)} %bitcast.39, s32[1,4096]{1,0:T(1,128)S(1)} %bitcast.41, s32[1,4096]{1,0:T(1,128)S(1)} %bitcast.43), custom_call_target="tpu_custom_call" | custom-call | tf_op jit(solution)/shard_map/loads/pallas_call | solution.py:141
  19.0 0.8 copy.30
  19.7 11.5 %all-to-all-start = ((f32[128,1,256]{2,1,0:T(1,128)}), f32[128,1,256]{2,1,0:T(1,128)S(1)}, u32[]{:S(2)}, u32[]{:S(2)}) async-start(f32[128,1,256]{2,1,0:T(1,128)} %copy.30), calls=%async_computation | async-start | bytes 262144 | tf_op jit(solution)/shard_map/all_to_all | solution.py:616
  31.2 0.0 copy-start.12
  31.3 0.0 copy-start.13
  31.3 0.0 copy-start.14
  31.3 0.0 copy-start.15
  31.3 7.1 %collide.1 = (f32[19,256,256]{2,1,0:T(8,128)S(1)}, f32[5,8,256]{2,1,0:T(8,128)S(1)}, f32[5,8,256]{2,1,0:T(8,128)S(1)}, f32[5,32,256]{2,1,0:T(8,128)S(1)}, f32[5,32,256]{2,1,0:T(8,128)S(1)}) custom-call(f32[19,256,256]{2,1,0:T(8,128)} %bitcast.45), custom_call_target="tpu_custom_call" | custom-call | tf_op jit(solution)/shard_map/collide/pallas_call | solution.py:209
  38.4 2.2 %copy-done.2 = f32[19,256,256]{2,1,0:T(8,128)} copy-done((f32[19,256,256]{2,1,0:T(8,128)}, f32[19,256,256]{2,1,0:T(8,128)S(1)}, u32[]{:S(2)}) %copy-start.2) | copy-done | bytes 4980760
  40.7 1.4 %collective-permute-start.12 = (f32[5,8,256]{2,1,0:T(8,128)S(1)}, f32[5,8,256]{2,1,0:T(8,128)S(1)}, u32[]{:S(2)}, u32[]{:S(2)}) collective-permute-start(f32[5,8,256]{2,1,0:T(8,128)S(1)} %get-tuple-element.113), channel_id=1, source_target_pairs={{0,32},{32,64},{64,96},{96,0},{1,33},{33,65},{65,97},{97,1},{2,34}... | collective-permute-start | bytes 122888 | tf_op jit(solution)/shard_map/ppermute | solution.py:577
  42.1 0.0 all-to-all-done
  42.1 3.2 %force.1 = (f32[3,64,128]{2,1,0:T(8,128)S(1)}, f32[8,128]{1,0:T(8,128)S(1)}, f32[16,128]{1,0:T(8,128)S(1)}) custom-call(f32[128,256]{1,0:T(8,128)S(1)} %bitcast.35, f32[64,128]{1,0:T(8,128)S(1)} %copy-done.12, f32[64,128]{1,0:T(8,128)S(1)} %copy-done.13, s32[64,128]{1,0:T(8,128)S(1)} %copy-done.14), custom_call_target="tpu_custom_call" | custom-call | tf_op jit(solution)/shard_map/force/pallas_call | solution.py:266
  45.4 1.4 %collective-permute-start.9 = (f32[16,128]{1,0:T(8,128)S(1)}, f32[16,128]{1,0:T(8,128)S(1)}, u32[]{:S(2)}, u32[]{:S(2)}) collective-permute-start(f32[16,128]{1,0:T(8,128)S(1)} %get-tuple-element.104), channel_id=1, source_target_pairs={{0,96},{32,0},{64,32},{96,64},{1,97},{33,1},{65,33},{97,65},{2,98}... | collective-permute-start | bytes 24584 | tf_op jit(solution)/shard_map/ppermute | solution.py:577
  46.7 0.2 collective-permute-start.8
  46.9 3.5 %collective-permute-done.8.low_ref.ulow_ref = f32[8,128]{1,0:T(8,128)S(1)} collective-permute-done((f32[8,128]{1,0:T(8,128)S(1)}, f32[8,128]{1,0:T(8,128)S(1)}, u32[]{:S(2)}, u32[]{:S(2)}) %collective-permute-start.8) | collective-permute-done | bytes 4128 | tf_op jit(solution)/shard_map/ppermute | solution.py:577
  50.4 0.0 collective-permute-done.9.high_ref.uhigh_ref
  50.4 0.6 copy-done.10
  51.0 0.0 copy-done.7
  51.0 1.5 %rim.1 = (f32[8,128]{1,0:T(8,128)}, f32[16,128]{1,0:T(8,128)}) custom-call(f32[3,64,128]{2,1,0:T(8,128)S(1)} %get-tuple-element.102.f_ref, f32[64,128]{1,0:T(8,128)S(1)} %copy-done.12, f32[64,128]{1,0:T(8,128)S(1)} %copy-done.13, s32[64,128]{1,0:T(8,128)S(1)} %copy-done.14, f32[8,128]{1,0:T(8,128)} %copy-done.10, f32[16,128]{1,0:T(8,128)} %copy-done.7), custom_call_target="tpu_custom_call" | custom-call | tf_op jit(solution)/shard_map/rim/pallas_call | solution.py:304
  52.5 2.8 %collective-permute-start.11 = (f32[16,128]{1,0:T(8,128)}, f32[16,128]{1,0:T(8,128)S(1)}, u32[]{:S(2)}, u32[]{:S(2)}) collective-permute-start(f32[16,128]{1,0:T(8,128)} %get-tuple-element.106), channel_id=1, source_target_pairs={{0,31},{1,0},{2,1},{3,2},{4,3},{5,4},{6,5},{7,6},{8,7},{9,8},{10,9... | collective-permute-start | bytes 24584 | tf_op jit(solution)/shard_map/ppermute | solution.py:577
  55.2 0.6 collective-permute-start.10
  55.8 0.0 collective-permute-start.13
  55.9 3.3 %collective-permute-done.10.vlow_ref = f32[8,128]{1,0:T(8,128)S(1)} collective-permute-done((f32[8,128]{1,0:T(8,128)}, f32[8,128]{1,0:T(8,128)S(1)}, u32[]{:S(2)}, u32[]{:S(2)}) %collective-permute-start.10) | collective-permute-done | bytes 4128 | tf_op jit(solution)/shard_map/ppermute | solution.py:577
  59.1 0.0 collective-permute-done.11.vhigh_ref
  59.2 0.7 copy-done.8
  59.8 0.7 copy-done.11
  60.5 6.3 %shell.1 = (f32[3,64,128]{2,1,0:T(8,128)S(1)}, f32[128,512]{1,0:T(8,128)S(1)}) custom-call(f32[12,12]{1,0:T(8,128)S(1)} %copy-done.15, f32[3,64,128]{2,1,0:T(8,128)S(1)} %get-tuple-element.102.f_ref, f32[64,128]{1,0:T(8,128)S(1)} %copy-done.12, f32[64,128]{1,0:T(8,128)S(1)} %copy-done.13, s32[64,128]{1,0:T(8,128)S(1)} %copy-done.14, ...), custom_call_target="tpu_custom_call" | custom-call | tf_op jit(solution)/shard_map/shell/pallas_call | solution.py:439
  66.8 1.0 copy.31
  67.8 9.1 %all-to-all-start.1 = ((f32[128,1,512]{2,1,0:T(1,128)}), f32[128,1,512]{2,1,0:T(1,128)S(1)}, u32[]{:S(2)}, u32[]{:S(2)}) async-start(f32[128,1,512]{2,1,0:T(1,128)} %copy.31), calls=%async_computation.1 | async-start | bytes 524288 | tf_op jit(solution)/shard_map/all_to_all | solution.py:633
  76.9 0.0 collective-permute-done.12.xp_ref
  77.0 0.0 collective-permute-done.13.xm_ref
  77.0 1.7 %collective-permute-start.14 = (f32[5,32,256]{2,1,0:T(8,128)S(1)}, f32[5,32,256]{2,1,0:T(8,128)S(1)}, u32[]{:S(2)}, u32[]{:S(2)}) collective-permute-start(f32[5,32,256]{2,1,0:T(8,128)S(1)} %scatter.15), channel_id=1, source_target_pairs={{0,1},{1,2},{2,3},{3,4},{4,5},{5,6},{6,7},{7,8},{8,9},{9,10},{10,1... | collective-permute-start | bytes 491528 | tf_op jit(solution)/shard_map/ppermute | solution.py:577
  78.8 9.4 %all-to-all-done.1 = f32[128,1,512]{2,1,0:T(1,128)S(1)} async-done(((f32[128,1,512]{2,1,0:T(1,128)}), f32[128,1,512]{2,1,0:T(1,128)S(1)}, u32[]{:S(2)}, u32[]{:S(2)}) %all-to-all-start.1) | async-done | bytes 262176 | tf_op jit(solution)/shard_map/all_to_all | solution.py:633
  88.3 0.6 fusion.21
  96.3 0.0 copy-start.4
  96.3 0.0 copy-start.6
  96.3 0.3 conditional.1
  96.6 1.1 collective-permute-start.15
  97.7 0.1 pad_maximum_fusion.18.pq_ref
  97.8 0.0 collective-permute-done.14.yp_ref
  97.8 3.6 %collective-permute-done.15.ym_ref = f32[5,32,256]{2,1,0:T(8,128)S(1)} collective-permute-done((f32[5,32,256]{2,1,0:T(8,128)S(1)}, f32[5,32,256]{2,1,0:T(8,128)S(1)}, u32[]{:S(2)}, u32[]{:S(2)}) %collective-permute-start.15) | collective-permute-done | bytes 163872 | tf_op jit(solution)/shard_map/ppermute | solution.py:577
  101.4 2.2 %copy-done.1 = f32[4096,256]{1,0:T(8,128)S(1)} copy-done((f32[4096,256]{1,0:T(8,128)S(1)}, f32[4096,256]{1,0:T(8,128)}, u32[]{:S(2)}) %copy-start.1) | copy-done | bytes 4194328
  103.6 16.5 %outputs.1 = (f32[19,256,256]{2,1,0:T(8,128)}, f32[3,64,128]{2,1,0:T(8,128)}) custom-call(f32[2]{0:T(128)S(1)} %pad_maximum_fusion.18.pq_ref, f32[128,512]{1,0:T(8,128)S(1)} %bitcast.34, f32[4096,256]{1,0:T(8,128)S(1)} %copy-done.1, s32[1,4096]{1,0:T(1,128)S(1)} %bitcast.40, s32[1,4096]{1,0:T(1,128)S(1)} %bitcast.42, ...), custom_call_target="tpu_custom_call" | custom-call | tf_op jit(solution)/shard_map/outputs/pallas_call | solution.py:543
  (24 shorter events, 0.2 us)
Async XLA Ops:
  0.6 2.2 %copy-start = (f32[4096,256]{1,0:T(8,128)S(1)}, f32[4096,256]{1,0:T(8,128)}, u32[]{:S(2)}) copy-start(f32[4096,256]{1,0:T(8,128)} %w_ref.3) | copy-start | bytes 12582916
  2.8 0.7 copy-start.3
  3.5 0.7 copy-start.5
  4.3 0.7 copy-start.9
  19.7 22.3 %all-to-all-start = ((f32[128,1,256]{2,1,0:T(1,128)}), f32[128,1,256]{2,1,0:T(1,128)S(1)}, u32[]{:S(2)}, u32[]{:S(2)}) async-start(f32[128,1,256]{2,1,0:T(1,128)} %copy.30), calls=%async_computation | async-start | bytes 262144 | tf_op jit(solution)/shard_map/all_to_all | solution.py:616
  31.2 10.8 %copy-start.12 = (f32[64,128]{1,0:T(8,128)S(1)}, f32[64,128]{1,0:T(8,128)}, u32[]{:S(2)}) copy-start(f32[64,128]{1,0:T(8,128)} %mass_ref.5) | copy-start | bytes 98308
  31.3 10.8 %copy-start.13 = (f32[64,128]{1,0:T(8,128)S(1)}, f32[64,128]{1,0:T(8,128)}, u32[]{:S(2)}) copy-start(f32[64,128]{1,0:T(8,128)} %mod_ref.5) | copy-start | bytes 98308
  31.3 10.8 %copy-start.14 = (s32[64,128]{1,0:T(8,128)S(1)}, s32[64,128]{1,0:T(8,128)}, u32[]{:S(2)}) copy-start(s32[64,128]{1,0:T(8,128)} %live_ref.5) | copy-start | bytes 98308
  31.3 27.9 %copy-start.15 = (f32[12,12]{1,0:T(8,128)S(1)}, f32[12,12]{1,0:T(8,128)}, u32[]{:S(2)}) copy-start(f32[12,12]{1,0:T(8,128)} %stiff_ref.1) | copy-start | bytes 1732
  38.4 2.2 %copy-start.2 = (f32[19,256,256]{2,1,0:T(8,128)}, f32[19,256,256]{2,1,0:T(8,128)S(1)}, u32[]{:S(2)}) copy-start(f32[19,256,256]{2,1,0:T(8,128)S(1)} %get-tuple-element.112.read_ref) | copy-start | bytes 14942212
  40.7 36.2 %collective-permute-start.12 = (f32[5,8,256]{2,1,0:T(8,128)S(1)}, f32[5,8,256]{2,1,0:T(8,128)S(1)}, u32[]{:S(2)}, u32[]{:S(2)}) collective-permute-start(f32[5,8,256]{2,1,0:T(8,128)S(1)} %get-tuple-element.113), channel_id=1, source_target_pairs={{0,32},{32,64},{64,96},{96,0},{1,33},{33,65},{65,97},{97,1},{2,34}... | collective-permute-start | bytes 122888 | tf_op jit(solution)/shard_map/ppermute | solution.py:577
  45.4 5.0 %collective-permute-start.9 = (f32[16,128]{1,0:T(8,128)S(1)}, f32[16,128]{1,0:T(8,128)S(1)}, u32[]{:S(2)}, u32[]{:S(2)}) collective-permute-start(f32[16,128]{1,0:T(8,128)S(1)} %get-tuple-element.104), channel_id=1, source_target_pairs={{0,96},{32,0},{64,32},{96,64},{1,97},{33,1},{65,33},{97,65},{2,98}... | collective-permute-start | bytes 24584 | tf_op jit(solution)/shard_map/ppermute | solution.py:577
  46.7 3.7 %collective-permute-start.8 = (f32[8,128]{1,0:T(8,128)S(1)}, f32[8,128]{1,0:T(8,128)S(1)}, u32[]{:S(2)}, u32[]{:S(2)}) collective-permute-start(f32[8,128]{1,0:T(8,128)S(1)} %get-tuple-element.103), channel_id=1, source_target_pairs={{0,32},{32,64},{64,96},{96,0},{1,33},{33,65},{65,97},{97,1},{2,34}... | collective-permute-start | bytes 12296 | tf_op jit(solution)/shard_map/ppermute | solution.py:577
  50.4 0.6 copy-start.10
  50.4 0.6 copy-start.7
  52.5 6.7 %collective-permute-start.11 = (f32[16,128]{1,0:T(8,128)}, f32[16,128]{1,0:T(8,128)S(1)}, u32[]{:S(2)}, u32[]{:S(2)}) collective-permute-start(f32[16,128]{1,0:T(8,128)} %get-tuple-element.106), channel_id=1, source_target_pairs={{0,31},{1,0},{2,1},{3,2},{4,3},{5,4},{6,5},{7,6},{8,7},{9,8},{10,9... | collective-permute-start | bytes 24584 | tf_op jit(solution)/shard_map/ppermute | solution.py:577
  55.2 3.9 %collective-permute-start.10 = (f32[8,128]{1,0:T(8,128)}, f32[8,128]{1,0:T(8,128)S(1)}, u32[]{:S(2)}, u32[]{:S(2)}) collective-permute-start(f32[8,128]{1,0:T(8,128)} %get-tuple-element.105), channel_id=1, source_target_pairs={{0,1},{1,2},{2,3},{3,4},{4,5},{5,6},{6,7},{7,8},{8,9},{9,10},{10,1... | collective-permute-start | bytes 12296 | tf_op jit(solution)/shard_map/ppermute | solution.py:577
  55.8 21.2 %collective-permute-start.13 = (f32[5,8,256]{2,1,0:T(8,128)S(1)}, f32[5,8,256]{2,1,0:T(8,128)S(1)}, u32[]{:S(2)}, u32[]{:S(2)}) collective-permute-start(f32[5,8,256]{2,1,0:T(8,128)S(1)} %get-tuple-element.114), channel_id=1, source_target_pairs={{0,96},{32,0},{64,32},{96,64},{1,97},{33,1},{65,33},{97,65},{2,98}... | collective-permute-start | bytes 122888 | tf_op jit(solution)/shard_map/ppermute | solution.py:577
  59.1 0.7 copy-start.8
  59.8 0.7 copy-start.11
  67.8 20.5 %all-to-all-start.1 = ((f32[128,1,512]{2,1,0:T(1,128)}), f32[128,1,512]{2,1,0:T(1,128)S(1)}, u32[]{:S(2)}, u32[]{:S(2)}) async-start(f32[128,1,512]{2,1,0:T(1,128)} %copy.31), calls=%async_computation.1 | async-start | bytes 524288 | tf_op jit(solution)/shard_map/all_to_all | solution.py:633
  77.0 20.7 %collective-permute-start.14 = (f32[5,32,256]{2,1,0:T(8,128)S(1)}, f32[5,32,256]{2,1,0:T(8,128)S(1)}, u32[]{:S(2)}, u32[]{:S(2)}) collective-permute-start(f32[5,32,256]{2,1,0:T(8,128)S(1)} %scatter.15), channel_id=1, source_target_pairs={{0,1},{1,2},{2,3},{3,4},{4,5},{5,6},{6,7},{7,8},{8,9},{9,10},{10,1... | collective-permute-start | bytes 491528 | tf_op jit(solution)/shard_map/ppermute | solution.py:577
  96.3 5.1 %copy-start.4 = (s32[4096]{0:T(1024)S(1)}, s32[4096]{0:T(1024)}, u32[]{:S(2)}) copy-start(s32[4096]{0:T(1024)} %param.24) | copy-start | bytes 49156
  96.3 5.1 %copy-start.6 = (s32[4096,1]{0,1:T(1,128)S(1)}, s32[4096,1]{0,1:T(1,128)}, u32[]{:S(2)}) copy-start(s32[4096,1]{0,1:T(1,128)} %param.25) | copy-start | bytes 49156
  96.6 4.8 %collective-permute-start.15 = (f32[5,32,256]{2,1,0:T(8,128)S(1)}, f32[5,32,256]{2,1,0:T(8,128)S(1)}, u32[]{:S(2)}, u32[]{:S(2)}) collective-permute-start(f32[5,32,256]{2,1,0:T(8,128)S(1)} %scatter.19), channel_id=1, source_target_pairs={{0,31},{1,0},{2,1},{3,2},{4,3},{5,4},{6,5},{7,6},{8,7},{9,8},{10,9... | collective-permute-start | bytes 491528 | tf_op jit(solution)/shard_map/ppermute | solution.py:577
  101.4 2.2 %copy-start.1 = (f32[4096,256]{1,0:T(8,128)S(1)}, f32[4096,256]{1,0:T(8,128)}, u32[]{:S(2)}) copy-start(f32[4096,256]{1,0:T(8,128)} %w_ref.3) | copy-start | bytes 12582916
where the time goes:
time: 121 us; the launch traced here: 120 us
  Pallas kernels  48.6 us (40%)
  starting transfers between devices  29.7 us (25%)
  waiting for transfers between devices  19.8 us (16%)
  local copies, waits for them, and re-layouts  13.3 us (11%)
  between operations  8.22 us (7%)
    pallas_call x1, Pallas kernels, outputs_of(): pl.pallas_call(next_kernel, grid=(RSTEPS + OSTEPS,), in_specs=[pl.BlockSp...  16.5 us
    pallas_call x1, Pallas kernels, loads_to_send(): pl.pallas_call(load_kernel, grid=(R // RB,), in_specs=[pl.BlockSpec((19,...  14 us
    all_to_all x1, starting transfers between devices, per_device(): recv = lax.all_to_all(send, ALL, 0, 0, tiled=True)  11.5 us
    unnamed x34, local copies, waits for them, and re-layouts  10.8 us
    ppermute x8, waiting for transfers between devices, pass_on(): lax.ppermute(x, axis, [(i, (i + shift) % count) for i in range(count)])  10.4 us
    all_to_all x1, waiting for transfers between devices, per_device(): back = lax.all_to_all(ret, ALL, 0, 0, tiled=True)  9.43 us
    ppermute x8, starting transfers between devices, pass_on(): lax.ppermute(x, axis, [(i, (i + shift) % count) for i in range(count)])  9.14 us
    all_to_all x1, starting transfers between devices, per_device(): back = lax.all_to_all(ret, ALL, 0, 0, tiled=True)  9.09 us
  transfers between devices with their start and end apart: 10, of which 4 were waited for; matrix products, arithmetic and copies ran while one was open for 2% of the time, Pallas kernels for 15%

commit v1 on v0

--- a/solution.py
+++ b/solution.py
@@ -8,7 +8,8 @@
 F32 = jnp.float32
 BF16 = jnp.bfloat16
 ALL = ("gx", "gy")
-VMEM_LIMIT = 48 * 1024 * 1024
+VMEM_LIMIT = 60 * 1024 * 1024
+SMALL_LIMIT = 16 * 1024 * 1024
 
 DIRS = (
     (0, 0, 0),
@@ -45,7 +46,7 @@
 ND = 128
 CAP = 64
 NU, NV = 64, 128
-RB = 512
+RB = 1024
 EU, EV = 72, 256
 
 
@@ -75,92 +76,112 @@
     return lax.dot_general(a, b, (((1,), (0,)), ((), ())), preferred_element_type=F32)
 
 
-def load_kernel(pop_ref, w_ref, blk_ref, own_ref, node_ref, send_ref, rank_ref, m_ref, tri_ref, carry_ref):
+MSTEPS = 2
+MROWS = NB // MSTEPS
+RSTEPS = R // RB
+
+
+def block_hot(row):
+    return jnp.where(iota((NB, RB), 0) == row, 1.0, 0.0).astype(BF16)
+
+
+def load_kernel(
+    pop_ref, w_ref, blk_ref, own_all_ref, own_ref, node_ref, send_ref, rank_ref, m_ref, mt_ref, tri_ref, carry_ref
+):
     step = pl.program_id(0)
 
     @pl.when(step == 0)
     def _():
-        def rows_of(i, _):
-            rows = pl.ds(pl.multiple_of(i * 16, 16), 16)
-            pops = [pop_ref[q, rows, :] for q in range(1, 19)]
-            for axis in range(3):
-                total = None
-                for q in range(1, 19):
-                    if DIRS[q][axis] != 0:
-                        term = pops[q - 1] if DIRS[q][axis] == 1 else -pops[q - 1]
-                        total = term if total is None else total + term
-                high = total.astype(BF16)
-                low = (total - high.astype(F32)).astype(BF16)
-                at = pl.ds(pl.multiple_of(axis * NB + i * 16, 16), 16)
-                m_ref[at, 0:NK] = high
-                m_ref[at, NK : 2 * NK] = low
-                m_ref[at, 2 * NK : 3 * NK] = high
-            return 0
-
-        lax.fori_loop(0, NB // 16, rows_of, 0)
         before = (iota((256, 256), 0) < iota((256, 256), 1)).astype(F32)
         tri_ref[:, 0:256] = before.astype(BF16)
         tri_ref[:, 256:512] = jnp.ones((256, 256), BF16)
         carry_ref[...] = jnp.zeros_like(carry_ref)
         send_ref[...] = jnp.zeros_like(send_ref)
 
-    w = w_ref[...]
-    w_high = w.astype(BF16)
-    w_low = (w - w_high.astype(F32)).astype(BF16)
-    w_all = jnp.concatenate([w_high, w_high, w_low], axis=1)
-    at_block = iota((NB, RB), 0) == blk_ref[...]
-    values = []
-    for axis in range(3):
-        product = dot_t(m_ref[axis * NB : (axis + 1) * NB, :], w_all)
-        values.append(jnp.sum(jnp.where(at_block, product, 0.0), axis=0, keepdims=True))
-    values.append(node_ref[...].astype(F32))
-
-    named = iota((ND, RB), 0) == own_ref[...]
-    named_bf = jnp.where(named, 1.0, 0.0).astype(BF16)
-    ranks = []
-    for part in range(RB // 256):
-        cols = slice(part * 256, (part + 1) * 256)
-        counts = dot(named_bf[:, cols], tri_ref[...])
-        upto = counts[:, 0:256] + carry_ref[...]
-        ranks.append(jnp.sum(jnp.where(named[:, cols], upto, 0.0), axis=0, keepdims=True))
-        carry_ref[...] += counts[:, 256:512]
-    rank = jnp.concatenate(ranks, axis=1).astype(jnp.int32)
-    rank_ref[...] = rank
-    in_slot = iota((CAP, RB), 0) == rank
-    highs, lows = [], []
-    for value in values:
-        high, low = halves(value)
-        highs.append(jnp.where(in_slot, high, 0.0).astype(BF16))
-        lows.append(jnp.where(in_slot, low, 0.0).astype(BF16))
-    packed = jnp.concatenate([jnp.concatenate(highs, axis=0), jnp.concatenate(lows, axis=0)], axis=1)
-    send_ref[...] += dot_t(jnp.concatenate([named_bf, named_bf], axis=1), packed)
+    for part in range(MSTEPS):
+
+        @pl.when(step == part)
+        def _():
+            def rows_of(i, _):
+                rows = pl.ds(pl.multiple_of(i * 8, 8), 8)
+                pops = [pop_ref[q, rows, :] for q in range(1, 19)]
+                for axis in range(3):
+                    total = None
+                    for q in range(1, 19):
+                        if DIRS[q][axis] != 0:
+                            term = pops[q - 1] if DIRS[q][axis] == 1 else -pops[q - 1]
+                            total = term if total is None else total + term
+                    m_ref[axis, rows, :] = total
+                return 0
+
+            lax.fori_loop(0, MROWS // 8, rows_of, 0, unroll=2)
+            for axis in range(3):
+                turned = m_ref[axis].T
+                high = turned.astype(BF16)
+                at = slice(axis * NK, (axis + 1) * NK)
+                mt_ref[at, part * MROWS : (part + 1) * MROWS] = high
+                low = (turned - high.astype(F32)).astype(BF16)
+                mt_ref[at, NB + part * MROWS : NB + (part + 1) * MROWS] = low
+            for k in range(R // 256 // MSTEPS):
+                cols = slice((part * (R // 256 // MSTEPS) + k) * 256, (part * (R // 256 // MSTEPS) + k + 1) * 256)
+                named = iota((ND, 256), 0) == own_all_ref[:, cols]
+                counts = dot(jnp.where(named, 1.0, 0.0).astype(BF16), tri_ref[...])
+                upto = jnp.where(named, counts[:, 0:256] + carry_ref[...], 0.0)
+                carry_ref[...] += counts[:, 256:512]
+                rank_ref[:, cols] = jnp.sum(upto, axis=0, keepdims=True).astype(jnp.int32)
+
+    @pl.when(step >= MSTEPS)
+    def _():
+        w_t = w_ref[...].T
+        hot = block_hot(blk_ref[...])
+        picked = dot(mt_ref[...], jnp.concatenate([hot, hot], axis=0))
+        values = [
+            jnp.sum(picked[axis * NK : (axis + 1) * NK, :] * w_t, axis=0, keepdims=True) for axis in range(3)
+        ]
+        values.append(node_ref[...].astype(F32))
+        named = jnp.where(iota((ND, RB), 0) == own_ref[...], 1.0, 0.0).astype(BF16)
+        rank = rank_ref[:, pl.ds(pl.multiple_of((step - MSTEPS) * RB, RB), RB)]
+        in_slot = iota((CAP, RB), 0) == rank
+        highs, lows = [], []
+        for value in values:
+            high, low = halves(value)
+            highs.append(jnp.where(in_slot, high, 0.0).astype(BF16))
+            lows.append(jnp.where(in_slot, low, 0.0).astype(BF16))
+        packed = jnp.concatenate([jnp.concatenate(highs, axis=0), jnp.concatenate(lows, axis=0)], axis=1)
+        send_ref[...] += dot_t(jnp.concatenate([named, named], axis=1), packed)
 
 
 def loads_to_send(pops, weights, block_row, owner_row, node_row):
-    row_spec = pl.BlockSpec((1, RB), lambda i: (0, i))
+    def record(i):
+        return jnp.maximum(i - MSTEPS, 0)
+
+    row_spec = pl.BlockSpec((1, RB), lambda i: (0, record(i)))
+    all_rows = pl.BlockSpec((1, R), lambda i: (0, 0))
     return pl.pallas_call(
         load_kernel,
-        grid=(R // RB,),
+        grid=(MSTEPS + RSTEPS,),
         in_specs=[
-            pl.BlockSpec((19, NB, NK), lambda i: (0, 0, 0)),
-            pl.BlockSpec((RB, NK), lambda i: (i, 0)),
+            pl.BlockSpec((19, MROWS, NK), lambda i: (0, jnp.minimum(i, MSTEPS - 1), 0)),
+            pl.BlockSpec((RB, NK), lambda i: (record(i), 0)),
+            row_spec,
+            all_rows,
             row_spec,
             row_spec,
-            row_spec,
-        ],
-        out_specs=[pl.BlockSpec((ND, 4 * CAP), lambda i: (0, 0)), row_spec],
+        ],
+        out_specs=[pl.BlockSpec((ND, 4 * CAP), lambda i: (0, 0)), all_rows],
         out_shape=[
             jax.ShapeDtypeStruct((ND, 4 * CAP), F32),
             jax.ShapeDtypeStruct((1, R), jnp.int32),
         ],
         scratch_shapes=[
-            pltpu.VMEM((3 * NB, 3 * NK), BF16),
+            pltpu.VMEM((3, MROWS, NK), F32),
+            pltpu.VMEM((3 * NK, 2 * NB), BF16),
             pltpu.VMEM((256, 512), BF16),
             pltpu.VMEM((ND, 256), F32),
         ],
         compiler_params=pltpu.CompilerParams(vmem_limit_bytes=VMEM_LIMIT),
         name="loads",
-    )(pops, weights, block_row, owner_row, node_row)
+    )(pops, weights, block_row, owner_row, owner_row, node_row)
 
 
 def collide_kernel(pop_ref, read_ref, xp_ref, xm_ref, yp_ref, ym_ref):
@@ -275,7 +296,7 @@
             pltpu.VMEM((CAP, ND), jnp.int32),
             pltpu.VMEM((6 * CAP, ND), F32),
         ],
-        compiler_params=pltpu.CompilerParams(vmem_limit_bytes=VMEM_LIMIT),
+        compiler_params=pltpu.CompilerParams(vmem_limit_bytes=SMALL_LIMIT),
         name="force",
     )(recv, mass, modulus, live)
 
@@ -304,6 +325,7 @@
     return pl.pallas_call(
         rim_kernel,
         out_shape=[jax.ShapeDtypeStruct((8, 128), F32), jax.ShapeDtypeStruct((16, 128), F32)],
+        compiler_params=pltpu.CompilerParams(vmem_limit_bytes=SMALL_LIMIT),
         name="rim",
     )(force, mass, modulus, live, low, high)
 
@@ -454,12 +476,49 @@
             pltpu.VMEM((CAP, ND), jnp.int32),
             pltpu.VMEM((6 * CAP, ND), F32),
         ],
-        compiler_params=pltpu.CompilerParams(vmem_limit_bytes=VMEM_LIMIT),
+        compiler_params=pltpu.CompilerParams(vmem_limit_bytes=SMALL_LIMIT),
         name="shell",
     )(stiff, force, mass, modulus, live, ulow, uhigh, vlow, vhigh, recv)
 
 
-RSTEPS = R // RB
+def scalar_kernel(part_ref, pq_ref, sound_ref):
+    row = jnp.sum(part_ref[...], axis=0, keepdims=True)
+    lane = iota((1, 128), 1)
+    m0, m1, m2, m3 = [
+        jnp.sum(jnp.where(lane == i, row, 0.0), axis=1, keepdims=True) for i in range(4)
+    ]
+    first = m0 / m1
+    left_over = first * first * m2 - m0
+    ratio = left_over / m0
+    gain = 1.0 + ratio
+    curve = gain * gain * m1 - 2.0 * gain * first * m2 + first * first * m3
+    second = left_over / curve
+    sound = (
+        (left_over > 1e-3 * m0)
+        & (curve > 1e-2 * gain * gain * m1)
+        & (curve < 1e30)
+        & (m1 > 1e-30)
+        & (m0 > 1e-30)
+    )
+    pq_ref[0] = (first + second * gain)[0, 0]
+    pq_ref[1] = -(first * second)[0, 0]
+    pq_ref[2] = first[0, 0]
+    pq_ref[3] = m0[0, 0]
+    sound_ref[0] = jnp.where(sound, 1, 0)[0, 0]
+
+
+def scalars_of(back):
+    smem = pl.BlockSpec(memory_space=pltpu.SMEM)
+    return pl.pallas_call(
+        scalar_kernel,
+        grid=(1,),
+        in_specs=[pl.BlockSpec((ND, 128), lambda i: (0, 3))],
+        out_specs=[smem, smem],
+        out_shape=[jax.ShapeDtypeStruct((4,), F32), jax.ShapeDtypeStruct((1,), jnp.int32)],
+        name="scalars",
+    )(back)
+
+
 XS = 4
 OSTEPS = 32 // XS
 
@@ -467,7 +526,7 @@
 def next_kernel(
     pq_ref, back_ref, w_ref, blk_ref, own_ref, rank_ref, f_ref, y_ref, read_ref, xp_ref, xm_ref, yp_ref, ym_ref,
     next_ref, disp_ref,
-    x_ref, force_ref,
+    x_ref, turned_ref, force_ref,
 ):
     step = pl.program_id(0)
 
@@ -481,26 +540,31 @@
         x_ref[:, 0:ND] = high
         x_ref[:, ND : 2 * ND] = (turned - high.astype(F32)).astype(BF16)
         disp_ref[...] = p * f_ref[...] + q * y_ref[...]
-        force_ref[...] = jnp.zeros_like(force_ref)
+        turned_ref[...] = jnp.zeros_like(turned_ref)
 
     @pl.when(step < RSTEPS)
     def _():
         named = jnp.where(iota((ND, RB), 0) == own_ref[...], 1.0, 0.0).astype(BF16)
         picked = dot(x_ref[...], jnp.concatenate([named, named], axis=0))
         in_slot = iota((CAP, RB), 0) == rank_ref[...]
-        at_block = iota((NB, RB), 0) == blk_ref[...]
-        w = w_ref[...]
-        w_high = w.astype(BF16)
-        w_low = (w - w_high.astype(F32)).astype(BF16)
-        w_all = jnp.concatenate([w_high, w_high, w_low], axis=0)
+        w_t = w_ref[...].T
+        highs, lows = [], []
         for c in range(3):
             moved = jnp.sum(
                 jnp.where(in_slot, picked[c * CAP : (c + 1) * CAP, :], 0.0), axis=0, keepdims=True
             )
-            high, low = halves(moved)
-            high = jnp.where(at_block, high, 0.0).astype(BF16)
-            low = jnp.where(at_block, low, 0.0).astype(BF16)
-            force_ref[c * NB : (c + 1) * NB, :] += dot(jnp.concatenate([high, low, high], axis=1), w_all)
+            part = w_t * moved
+            high = part.astype(BF16)
+            highs.append(high)
+            lows.append((part - high.astype(F32)).astype(BF16))
+        hot = block_hot(blk_ref[...])
+        parts = jnp.concatenate([jnp.concatenate(highs, axis=0), jnp.concatenate(lows, axis=0)], axis=1)
+        turned_ref[...] += dot_t(parts, jnp.concatenate([hot, hot], axis=1))
+
+    @pl.when(step == RSTEPS)
+    def _():
+        for c in range(3):
+            force_ref[c * NB : (c + 1) * NB, :] = turned_ref[c * NK : (c + 1) * NK, :].T
 
     @pl.when(step >= RSTEPS)
     def _():
@@ -565,6 +629,7 @@
         ],
         scratch_shapes=[
             pltpu.VMEM((3 * CAP, 2 * ND), BF16),
+            pltpu.VMEM((3 * NK, NB), F32),
             pltpu.VMEM((3 * NB, NK), F32),
         ],
         compiler_params=pltpu.CompilerParams(vmem_limit_bytes=VMEM_LIMIT),
@@ -632,35 +697,24 @@
     image, ret = shell_of(stiff, force, mass, modulus, live, ulow, uhigh, vlow, vhigh, recv)
     back = lax.all_to_all(ret, ALL, 0, 0, tiled=True)
 
-    moments = jnp.sum(back[:, 6 * CAP : 6 * CAP + 4], axis=0)
-    m0, m1, m2, m3 = moments[0], moments[1], moments[2], moments[3]
-    first = m0 / m1
-    left_over = first * first * m2 - m0
-    ratio = left_over / m0
-    gain = 1.0 + ratio
-    curve = gain * gain * m1 - 2.0 * gain * first * m2 + first * first * m3
-    sound = (
-        (left_over > 1e-3 * m0)
-        & (curve > 1e-2 * gain * gain * m1)
-        & (curve < 1e30)
-        & (m1 > 1e-30)
-        & (m0 > 1e-30)
-    )
-
-    def quick(_):
-        return ratio, left_over / curve
+    back, yp, ym = lax.optimization_barrier((back, yp, ym))
+    pq, sound = scalars_of(back)
+
+    def quick(operands):
+        return operands[0]
 
     def careful(operands):
-        force, image, mass, modulus, live, stiff = operands
+        pq, force, image, mass, modulus, live, stiff = operands
+        first = pq[2]
         residual = force - first * image
         norm = lax.psum(jnp.sum(residual * residual), ALL)
-        ratio = norm / m0
+        ratio = norm / pq[3]
         direction = residual + ratio * force
         along = operate(direction, mass, modulus, live, stiff)
-        return ratio, norm / lax.psum(jnp.sum(direction * along), ALL)
-
-    ratio, second = lax.cond(sound, quick, careful, (force, image, mass, modulus, live, stiff))
-    pq = jnp.stack([first + second * (1.0 + ratio), -(first * second)])
+        second = norm / lax.psum(jnp.sum(direction * along), ALL)
+        return jnp.stack([first + second * (1.0 + ratio), -(first * second), first, pq[3]])
+
+    pq = lax.cond(sound[0] == 1, quick, careful, (pq, force, image, mass, modulus, live, stiff))
 
     populations_next, displacement = outputs_of(
         pq, back, weights, block_row, owner_row, rank_row, force, image, read, xp, xm, yp, ym

time: 121 us -> 96.5 us (0.80)
  local copies, waits for them, and re-layouts: 13.3 us -> 3.61 us
  between operations: 8.22 us -> 1.69 us
  waiting for transfers between devices: 19.8 us -> 13.3 us
  Pallas kernels: 48.6 us -> 46.4 us
    unnamed x34 -> x22, local copies, waits for them, and re-layouts: 10.8 us -> 0.78 us
    ppermute x8, waiting for transfers between devices: 10.4 us -> 4.06 us  [pass_on(): lax.ppermute(x, axis, [(i, (i + shift) % count) for i in range(count)])]
    pallas_call x1, Pallas kernels: 16.5 us -> 13.9 us  [outputs_of(): pl.pallas_call(next_kernel, grid=(RSTEPS + OSTEPS,), in_specs=[pl.BlockSp...]
    pallas_call x1, Pallas kernels: 7.13 us -> 9.49 us  [collide_and_run(): pl.pallas_call(collide_kernel, out_shape=[jax.ShapeDtypeStruct((19, NB, N...]
    ppermute x8, starting transfers between devices: 9.14 us -> 10.6 us  [pass_on(): lax.ppermute(x, axis, [(i, (i + shift) % count) for i in range(count)])]
    pallas_call x1, Pallas kernels: 1.47 us -> 0.16 us  [rim_columns(): pl.pallas_call(rim_kernel, out_shape=[jax.ShapeDtypeStruct((8, 128), F32)...]
    pallas_call x1 -> x2, Pallas kernels: 14 us -> 13.4 us  [the longest x1 11.7 us: loads_to_send(): pl.pallas_call(load_kernel, grid=(MSTEPS + RSTEPS,), in_specs=[pl.BlockSp...]
  transfers between devices with their start and end apart: 10 -> 10, of which waited for: 4 -> 4; matrix products, arithmetic and copies ran while one was open for 2% -> 2% of each run, Pallas kernels for 15% -> 20%
where the time goes in v1:
time: 96.5 us; the launch traced here: 96.1 us
  Pallas kernels  46.4 us (48%)
  starting transfers between devices  30.8 us (32%)
  waiting for transfers between devices  13.3 us (14%)
  local copies, waits for them, and re-layouts  3.61 us (4%)
  between operations  1.69 us (2%)
    pallas_call x1, Pallas kernels, outputs_of(): pl.pallas_call(next_kernel, grid=(RSTEPS + OSTEPS,), in_specs=[pl.BlockSp...  13.9 us
    pallas_call x1, Pallas kernels, loads_to_send(): pl.pallas_call(load_kernel, grid=(MSTEPS + RSTEPS,), in_specs=[pl.BlockSp...  11.7 us
    all_to_all x1, starting transfers between devices, per_device(): recv = lax.all_to_all(send, ALL, 0, 0, tiled=True)  11.5 us
    ppermute x8, starting transfers between devices, pass_on(): lax.ppermute(x, axis, [(i, (i + shift) % count) for i in range(count)])  10.6 us
    pallas_call x1, Pallas kernels, collide_and_run(): pl.pallas_call(collide_kernel, out_shape=[jax.ShapeDtypeStruct((19, NB, N...  9.49 us
    all_to_all x1, waiting for transfers between devices, per_device(): back = lax.all_to_all(ret, ALL, 0, 0, tiled=True)  9.22 us
    all_to_all x1, starting transfers between devices, per_device(): back = lax.all_to_all(ret, ALL, 0, 0, tiled=True)  8.69 us
    pallas_call x1, Pallas kernels, shell_of(): pl.pallas_call(shell_kernel, in_specs=[pl.BlockSpec(memory_space=pltpu.SM...  6.28 us
  transfers between devices with their start and end apart: 10, of which 4 were waited for; matrix products, arithmetic and copies ran while one was open for 2% of the time, Pallas kernels for 20%

profile of v1, /device:TPU:1, one launch (start us, length us, event | category | flops | bytes accessed | tf_op | source)
XLA Modules:
  0.0 96.1 jit_solution(196310817399642492)
XLA Ops:
  0.6 11.7 %loads.1 = (f32[128,256]{1,0:T(8,128)}, s32[1,4096]{1,0:T(1,128)}) custom-call(f32[19,256,256]{2,1,0:T(8,128)} %bitcast.35, f32[4096,256]{1,0:T(8,128)} %w_ref.3, s32[1,4096]{1,0:T(1,128)} %bitcast.47, s32[1,4096]{1,0:T(1,128)} %bitcast.43, s32[1,4096]{1,0:T(1,128)} %bitcast.44, s32[1,4096]{1,0:T(1,128)} %bitcast.49), custom_call_target="tpu_custom_call" | custom-call | tf_op jit(solution)/shard_map/loads/pallas_call | solution.py:160
  12.3 1.7 %copy.30 = f32[128,1,256]{2,1,0:T(1,128)} copy(f32[128,1,256]{2,0,1:T(8,128)} %bitcast.46) | data formatting | bytes 262144 | tf_op jit(solution)/shard_map/all_to_all | solution.py:681
  14.0 11.5 %all-to-all-start = ((f32[128,1,256]{2,1,0:T(1,128)}), f32[128,1,256]{2,1,0:T(1,128)S(1)}, u32[]{:S(2)}, u32[]{:S(2)}) async-start(f32[128,1,256]{2,1,0:T(1,128)} %copy.30), calls=%async_computation | async-start | bytes 262144 | tf_op jit(solution)/shard_map/all_to_all | solution.py:681
  25.5 0.0 copy-start
  25.5 0.0 copy-start.1
  25.5 0.0 copy-start.2
  25.5 0.0 copy-start.7
  25.6 9.5 %collide.1 = (f32[19,256,256]{2,1,0:T(8,128)}, f32[5,8,256]{2,1,0:T(8,128)}, f32[5,8,256]{2,1,0:T(8,128)}, f32[5,32,256]{2,1,0:T(8,128)}, f32[5,32,256]{2,1,0:T(8,128)}) custom-call(f32[19,256,256]{2,1,0:T(8,128)} %bitcast.36), custom_call_target="tpu_custom_call" | custom-call | tf_op jit(solution)/shard_map/collide/pallas_call | solution.py:230
  35.0 0.0 copy-start.9
  35.0 1.4 %collective-permute-start.12 = (f32[5,8,256]{2,1,0:T(8,128)}, f32[5,8,256]{2,1,0:T(8,128)S(1)}, u32[]{:S(2)}, u32[]{:S(2)}) collective-permute-start(f32[5,8,256]{2,1,0:T(8,128)} %get-tuple-element.104), channel_id=1, source_target_pairs={{0,32},{32,64},{64,96},{96,0},{1,33},{33,65},{65,97},{97,1},{2,34}... | collective-permute-start | bytes 122888 | tf_op jit(solution)/shard_map/ppermute | solution.py:642
  36.5 0.0 all-to-all-done
  36.5 0.0 copy-done
  36.5 0.0 copy-done.1
  36.5 0.0 copy-done.2
  36.5 3.2 %force.1 = (f32[3,64,128]{2,1,0:T(8,128)S(1)}, f32[8,128]{1,0:T(8,128)S(1)}, f32[16,128]{1,0:T(8,128)S(1)}) custom-call(f32[128,256]{1,0:T(8,128)S(1)} %bitcast.32, f32[64,128]{1,0:T(8,128)S(1)} %copy-done, f32[64,128]{1,0:T(8,128)S(1)} %copy-done.1, s32[64,128]{1,0:T(8,128)S(1)} %copy-done.2), custom_call_target="tpu_custom_call" | custom-call | tf_op jit(solution)/shard_map/force/pallas_call | solution.py:287
  39.8 1.4 %collective-permute-start.9 = (f32[16,128]{1,0:T(8,128)S(1)}, f32[16,128]{1,0:T(8,128)S(1)}, u32[]{:S(2)}, u32[]{:S(2)}) collective-permute-start(f32[16,128]{1,0:T(8,128)S(1)} %get-tuple-element.99), channel_id=1, source_target_pairs={{0,96},{32,0},{64,32},{96,64},{1,97},{33,1},{65,33},{97,65},{2,98}... | collective-permute-start | bytes 24584 | tf_op jit(solution)/shard_map/ppermute | solution.py:642
  41.1 0.2 collective-permute-start.8
  41.3 2.5 %collective-permute-start.13 = (f32[5,8,256]{2,1,0:T(8,128)}, f32[5,8,256]{2,1,0:T(8,128)S(1)}, u32[]{:S(2)}, u32[]{:S(2)}) collective-permute-start(f32[5,8,256]{2,1,0:T(8,128)} %get-tuple-element.105), channel_id=1, source_target_pairs={{0,96},{32,0},{64,32},{96,64},{1,97},{33,1},{65,33},{97,65},{2,98}... | collective-permute-start | bytes 122888 | tf_op jit(solution)/shard_map/ppermute | solution.py:642
  43.8 1.0 %collective-permute-done.8.low_ref.ulow_ref = f32[8,128]{1,0:T(8,128)S(1)} collective-permute-done((f32[8,128]{1,0:T(8,128)S(1)}, f32[8,128]{1,0:T(8,128)S(1)}, u32[]{:S(2)}, u32[]{:S(2)}) %collective-permute-start.8) | collective-permute-done | bytes 4128 | tf_op jit(solution)/shard_map/ppermute | solution.py:642
  44.8 0.0 collective-permute-done.9.high_ref.uhigh_ref
  44.8 0.2 rim.1
  45.0 3.4 %collective-permute-start.10 = (f32[8,128]{1,0:T(8,128)S(1)}, f32[8,128]{1,0:T(8,128)S(1)}, u32[]{:S(2)}, u32[]{:S(2)}) collective-permute-start(f32[8,128]{1,0:T(8,128)S(1)} %get-tuple-element.100), channel_id=1, source_target_pairs={{0,1},{1,2},{2,3},{3,4},{4,5},{5,6},{6,7},{7,8},{8,9},{9,10},{10,1... | collective-permute-start | bytes 12296 | tf_op jit(solution)/shard_map/ppermute | solution.py:642
  48.4 0.0 collective-permute-start.11
  48.4 0.0 collective-permute-done.12.xp_ref
  48.4 0.7 collective-permute-done.10.vlow_ref
  49.1 2.3 %collective-permute-done.11.vhigh_ref = f32[16,128]{1,0:T(8,128)S(1)} collective-permute-done((f32[16,128]{1,0:T(8,128)S(1)}, f32[16,128]{1,0:T(8,128)S(1)}, u32[]{:S(2)}, u32[]{:S(2)}) %collective-permute-start.11) | collective-permute-done | bytes 8224 | tf_op jit(solution)/shard_map/ppermute | solution.py:642
  51.4 0.0 copy-done.7
  51.4 6.3 %shell.1 = (f32[3,64,128]{2,1,0:T(8,128)S(1)}, f32[128,512]{1,0:T(8,128)S(1)}) custom-call(f32[12,12]{1,0:T(8,128)S(1)} %copy-done.7, f32[3,64,128]{2,1,0:T(8,128)S(1)} %get-tuple-element.97.f_ref, f32[64,128]{1,0:T(8,128)S(1)} %copy-done, f32[64,128]{1,0:T(8,128)S(1)} %copy-done.1, s32[64,128]{1,0:T(8,128)S(1)} %copy-done.2, ...), custom_call_target="tpu_custom_call" | custom-call | tf_op jit(solution)/shard_map/shell/pallas_call | solution.py:461
  57.7 1.0 %copy.31 = f32[128,1,512]{2,1,0:T(1,128)} copy(f32[128,1,512]{2,0,1:T(8,128)S(1)} %bitcast.34) | data formatting | bytes 524288 | tf_op jit(solution)/shard_map/all_to_all | solution.py:698
  58.7 8.7 %all-to-all-start.1 = ((f32[128,1,512]{2,1,0:T(1,128)}), f32[128,1,512]{2,1,0:T(1,128)S(1)}, u32[]{:S(2)}, u32[]{:S(2)}) async-start(f32[128,1,512]{2,1,0:T(1,128)} %copy.31), calls=%async_computation.1 | async-start | bytes 524288 | tf_op jit(solution)/shard_map/all_to_all | solution.py:698
  67.4 0.0 collective-permute-done.13.xm_ref
  67.4 0.0 copy-start.6
  67.4 0.0 copy-done.9
  67.5 1.7 %collective-permute-start.14 = (f32[5,32,256]{2,1,0:T(8,128)S(1)}, f32[5,32,256]{2,1,0:T(8,128)S(1)}, u32[]{:S(2)}, u32[]{:S(2)}) collective-permute-start(f32[5,32,256]{2,1,0:T(8,128)S(1)} %scatter.15), channel_id=1, source_target_pairs={{0,1},{1,2},{2,3},{3,4},{4,5},{5,6},{6,7},{7,8},{8,9},{9,10},{10,1... | collective-permute-start | bytes 491528 | tf_op jit(solution)/shard_map/ppermute | solution.py:642
  69.2 0.0 copy-done.8
  69.3 0.1 collective-permute-start.15
  69.4 9.2 %all-to-all-done.1 = f32[128,1,512]{2,1,0:T(1,128)S(1)} async-done(((f32[128,1,512]{2,1,0:T(1,128)}), f32[128,1,512]{2,1,0:T(1,128)S(1)}, u32[]{:S(2)}, u32[]{:S(2)}) %all-to-all-start.1) | async-done | bytes 262176 | tf_op jit(solution)/shard_map/all_to_all | solution.py:698
  78.6 0.7 copy.41
  79.3 0.0 collective-permute-done.14.yp_ref
  79.3 0.0 collective-permute-done.15.ym_ref
  79.4 0.0 copy-start.4
  79.4 1.7 %scalars.1 = (f32[4]{0:T(128)S(1)}, s32[1]{0:T(128)}) custom-call(f32[128,512]{1,0:T(8,128)} %bitcast.37), custom_call_target="tpu_custom_call" | custom-call | tf_op jit(solution)/shard_map/scalars/pallas_call | solution.py:512
  81.1 0.0 copy-done.5
  81.7 0.0 copy-done.6
  81.7 0.0 copy-done.3
  81.7 0.0 copy-done.4
  81.8 0.2 conditional.1
  82.0 13.9 %outputs.1 = (f32[19,256,256]{2,1,0:T(8,128)}, f32[3,64,128]{2,1,0:T(8,128)}) custom-call(f32[4]{0:T(128)S(1)} %get-tuple-element.160.pq_ref, f32[128,512]{1,0:T(8,128)} %bitcast.38, f32[4096,256]{1,0:T(8,128)} %w_ref.3, s32[1,4096]{1,0:T(1,128)} %bitcast.48, s32[1,4096]{1,0:T(1,128)} %bitcast.45, s32[1,4096]{1,0:T(1,128)} %get-tuple-element.111.rank_ref, ...), custom_call_target="tpu_custom_call" | custom-call | tf_op jit(solution)/shard_map/outputs/pallas_call | solution.py:607
  (10 shorter events, 0.2 us)
Async XLA Ops:
  14.0 22.5 %all-to-all-start = ((f32[128,1,256]{2,1,0:T(1,128)}), f32[128,1,256]{2,1,0:T(1,128)S(1)}, u32[]{:S(2)}, u32[]{:S(2)}) async-start(f32[128,1,256]{2,1,0:T(1,128)} %copy.30), calls=%async_computation | async-start | bytes 262144 | tf_op jit(solution)/shard_map/all_to_all | solution.py:681
  25.5 11.0 %copy-start = (f32[64,128]{1,0:T(8,128)S(1)}, f32[64,128]{1,0:T(8,128)}, u32[]{:S(2)}) copy-start(f32[64,128]{1,0:T(8,128)} %mass_ref.5) | copy-start | bytes 98308
  25.5 11.0 %copy-start.1 = (f32[64,128]{1,0:T(8,128)S(1)}, f32[64,128]{1,0:T(8,128)}, u32[]{:S(2)}) copy-start(f32[64,128]{1,0:T(8,128)} %mod_ref.5) | copy-start | bytes 98308
  25.5 11.0 %copy-start.2 = (s32[64,128]{1,0:T(8,128)S(1)}, s32[64,128]{1,0:T(8,128)}, u32[]{:S(2)}) copy-start(s32[64,128]{1,0:T(8,128)} %live_ref.5) | copy-start | bytes 98308
  25.5 25.9 %copy-start.7 = (f32[12,12]{1,0:T(8,128)S(1)}, f32[12,12]{1,0:T(8,128)}, u32[]{:S(2)}) copy-start(f32[12,12]{1,0:T(8,128)} %stiff_ref.1) | copy-start | bytes 1732
  35.0 32.4 %copy-start.9 = (f32[5,32,256]{2,1,0:T(8,128)S(1)}, f32[5,32,256]{2,1,0:T(8,128)}, u32[]{:S(2)}) copy-start(f32[5,32,256]{2,1,0:T(8,128)} %get-tuple-element.103) | copy-start | bytes 491524
  35.0 34.2 %copy-start.8 = (f32[5,32,256]{2,1,0:T(8,128)S(1)}, f32[5,32,256]{2,1,0:T(8,128)}, u32[]{:S(2)}) copy-start(f32[5,32,256]{2,1,0:T(8,128)} %get-tuple-element.106) | copy-start | bytes 491524
  35.0 13.3 %collective-permute-start.12 = (f32[5,8,256]{2,1,0:T(8,128)}, f32[5,8,256]{2,1,0:T(8,128)S(1)}, u32[]{:S(2)}, u32[]{:S(2)}) collective-permute-start(f32[5,8,256]{2,1,0:T(8,128)} %get-tuple-element.104), channel_id=1, source_target_pairs={{0,32},{32,64},{64,96},{96,0},{1,33},{33,65},{65,97},{97,1},{2,34}... | collective-permute-start | bytes 122888 | tf_op jit(solution)/shard_map/ppermute | solution.py:642
  39.8 5.0 %collective-permute-start.9 = (f32[16,128]{1,0:T(8,128)S(1)}, f32[16,128]{1,0:T(8,128)S(1)}, u32[]{:S(2)}, u32[]{:S(2)}) collective-permute-start(f32[16,128]{1,0:T(8,128)S(1)} %get-tuple-element.99), channel_id=1, source_target_pairs={{0,96},{32,0},{64,32},{96,64},{1,97},{33,1},{65,33},{97,65},{2,98}... | collective-permute-start | bytes 24584 | tf_op jit(solution)/shard_map/ppermute | solution.py:642
  41.1 3.7 %collective-permute-start.8 = (f32[8,128]{1,0:T(8,128)S(1)}, f32[8,128]{1,0:T(8,128)S(1)}, u32[]{:S(2)}, u32[]{:S(2)}) collective-permute-start(f32[8,128]{1,0:T(8,128)S(1)} %get-tuple-element.98), channel_id=1, source_target_pairs={{0,32},{32,64},{64,96},{96,0},{1,33},{33,65},{65,97},{97,1},{2,34}... | collective-permute-start | bytes 12296 | tf_op jit(solution)/shard_map/ppermute | solution.py:642
  41.3 26.1 %collective-permute-start.13 = (f32[5,8,256]{2,1,0:T(8,128)}, f32[5,8,256]{2,1,0:T(8,128)S(1)}, u32[]{:S(2)}, u32[]{:S(2)}) collective-permute-start(f32[5,8,256]{2,1,0:T(8,128)} %get-tuple-element.105), channel_id=1, source_target_pairs={{0,96},{32,0},{64,32},{96,64},{1,97},{33,1},{65,33},{97,65},{2,98}... | collective-permute-start | bytes 122888 | tf_op jit(solution)/shard_map/ppermute | solution.py:642
  45.0 4.2 %collective-permute-start.10 = (f32[8,128]{1,0:T(8,128)S(1)}, f32[8,128]{1,0:T(8,128)S(1)}, u32[]{:S(2)}, u32[]{:S(2)}) collective-permute-start(f32[8,128]{1,0:T(8,128)S(1)} %get-tuple-element.100), channel_id=1, source_target_pairs={{0,1},{1,2},{2,3},{3,4},{4,5},{5,6},{6,7},{7,8},{8,9},{9,10},{10,1... | collective-permute-start | bytes 12296 | tf_op jit(solution)/shard_map/ppermute | solution.py:642
  48.4 3.1 %collective-permute-start.11 = (f32[16,128]{1,0:T(8,128)S(1)}, f32[16,128]{1,0:T(8,128)S(1)}, u32[]{:S(2)}, u32[]{:S(2)}) collective-permute-start(f32[16,128]{1,0:T(8,128)S(1)} %get-tuple-element.101), channel_id=1, source_target_pairs={{0,31},{1,0},{2,1},{3,2},{4,3},{5,4},{6,5},{7,6},{8,7},{9,8},{10,9... | collective-permute-start | bytes 24584 | tf_op jit(solution)/shard_map/ppermute | solution.py:642
  48.4 32.7 %copy-start.5 = (f32[5,8,256]{2,1,0:T(8,128)}, f32[5,8,256]{2,1,0:T(8,128)S(1)}, u32[]{:S(2)}) copy-start(f32[5,8,256]{2,1,0:T(8,128)S(1)} %collective-permute-done.12.xp_ref) | copy-start | bytes 122884
  58.7 19.9 %all-to-all-start.1 = ((f32[128,1,512]{2,1,0:T(1,128)}), f32[128,1,512]{2,1,0:T(1,128)S(1)}, u32[]{:S(2)}, u32[]{:S(2)}) async-start(f32[128,1,512]{2,1,0:T(1,128)} %copy.31), calls=%async_computation.1 | async-start | bytes 524288 | tf_op jit(solution)/shard_map/all_to_all | solution.py:698
  67.4 14.3 %copy-start.6 = (f32[5,8,256]{2,1,0:T(8,128)}, f32[5,8,256]{2,1,0:T(8,128)S(1)}, u32[]{:S(2)}) copy-start(f32[5,8,256]{2,1,0:T(8,128)S(1)} %collective-permute-done.13.xm_ref) | copy-start | bytes 122884
  67.5 11.8 %collective-permute-start.14 = (f32[5,32,256]{2,1,0:T(8,128)S(1)}, f32[5,32,256]{2,1,0:T(8,128)S(1)}, u32[]{:S(2)}, u32[]{:S(2)}) collective-permute-start(f32[5,32,256]{2,1,0:T(8,128)S(1)} %scatter.15), channel_id=1, source_target_pairs={{0,1},{1,2},{2,3},{3,4},{4,5},{5,6},{6,7},{7,8},{8,9},{9,10},{10,1... | collective-permute-start | bytes 491528 | tf_op jit(solution)/shard_map/ppermute | solution.py:642
  69.3 10.0 %collective-permute-start.15 = (f32[5,32,256]{2,1,0:T(8,128)S(1)}, f32[5,32,256]{2,1,0:T(8,128)S(1)}, u32[]{:S(2)}, u32[]{:S(2)}) collective-permute-start(f32[5,32,256]{2,1,0:T(8,128)S(1)} %scatter.19), channel_id=1, source_target_pairs={{0,31},{1,0},{2,1},{3,2},{4,3},{5,4},{6,5},{7,6},{8,7},{9,8},{10,9... | collective-permute-start | bytes 491528 | tf_op jit(solution)/shard_map/ppermute | solution.py:642
  79.3 2.4 %copy-start.3 = (f32[5,32,256]{2,1,0:T(8,128)}, f32[5,32,256]{2,1,0:T(8,128)S(1)}, u32[]{:S(2)}) copy-start(f32[5,32,256]{2,1,0:T(8,128)S(1)} %collective-permute-done.14.yp_ref) | copy-start | bytes 491524
  79.4 2.4 %copy-start.4 = (f32[5,32,256]{2,1,0:T(8,128)}, f32[5,32,256]{2,1,0:T(8,128)S(1)}, u32[]{:S(2)}) copy-start(f32[5,32,256]{2,1,0:T(8,128)S(1)} %collective-permute-done.15.ym_ref) | copy-start | bytes 491524

commit v2 on v1

--- a/solution.py
+++ b/solution.py
@@ -45,6 +45,8 @@
 NK = 256
 ND = 128
 CAP = 64
+RIM = 32
+MAIN = 4 * CAP
 NU, NV = 64, 128
 RB = 1024
 EU, EV = 72, 256
@@ -85,8 +87,29 @@
     return jnp.where(iota((NB, RB), 0) == row, 1.0, 0.0).astype(BF16)
 
 
+def rim_rows(own, node):
+    u, v = node >> 7, node & 127
+    ox, oy = own >> 5, own & 31
+    su = jnp.where(u == NU - 1, 1, jnp.where(u <= 1, -1, 0))
+    sv = jnp.where(v == NV - 1, 1, jnp.where(v <= 1, -1, 0))
+    ox2, oy2 = (ox + su) & 3, (oy + sv) & 31
+    dests = [
+        jnp.where(su != 0, ox2 * 32 + oy, -1),
+        jnp.where(sv != 0, ox * 32 + oy2, -1),
+        jnp.where((su != 0) & (sv != 0), ox2 * 32 + oy2, -1),
+    ]
+    row = jnp.where(u == NU - 1, 0, u + 1) * EV
+    codes = [
+        row + v,
+        jnp.where(v == NV - 1, 3, v + 4) * EV + u,
+        row + jnp.where(v == NV - 1, EV - 1, v + NV),
+    ]
+    return dests, codes
+
+
 def load_kernel(
-    pop_ref, w_ref, blk_ref, own_all_ref, own_ref, node_ref, send_ref, rank_ref, m_ref, mt_ref, tri_ref, carry_ref
+    pop_ref, w_ref, blk_ref, own_all_ref, node_all_ref, own_ref, node_ref, send_ref, rank_ref,
+    m_ref, mt_ref, tri_ref, carry_ref, dest_ref, code_ref, place_ref, over_ref,
 ):
     step = pl.program_id(0)
 
@@ -97,6 +120,11 @@
         tri_ref[:, 256:512] = jnp.ones((256, 256), BF16)
         carry_ref[...] = jnp.zeros_like(carry_ref)
         send_ref[...] = jnp.zeros_like(send_ref)
+        over_ref[...] = jnp.zeros_like(over_ref)
+        dests, codes = rim_rows(own_all_ref[...], node_all_ref[...])
+        for i in range(3):
+            dest_ref[i : i + 1, :] = dests[i]
+            code_ref[i : i + 1, :] = codes[i].astype(F32)
 
     for part in range(MSTEPS):
 
@@ -123,32 +151,58 @@
                 low = (turned - high.astype(F32)).astype(BF16)
                 mt_ref[at, NB + part * MROWS : NB + (part + 1) * MROWS] = low
             for k in range(R // 256 // MSTEPS):
-                cols = slice((part * (R // 256 // MSTEPS) + k) * 256, (part * (R // 256 // MSTEPS) + k + 1) * 256)
-                named = iota((ND, 256), 0) == own_all_ref[:, cols]
-                counts = dot(jnp.where(named, 1.0, 0.0).astype(BF16), tri_ref[...])
-                upto = jnp.where(named, counts[:, 0:256] + carry_ref[...], 0.0)
+                start = (part * (R // 256 // MSTEPS) + k) * 256
+                cols = slice(start, start + 256)
+                device = iota((ND, 256), 0)
+                hots = [device == own_all_ref[:, cols]] + [device == dest_ref[i : i + 1, cols] for i in range(3)]
+                main = jnp.where(hots[0], 1.0, 0.0).astype(BF16)
+                rims = jnp.where(hots[1] | hots[2] | hots[3], 1.0, 0.0).astype(BF16)
+                counts = dot(jnp.concatenate([main, rims], axis=0), tri_ref[...])
+                upto = counts[:, 0:256] + carry_ref[...]
                 carry_ref[...] += counts[:, 256:512]
-                rank_ref[:, cols] = jnp.sum(upto, axis=0, keepdims=True).astype(jnp.int32)
+                rank_ref[:, cols] = jnp.sum(jnp.where(hots[0], upto[0:ND], 0.0), axis=0, keepdims=True).astype(
+                    jnp.int32
+                )
+                for i in range(3):
+                    place = jnp.sum(jnp.where(hots[i + 1], upto[ND : 2 * ND], 0.0), axis=0, keepdims=True)
+                    over_ref[...] = jnp.maximum(over_ref[...], place)
+                    place_ref[i : i + 1, cols] = jnp.where(place < RIM - 1, place, 2.0 * RIM).astype(jnp.int32)
 
     @pl.when(step >= MSTEPS)
     def _():
+        here = pl.ds(pl.multiple_of((step - MSTEPS) * RB, RB), RB)
         w_t = w_ref[...].T
         hot = block_hot(blk_ref[...])
         picked = dot(mt_ref[...], jnp.concatenate([hot, hot], axis=0))
         values = [
             jnp.sum(picked[axis * NK : (axis + 1) * NK, :] * w_t, axis=0, keepdims=True) for axis in range(3)
         ]
-        values.append(node_ref[...].astype(F32))
+        parts = [halves(value) for value in values]
+        node = halves(node_ref[...].astype(F32))
+
+        def placed(in_slot, code):
+            both = [
+                jnp.concatenate(
+                    [jnp.where(in_slot, part[side], 0.0).astype(BF16) for part in parts + [code]], axis=0
+                )
+                for side in range(2)
+            ]
+            return jnp.concatenate(both, axis=1)
+
         named = jnp.where(iota((ND, RB), 0) == own_ref[...], 1.0, 0.0).astype(BF16)
-        rank = rank_ref[:, pl.ds(pl.multiple_of((step - MSTEPS) * RB, RB), RB)]
-        in_slot = iota((CAP, RB), 0) == rank
-        highs, lows = [], []
-        for value in values:
-            high, low = halves(value)
-            highs.append(jnp.where(in_slot, high, 0.0).astype(BF16))
-            lows.append(jnp.where(in_slot, low, 0.0).astype(BF16))
-        packed = jnp.concatenate([jnp.concatenate(highs, axis=0), jnp.concatenate(lows, axis=0)], axis=1)
-        send_ref[...] += dot_t(jnp.concatenate([named, named], axis=1), packed)
+        packed = placed(iota((CAP, RB), 0) == rank_ref[:, here], node)
+        send_ref[:, 0:MAIN] += dot_t(jnp.concatenate([named, named], axis=1), packed)
+        for i in range(3):
+            named = jnp.where(iota((ND, RB), 0) == dest_ref[i : i + 1, here], 1.0, 0.0).astype(BF16)
+            packed = placed(iota((RIM, RB), 0) == place_ref[i : i + 1, here], halves(code_ref[i : i + 1, here]))
+            send_ref[:, MAIN : MAIN + 4 * RIM] += dot_t(jnp.concatenate([named, named], axis=1), packed)
+
+    @pl.when(step == MSTEPS + RSTEPS - 1)
+    def _():
+        most = jnp.max(over_ref[...], axis=1, keepdims=True)
+        flag = jnp.where(most >= RIM - 1, 1.0, 0.0)
+        tail = send_ref[:, MAIN : MAIN + 4 * RIM]
+        send_ref[:, MAIN : MAIN + 4 * RIM] = jnp.where(iota((ND, 4 * RIM), 1) == 4 * RIM - 1, flag, tail)
 
 
 def loads_to_send(pops, weights, block_row, owner_row, node_row):
@@ -165,23 +219,28 @@
             pl.BlockSpec((RB, NK), lambda i: (record(i), 0)),
             row_spec,
             all_rows,
+            all_rows,
             row_spec,
             row_spec,
         ],
-        out_specs=[pl.BlockSpec((ND, 4 * CAP), lambda i: (0, 0)), all_rows],
+        out_specs=[pl.BlockSpec((ND, MAIN + 4 * RIM), lambda i: (0, 0)), all_rows],
         out_shape=[
-            jax.ShapeDtypeStruct((ND, 4 * CAP), F32),
+            jax.ShapeDtypeStruct((ND, MAIN + 4 * RIM), F32),
             jax.ShapeDtypeStruct((1, R), jnp.int32),
         ],
         scratch_shapes=[
             pltpu.VMEM((3, MROWS, NK), F32),
             pltpu.VMEM((3 * NK, 2 * NB), BF16),
             pltpu.VMEM((256, 512), BF16),
-            pltpu.VMEM((ND, 256), F32),
+            pltpu.VMEM((2 * ND, 256), F32),
+            pltpu.VMEM((8, R), jnp.int32),
+            pltpu.VMEM((8, R), F32),
+            pltpu.VMEM((8, R), jnp.int32),
+            pltpu.VMEM((1, 256), F32),
         ],
         compiler_params=pltpu.CompilerParams(vmem_limit_bytes=VMEM_LIMIT),
         name="loads",
-    )(pops, weights, block_row, owner_row, owner_row, node_row)
+    )(pops, weights, block_row, owner_row, node_row, owner_row, node_row)
 
 
 def collide_kernel(pop_ref, read_ref, xp_ref, xm_ref, yp_ref, ym_ref):
@@ -242,63 +301,75 @@
 
 
 def node_rows(recv_t):
-    node = recv_t[3 * CAP : 4 * CAP, :].astype(jnp.int32)
+    node = recv_t[3 * CAP : MAIN, :].astype(jnp.int32)
     return node >> 7, node & 127
 
 
-def force_kernel(recv_ref, mass_ref, mod_ref, live_ref, f_ref, low_ref, high_ref, u_ref, v_ref, hl_ref):
+def force_kernel(recv_ref, f_ref, rim_ref, u_ref, v_ref, hl_ref, ru_ref, rv_ref, rhl_ref):
     recv_t = recv_ref[...].T
     u_ref[...], v_ref[...] = node_rows(recv_t)
     high, low = halves(recv_t[0 : 3 * CAP, :])
     hl_ref[0 : 3 * CAP, :] = high
     hl_ref[3 * CAP : 6 * CAP, :] = low
-    u_of = iota((NU, ND), 0)
-    v_of = iota((NV, ND), 0)
-
-    def chunk(i, acc):
-        at = pl.multiple_of(i * 8, 8)
-        u8 = u_ref[pl.ds(at, 8), :]
-        v8 = v_ref[pl.ds(at, 8), :]
-        vals = [hl_ref[pl.ds(pl.multiple_of(part * CAP + at, 8), 8), :] for part in range(6)]
-        lhs, rhs = [], []
-        for r in range(8):
-            here = u_of == u8[r : r + 1, :]
-            lhs.append(
-                jnp.concatenate(
-                    [jnp.where(here, vals[part][r : r + 1, :], 0.0).astype(BF16) for part in range(6)], axis=0
+    code = recv_t[MAIN + 3 * RIM : MAIN + 4 * RIM, :].astype(jnp.int32)
+    ru_ref[...] = code >> 8
+    rv_ref[...] = code & 255
+    high, low = halves(recv_t[MAIN : MAIN + 3 * RIM, :])
+    rhl_ref[0 : 3 * RIM, :] = high
+    rhl_ref[3 * RIM : 6 * RIM, :] = low
+
+    def chunk_of(rows_ref, cols_ref, vals_ref, slots, height, width):
+        u_of = iota((height, ND), 0)
+        v_of = iota((width, ND), 0)
+
+        def chunk(i, acc):
+            at = pl.multiple_of(i * 8, 8)
+            u8 = rows_ref[pl.ds(at, 8), :]
+            v8 = cols_ref[pl.ds(at, 8), :]
+            vals = [vals_ref[pl.ds(pl.multiple_of(part * slots + at, 8), 8), :] for part in range(6)]
+            lhs, rhs = [], []
+            for r in range(8):
+                here = u_of == u8[r : r + 1, :]
+                lhs.append(
+                    jnp.concatenate([jnp.where(here, vals[part][r : r + 1, :], 0.0) for part in range(6)], axis=0)
+                    .astype(BF16)
                 )
-            )
-            rhs.append(jnp.where(v_of == v8[r : r + 1, :], 1.0, 0.0).astype(BF16))
-        return acc + dot_t(jnp.concatenate(lhs, axis=1), jnp.concatenate(rhs, axis=1))
-
-    acc = lax.fori_loop(0, CAP // 8, chunk, jnp.zeros((6 * NU, NV), F32))
-    fields = [acc[c * NU : (c + 1) * NU, :] + acc[(3 + c) * NU : (4 + c) * NU, :] for c in range(3)]
+                rhs.append(jnp.where(v_of == v8[r : r + 1, :], 1.0, 0.0).astype(BF16))
+            return acc + dot_t(jnp.concatenate(lhs, axis=1), jnp.concatenate(rhs, axis=1))
+
+        return lax.fori_loop(0, slots // 8, chunk, jnp.zeros((6 * height, width), F32))
+
+    acc = chunk_of(u_ref, v_ref, hl_ref, CAP, NU, NV)
     for c in range(3):
-        f_ref[c] = fields[c]
-    fields = fields + [mass_ref[...], mod_ref[...], live_ref[...].astype(F32)]
-    low_ref[...] = jnp.zeros_like(low_ref)
-    high_ref[...] = jnp.zeros_like(high_ref)
-    for i, field in enumerate(fields):
-        low_ref[i : i + 1, :] = field[NU - 1 : NU, :]
-        high_ref[2 * i : 2 * i + 2, :] = field[0:2, :]
-
-
-def force_of(recv, mass, modulus, live):
+        f_ref[c] = acc[c * NU : (c + 1) * NU, :] + acc[(3 + c) * NU : (4 + c) * NU, :]
+    acc = chunk_of(ru_ref, rv_ref, rhl_ref, RIM, 8, EV)
+    for c in range(3):
+        rim_ref[c] = acc[c * 8 : (c + 1) * 8, :] + acc[(3 + c) * 8 : (4 + c) * 8, :]
+
+
+def force_of(recv):
     return pl.pallas_call(
         force_kernel,
-        out_shape=[
-            jax.ShapeDtypeStruct((3, NU, NV), F32),
-            jax.ShapeDtypeStruct((8, 128), F32),
-            jax.ShapeDtypeStruct((16, 128), F32),
-        ],
+        out_shape=[jax.ShapeDtypeStruct((3, NU, NV), F32), jax.ShapeDtypeStruct((3, 8, EV), F32)],
         scratch_shapes=[
             pltpu.VMEM((CAP, ND), jnp.int32),
             pltpu.VMEM((CAP, ND), jnp.int32),
             pltpu.VMEM((6 * CAP, ND), F32),
+            pltpu.VMEM((RIM, ND), jnp.int32),
+            pltpu.VMEM((RIM, ND), jnp.int32),
+            pltpu.VMEM((6 * RIM, ND), F32),
         ],
         compiler_params=pltpu.CompilerParams(vmem_limit_bytes=SMALL_LIMIT),
         name="force",
-    )(recv, mass, modulus, live)
+    )(recv)
+
+
+def edge_kernel(mass_ref, mod_ref, live_ref, low_ref, high_ref):
+    low_ref[...] = jnp.zeros_like(low_ref)
+    high_ref[...] = jnp.zeros_like(high_ref)
+    for i, field in enumerate([mass_ref[...], mod_ref[...], live_ref[...].astype(F32)]):
+        low_ref[i : i + 1, :] = field[NU - 1 : NU, :]
+        high_ref[2 * i : 2 * i + 2, :] = field[0:2, :]
 
 
 def rim_tile(i, low_ref, high_ref):
@@ -308,11 +379,10 @@
     return jnp.where(sub == 7, low_ref[i : i + 1, :], tile)
 
 
-def rim_kernel(f_ref, mass_ref, mod_ref, live_ref, low_ref, high_ref, to_low_ref, to_high_ref):
-    fields = [f_ref[0], f_ref[1], f_ref[2], mass_ref[...], mod_ref[...], live_ref[...].astype(F32)]
+def side_kernel(mass_ref, mod_ref, live_ref, low_ref, high_ref, to_low_ref, to_high_ref):
     to_low_ref[...] = jnp.zeros_like(to_low_ref)
     to_high_ref[...] = jnp.zeros_like(to_high_ref)
-    for i, field in enumerate(fields):
+    for i, field in enumerate([mass_ref[...], mod_ref[...], live_ref[...].astype(F32)]):
         whole = jnp.concatenate(
             [field, rim_tile(i, low_ref, high_ref), jnp.zeros((128 - EU, 128), F32)], axis=0
         )
@@ -321,30 +391,51 @@
         to_high_ref[2 * i : 2 * i + 2, :] = turned[0:2, :]
 
 
-def rim_columns(force, mass, modulus, live, low, high):
+def edge_call(kernel, name, *args):
     return pl.pallas_call(
-        rim_kernel,
-        out_shape=[jax.ShapeDtypeStruct((8, 128), F32), jax.ShapeDtypeStruct((16, 128), F32)],
+        kernel,
+        out_shape=[jax.ShapeDtypeStruct((8, 128), F32), jax.ShapeDtypeStruct((8, 128), F32)],
         compiler_params=pltpu.CompilerParams(vmem_limit_bytes=SMALL_LIMIT),
-        name="rim",
-    )(force, mass, modulus, live, low, high)
+        name=name,
+    )(*args)
+
+
+def static_rims(mass, modulus, live):
+    low, high = edge_call(edge_kernel, "edges", mass, modulus, live)
+    ulow = pass_on(low, "gx", 1)
+    uhigh = pass_on(high, "gx", -1)
+    low, high = edge_call(side_kernel, "sides", mass, modulus, live, ulow, uhigh)
+    return ulow, uhigh, pass_on(low, "gy", 1), pass_on(high, "gy", -1)
 
 
 def shell_kernel(
-    stiff_ref, f_ref, mass_ref, mod_ref, live_ref, ulow_ref, uhigh_ref, vlow_ref, vhigh_ref, recv_ref,
+    stiff_ref, f_ref, rim_ref, mass_ref, mod_ref, live_ref, ulow_ref, uhigh_ref, vlow_ref, vhigh_ref, recv_ref,
     y_ref, ret_ref,
     e_ref, c_ref, g_ref, y_ext_ref, fy_ref, u_ref, v_ref, rt_ref,
 ):
-    fields = [f_ref[0], f_ref[1], f_ref[2], mass_ref[...], mod_ref[...], live_ref[...].astype(F32)]
     sub = iota((8, 128), 0)
-    for i, field in enumerate(fields):
-        e_ref[i, 0:NU, 0:NV] = field
-        e_ref[i, NU:EU, 0:NV] = rim_tile(i, ulow_ref, uhigh_ref)
-        first = jnp.where(sub == 0, vhigh_ref[2 * i : 2 * i + 1, :], 0.0)
-        first = jnp.where(sub == 1, vhigh_ref[2 * i + 1 : 2 * i + 2, :], first)
-        last = jnp.where(sub == 7, vlow_ref[i : i + 1, :], 0.0)
-        side = jnp.concatenate([first, jnp.zeros((112, 128), F32), last], axis=0).T
-        e_ref[i, :, NV:EV] = side[0:EU, :]
+
+    def columns(near, far, before):
+        first = jnp.where(sub == 0, near, 0.0)
+        first = jnp.where(sub == 1, far, first)
+        last = jnp.where(sub == 7, before, 0.0)
+        return jnp.concatenate([first, jnp.zeros((112, 128), F32), last], axis=0).T
+
+    for i, field in enumerate([mass_ref[...], mod_ref[...], live_ref[...].astype(F32)]):
+        e_ref[3 + i, 0:NU, 0:NV] = field
+        e_ref[3 + i, NU:EU, 0:NV] = rim_tile(i, ulow_ref, uhigh_ref)
+        side = columns(
+            vhigh_ref[2 * i : 2 * i + 1, :], vhigh_ref[2 * i + 1 : 2 * i + 2, :], vlow_ref[i : i + 1, :]
+        )
+        e_ref[3 + i, :, NV:EV] = side[0:EU, :]
+    wide = iota((8, EV), 0)
+    for i in range(3):
+        e_ref[i, 0:NU, 0:NV] = f_ref[i]
+        tile = jnp.where(wide == 0, rim_ref[i, 1:2, :], 0.0)
+        tile = jnp.where(wide == 1, rim_ref[i, 2:3, :], tile)
+        e_ref[i, NU:EU, :] = jnp.where(wide == 7, rim_ref[i, 0:1, :], tile)
+        side = columns(rim_ref[i, 4:5, 0:128], rim_ref[i, 5:6, 0:128], rim_ref[i, 3:4, 0:128])
+        e_ref[i, 0:NU, NV:EV] = side[0:NU, :]
 
     def up(x):
         return pltpu.roll(x, EU - 1, 0)
@@ -422,13 +513,15 @@
     for i in range(4):
         whole = jnp.sum(jnp.sum(sums[i], axis=0, keepdims=True), axis=1, keepdims=True)
         moments = jnp.where(lane == i, whole, moments)
+    over = jnp.max(recv_ref[:, MAIN + 4 * RIM - 1 : MAIN + 4 * RIM], axis=0, keepdims=True)
+    moments = jnp.where(lane == 4, over, moments)
 
     for c in range(3):
         for part, field in ((c, f_ref[c]), (3 + c, y_ref[c])):
             high = field.astype(BF16)
             fy_ref[part * NU : (part + 1) * NU, 0:NV] = high
             fy_ref[part * NU : (part + 1) * NU, NV : 2 * NV] = (field - high.astype(F32)).astype(BF16)
-    u_ref[...], v_ref[...] = node_rows(recv_ref[...].T)
+    u_ref[...], v_ref[...] = node_rows(recv_ref[:, 0:MAIN].T)
     u_of = iota((NU, ND), 0)
     v_of = iota((NV, ND), 0)
 
@@ -456,11 +549,11 @@
     ret_ref[:, 6 * CAP : 8 * CAP] = jnp.broadcast_to(moments, (ND, 128))
 
 
-def shell_of(stiff, force, mass, modulus, live, ulow, uhigh, vlow, vhigh, recv):
+def shell_of(stiff, force, rim, mass, modulus, live, rims, recv):
     vmem = pl.BlockSpec(memory_space=pltpu.VMEM)
     return pl.pallas_call(
         shell_kernel,
-        in_specs=[pl.BlockSpec(memory_space=pltpu.SMEM)] + [vmem] * 9,
+        in_specs=[pl.BlockSpec(memory_space=pltpu.SMEM)] + [vmem] * 10,
         out_specs=[vmem, vmem],
         out_shape=[
             jax.ShapeDtypeStruct((3, NU, NV), F32),
@@ -478,14 +571,14 @@
         ],
         compiler_params=pltpu.CompilerParams(vmem_limit_bytes=SMALL_LIMIT),
         name="shell",
-    )(stiff, force, mass, modulus, live, ulow, uhigh, vlow, vhigh, recv)
+    )(stiff, force, rim, mass, modulus, live, *rims, recv)
 
 
 def scalar_kernel(part_ref, pq_ref, sound_ref):
     row = jnp.sum(part_ref[...], axis=0, keepdims=True)
     lane = iota((1, 128), 1)
-    m0, m1, m2, m3 = [
-        jnp.sum(jnp.where(lane == i, row, 0.0), axis=1, keepdims=True) for i in range(4)
+    m0, m1, m2, m3, over = [
+        jnp.sum(jnp.where(lane == i, row, 0.0), axis=1, keepdims=True) for i in range(5)
     ]
     first = m0 / m1
     left_over = first * first * m2 - m0
@@ -494,7 +587,8 @@
     curve = gain * gain * m1 - 2.0 * gain * first * m2 + first * first * m3
     second = left_over / curve
     sound = (
-        (left_over > 1e-3 * m0)
+        (over == 0.0)
+        & (left_over > 1e-3 * m0)
         & (curve > 1e-2 * gain * gain * m1)
         & (curve < 1e30)
         & (m1 > 1e-30)
@@ -502,8 +596,6 @@
     )
     pq_ref[0] = (first + second * gain)[0, 0]
     pq_ref[1] = -(first * second)[0, 0]
-    pq_ref[2] = first[0, 0]
-    pq_ref[3] = m0[0, 0]
     sound_ref[0] = jnp.where(sound, 1, 0)[0, 0]
 
 
@@ -514,7 +606,7 @@
         grid=(1,),
         in_specs=[pl.BlockSpec((ND, 128), lambda i: (0, 3))],
         out_specs=[smem, smem],
-        out_shape=[jax.ShapeDtypeStruct((4,), F32), jax.ShapeDtypeStruct((1,), jnp.int32)],
+        out_shape=[jax.ShapeDtypeStruct((2,), F32), jax.ShapeDtypeStruct((1,), jnp.int32)],
         name="scalars",
     )(back)
 
@@ -671,14 +763,37 @@
     )
 
 
+def rim_of(force):
+    before = pass_on(force[:, NU - 1 : NU, :], "gx", 1)
+    after = pass_on(force[:, 0:2, :], "gx", -1)
+    tall = jnp.concatenate([force, after, before], axis=1)
+    left = pass_on(tall[:, :, NV - 1 : NV], "gy", 1)
+    right = pass_on(tall[:, :, 0:2], "gy", -1)
+    gap = jnp.zeros((3, EV - NV - 3), F32)
+    rows = [
+        jnp.concatenate([tall[:, r], right[:, r], gap, left[:, r]], axis=1) for r in (NU + 2, NU, NU + 1)
+    ]
+    beside = [
+        jnp.concatenate([column[:, 0:NU], jnp.zeros((3, EV - NU), F32)], axis=1)
+        for column in (left[:, :, 0], right[:, :, 0], right[:, :, 1])
+    ]
+    empty = jnp.zeros((3, EV), F32)
+    return jnp.stack(rows + beside + [empty, empty], axis=1)
+
+
+def exchange(x):
+    return lax.all_to_all(x, ALL, 0, 0, tiled=True)
+
+
 def per_device(populations, mass, modulus, live, stiff, rec_block, rec_owner, rec_node, weights):
     pops = populations.reshape(19, NB, NK)
     block_row = rec_block.reshape(1, R)
     owner_row = rec_owner.reshape(1, R)
     node_row = rec_node.reshape(1, R)
 
+    rims = static_rims(mass, modulus, live)
     send, rank_row = loads_to_send(pops, weights, block_row, owner_row, node_row)
-    recv = lax.all_to_all(send, ALL, 0, 0, tiled=True)
+    recv = exchange(send)
 
     read, xp, xm, yp, ym = collide_and_run(pops)
     xp = pass_on(xp, "gx", 1)
@@ -688,33 +803,33 @@
     yp = pass_on(yp, "gy", 1)
     ym = pass_on(ym, "gy", -1)
 
-    force, low, high = force_of(recv, mass, modulus, live)
-    ulow = pass_on(low, "gx", 1)
-    uhigh = pass_on(high, "gx", -1)
-    low, high = rim_columns(force, mass, modulus, live, ulow, uhigh)
-    vlow = pass_on(low, "gy", 1)
-    vhigh = pass_on(high, "gy", -1)
-    image, ret = shell_of(stiff, force, mass, modulus, live, ulow, uhigh, vlow, vhigh, recv)
-    back = lax.all_to_all(ret, ALL, 0, 0, tiled=True)
+    force, rim = force_of(recv)
+    image, ret = shell_of(stiff, force, rim, mass, modulus, live, rims, recv)
+    back = exchange(ret)
 
     back, yp, ym = lax.optimization_barrier((back, yp, ym))
     pq, sound = scalars_of(back)
 
     def quick(operands):
-        return operands[0]
+        return operands[0:3]
 
     def careful(operands):
-        pq, force, image, mass, modulus, live, stiff = operands
-        first = pq[2]
+        _, _, _, force, mass, modulus, live, stiff, rims, recv = operands
+        image, ret = shell_of(stiff, force, rim_of(force), mass, modulus, live, rims, recv)
+        back = exchange(ret)
+        start = lax.psum(jnp.sum(force * force), ALL)
+        first = start / lax.psum(jnp.sum(force * image), ALL)
         residual = force - first * image
         norm = lax.psum(jnp.sum(residual * residual), ALL)
-        ratio = norm / pq[3]
+        ratio = norm / start
         direction = residual + ratio * force
         along = operate(direction, mass, modulus, live, stiff)
         second = norm / lax.psum(jnp.sum(direction * along), ALL)
-        return jnp.stack([first + second * (1.0 + ratio), -(first * second), first, pq[3]])
-
-    pq = lax.cond(sound[0] == 1, quick, careful, (pq, force, image, mass, modulus, live, stiff))
+        return jnp.stack([first + second * (1.0 + ratio), -(first * second)]), image, back
+
+    pq, image, back = lax.cond(
+        sound[0] == 1, quick, careful, (pq, image, back, force, mass, modulus, live, stiff, rims, recv)
+    )
 
     populations_next, displacement = outputs_of(
         pq, back, weights, block_row, owner_row, rank_row, force, image, read, xp, xm, yp, ym

time: 96.5 us -> 95.9 us (level)
  starting transfers between devices: 30.8 us -> 25.6 us
  Pallas kernels: 46.4 us -> 50 us
  waiting for transfers between devices: 13.3 us -> 14.9 us
    all_to_all x2, starting transfers between devices: 20.2 us -> 14.5 us  [exchange(): return lax.all_to_all(x, ALL, 0, 0, tiled=True)]
    all_to_all x2, waiting for transfers between devices: 9.23 us -> 14.9 us  [exchange(): return lax.all_to_all(x, ALL, 0, 0, tiled=True)]
    ppermute x8, waiting for transfers between devices: 4.06 us -> 0.02 us  [pass_on(): lax.ppermute(x, axis, [(i, (i + shift) % count) for i in range(count)])]
    pallas_call x1, Pallas kernels: 11.7 us -> 15.2 us  [loads_to_send(): pl.pallas_call(load_kernel, grid=(MSTEPS + RSTEPS,), in_specs=[pl.BlockSp...]
    pallas_call x1, Pallas kernels: 3.24 us -> 4.32 us  [force_of(): pl.pallas_call(force_kernel, out_shape=[jax.ShapeDtypeStruct((3, NU, NV),...]
  transfers between devices with their start and end apart: 10 -> 10, of which waited for: 4 -> 2; matrix products, arithmetic and copies ran while one was open for 2% -> 3% of each run, Pallas kernels for 20% -> 27%
where the time goes in v2:
time: 95.9 us; the launch traced here: 95.5 us
  Pallas kernels  50 us (52%)
  starting transfers between devices  25.6 us (27%)
  waiting for transfers between devices  14.9 us (16%)
  local copies, waits for them, and re-layouts  3.04 us (3%)
  between operations  1.72 us (2%)
    pallas_call x1, Pallas kernels, loads_to_send(): pl.pallas_call(load_kernel, grid=(MSTEPS + RSTEPS,), in_specs=[pl.BlockSp...  15.2 us
    all_to_all x2, waiting for transfers between devices, exchange(): return lax.all_to_all(x, ALL, 0, 0, tiled=True)  14.9 us
    all_to_all x2, starting transfers between devices, exchange(): return lax.all_to_all(x, ALL, 0, 0, tiled=True)  14.5 us
    pallas_call x1, Pallas kernels, outputs_of(): pl.pallas_call(next_kernel, grid=(RSTEPS + OSTEPS,), in_specs=[pl.BlockSp...  13.8 us
    ppermute x8, starting transfers between devices, pass_on(): lax.ppermute(x, axis, [(i, (i + shift) % count) for i in range(count)])  11.2 us
    pallas_call x1, Pallas kernels, collide_and_run(): pl.pallas_call(collide_kernel, out_shape=[jax.ShapeDtypeStruct((19, NB, N...  9.5 us
    pallas_call x1, Pallas kernels, shell_of(): pl.pallas_call(shell_kernel, in_specs=[pl.BlockSpec(memory_space=pltpu.SM...  6.28 us
    pallas_call x1, Pallas kernels, force_of(): pl.pallas_call(force_kernel, out_shape=[jax.ShapeDtypeStruct((3, NU, NV),...  4.32 us
  transfers between devices with their start and end apart: 10, of which 2 were waited for; matrix products, arithmetic and copies ran while one was open for 3% of the time, Pallas kernels for 27%

profile of v2, /device:TPU:1, one launch (start us, length us, event | category | flops | bytes accessed | tf_op | source)
XLA Modules:
  0.0 95.5 jit_solution(13402819439690326781)
XLA Ops:
  0.6 0.0 copy-start
  0.6 0.0 copy-start.3
  0.7 0.0 copy-start.4
  0.7 9.5 %collide.1 = (f32[19,256,256]{2,1,0:T(8,128)}, f32[5,8,256]{2,1,0:T(8,128)}, f32[5,8,256]{2,1,0:T(8,128)}, f32[5,32,256]{2,1,0:T(8,128)}, f32[5,32,256]{2,1,0:T(8,128)}) custom-call(f32[19,256,256]{2,1,0:T(8,128)} %bitcast.64), custom_call_target="tpu_custom_call" | custom-call | tf_op jit(solution)/shard_map/collide/pallas_call | solution.py:289
  10.2 2.1 %collective-permute-start.16 = (f32[5,8,256]{2,1,0:T(8,128)}, f32[5,8,256]{2,1,0:T(8,128)S(1)}, u32[]{:S(2)}, u32[]{:S(2)}) collective-permute-start(f32[5,8,256]{2,1,0:T(8,128)} %get-tuple-element.122), channel_id=1, source_target_pairs={{0,32},{32,64},{64,96},{96,0},{1,33},{33,65},{65,97},{97,1},{2,34}... | collective-permute-start | bytes 122888 | tf_op jit(solution)/shard_map/ppermute | solution.py:734
  12.3 0.0 copy-done
  12.3 0.0 copy-done.3
  12.3 0.0 copy-done.4
  12.3 1.4 %collective-permute-start.12 = (f32[8,128]{1,0:T(8,128)S(1)}, f32[8,128]{1,0:T(8,128)S(1)}, u32[]{:S(2)}, u32[]{:S(2)}) collective-permute-start(f32[8,128]{1,0:T(8,128)S(1)} %get-tuple-element.116), channel_id=1, source_target_pairs={{0,32},{32,64},{64,96},{96,0},{1,33},{33,65},{65,97},{97,1},{2,34}... | collective-permute-start | bytes 12296 | tf_op jit(solution)/shard_map/ppermute | solution.py:734
  13.7 1.4 %collective-permute-start.13 = (f32[8,128]{1,0:T(8,128)S(1)}, f32[8,128]{1,0:T(8,128)S(1)}, u32[]{:S(2)}, u32[]{:S(2)}) collective-permute-start(f32[8,128]{1,0:T(8,128)S(1)} %get-tuple-element.117), channel_id=1, source_target_pairs={{0,96},{32,0},{64,32},{96,64},{1,97},{33,1},{65,33},{97,65},{2,98}... | collective-permute-start | bytes 12296 | tf_op jit(solution)/shard_map/ppermute | solution.py:734
  15.0 15.2 %loads.1 = (f32[128,384]{1,0:T(8,128)}, s32[1,4096]{1,0:T(1,128)}) custom-call(f32[19,256,256]{2,1,0:T(8,128)} %bitcast.65, f32[4096,256]{1,0:T(8,128)} %w_ref.3, s32[1,4096]{1,0:T(1,128)} %bitcast.83, s32[1,4096]{1,0:T(1,128)} %bitcast.78, s32[1,4096]{1,0:T(1,128)} %bitcast.81, s32[1,4096]{1,0:T(1,128)} %bitcast.79, s32[1,4096]{1,0:T(1,128)} %bitcast.82), custom_call_target="tpu_custom_call" | custom-call | tf_op jit(solution)/shard_map/loads/pallas_call | solution.py:214
  30.3 1.8 %copy.53 = f32[128,1,384]{2,1,0:T(1,128)} copy(f32[128,1,384]{2,0,1:T(8,128)} %bitcast.77) | data formatting | bytes 393216 | tf_op jit(solution)/shard_map/all_to_all | solution.py:785
  32.1 10.0 %all-to-all-start.1 = ((f32[128,1,384]{2,1,0:T(1,128)}), f32[128,1,384]{2,1,0:T(1,128)S(1)}, u32[]{:S(2)}, u32[]{:S(2)}) async-start(f32[128,1,384]{2,1,0:T(1,128)} %copy.53), calls=%async_computation.1 | async-start | bytes 393216 | tf_op jit(solution)/shard_map/all_to_all | solution.py:785
  42.1 0.0 copy-done.12
  42.1 2.7 %collective-permute-start.17 = (f32[5,8,256]{2,1,0:T(8,128)S(1)}, f32[5,8,256]{2,1,0:T(8,128)S(1)}, u32[]{:S(2)}, u32[]{:S(2)}) collective-permute-start(f32[5,8,256]{2,1,0:T(8,128)S(1)} %copy-done.12), channel_id=1, source_target_pairs={{0,96},{32,0},{64,32},{96,64},{1,97},{33,1},{65,33},{97,65},{2,98}... | collective-permute-start | bytes 122888 | tf_op jit(solution)/shard_map/ppermute | solution.py:734
  44.8 0.0 collective-permute-done.12.low_ref.ulow_ref
  44.8 0.0 collective-permute-done.13.high_ref.uhigh_ref
  44.8 0.1 sides.1
  44.9 0.0 copy-start.11
  45.0 1.8 %collective-permute-start.14 = (f32[8,128]{1,0:T(8,128)S(1)}, f32[8,128]{1,0:T(8,128)S(1)}, u32[]{:S(2)}, u32[]{:S(2)}) collective-permute-start(f32[8,128]{1,0:T(8,128)S(1)} %get-tuple-element.118), channel_id=1, source_target_pairs={{0,1},{1,2},{2,3},{3,4},{4,5},{5,6},{6,7},{7,8},{8,9},{9,10},{10,1... | collective-permute-start | bytes 12296 | tf_op jit(solution)/shard_map/ppermute | solution.py:734
  46.8 0.0 collective-permute-start.15
  46.8 0.0 collective-permute-done.16.xp_ref
  46.8 0.0 copy-start.8
  46.8 5.7 %all-to-all-done.1 = f32[128,1,384]{2,1,0:T(1,128)S(1)} async-done(((f32[128,1,384]{2,1,0:T(1,128)}), f32[128,1,384]{2,1,0:T(1,128)S(1)}, u32[]{:S(2)}, u32[]{:S(2)}) %all-to-all-start.1) | async-done | bytes 196640 | tf_op jit(solution)/shard_map/all_to_all | solution.py:785
  52.5 4.3 %force.1 = (f32[3,64,128]{2,1,0:T(8,128)S(1)}, f32[3,8,256]{2,1,0:T(8,128)S(1)}) custom-call(f32[128,384]{1,0:T(8,128)S(1)} %bitcast.66), custom_call_target="tpu_custom_call" | custom-call | tf_op jit(solution)/shard_map/force/pallas_call | solution.py:351
  56.8 0.0 collective-permute-done.14.vlow_ref
  56.8 0.0 collective-permute-done.15.vhigh_ref
  56.8 0.0 copy-done.7
  56.8 6.3 %shell.3 = (f32[3,64,128]{2,1,0:T(8,128)S(1)}, f32[128,512]{1,0:T(8,128)S(1)}) custom-call(f32[12,12]{1,0:T(8,128)S(1)} %copy-done.7, f32[3,64,128]{2,1,0:T(8,128)S(1)} %get-tuple-element.114.f_ref, f32[3,8,256]{2,1,0:T(8,128)S(1)} %get-tuple-element.115.rim_ref, f32[64,128]{1,0:T(8,128)S(1)} %copy-done.3, f32[64,128]{1,0:T(8,128)S(1)} %copy-done, ...), custom_call_target="tpu_custom_call" | custom-call | tf_op jit(solution)/shard_map/shell/pallas_call | solution.py:554
  63.1 1.0 %copy.54 = f32[128,1,512]{2,1,0:T(1,128)} copy(f32[128,1,512]{2,0,1:T(8,128)S(1)} %bitcast.63) | data formatting | bytes 524288 | tf_op jit(solution)/shard_map/all_to_all | solution.py:785
  64.1 4.5 %all-to-all-start.2 = ((f32[128,1,512]{2,1,0:T(1,128)}), f32[128,1,512]{2,1,0:T(1,128)S(1)}, u32[]{:S(2)}, u32[]{:S(2)}) async-start(f32[128,1,512]{2,1,0:T(1,128)} %copy.54), calls=%async_computation.2 | async-start | bytes 524288 | tf_op jit(solution)/shard_map/all_to_all | solution.py:785
  68.6 0.0 collective-permute-done.17.xm_ref
  68.6 0.0 copy-start.9
  68.6 0.0 copy-done.11
  68.7 1.7 %collective-permute-start.18 = (f32[5,32,256]{2,1,0:T(8,128)S(1)}, f32[5,32,256]{2,1,0:T(8,128)S(1)}, u32[]{:S(2)}, u32[]{:S(2)}) collective-permute-start(f32[5,32,256]{2,1,0:T(8,128)S(1)} %scatter.15), channel_id=1, source_target_pairs={{0,1},{1,2},{2,3},{3,4},{4,5},{5,6},{6,7},{7,8},{8,9},{9,10},{10,1... | collective-permute-start | bytes 491528 | tf_op jit(solution)/shard_map/ppermute | solution.py:734
  70.4 0.0 copy-done.8
  70.4 0.0 copy-done.10
  70.5 0.1 collective-permute-start.19
  70.6 9.2 %all-to-all-done.2 = f32[128,1,512]{2,1,0:T(1,128)S(1)} async-done(((f32[128,1,512]{2,1,0:T(1,128)}), f32[128,1,512]{2,1,0:T(1,128)S(1)}, u32[]{:S(2)}, u32[]{:S(2)}) %all-to-all-start.2) | async-done | bytes 262176 | tf_op jit(solution)/shard_map/all_to_all | solution.py:785
  79.8 0.0 collective-permute-done.18.yp_ref
  79.8 0.0 copy-start.5
  79.8 0.0 collective-permute-done.19.ym_ref
  79.8 0.0 copy-start.6
  79.9 0.8 scalars.1
  81.3 0.0 copy-done.6
  81.3 0.0 copy-done.9
  81.3 0.2 conditional.1
  81.5 13.8 %outputs.1 = (f32[19,256,256]{2,1,0:T(8,128)}, f32[3,64,128]{2,1,0:T(8,128)}) custom-call(f32[2]{0:T(128)S(1)} %get-tuple-element.129.pq_ref, f32[128,512]{1,0:T(8,128)S(1)} %get-tuple-element.130.back_ref, f32[4096,256]{1,0:T(8,128)} %w_ref.3, s32[1,4096]{1,0:T(1,128)} %bitcast.84, s32[1,4096]{1,0:T(1,128)} %bitcast.80, ...), custom_call_target="tpu_custom_call" | custom-call | tf_op jit(solution)/shard_map/outputs/pallas_call | solution.py:699
  (13 shorter events, 0.2 us)
Async XLA Ops:
  0.6 11.7 %copy-start = (f32[64,128]{1,0:T(8,128)S(1)}, f32[64,128]{1,0:T(8,128)}, u32[]{:S(2)}) copy-start(f32[64,128]{1,0:T(8,128)} %mod_ref.5) | copy-start | bytes 98308
  0.6 11.6 %copy-start.3 = (f32[64,128]{1,0:T(8,128)S(1)}, f32[64,128]{1,0:T(8,128)}, u32[]{:S(2)}) copy-start(f32[64,128]{1,0:T(8,128)} %mass_ref.5) | copy-start | bytes 98308
  0.7 11.6 %copy-start.4 = (s32[64,128]{1,0:T(8,128)S(1)}, s32[64,128]{1,0:T(8,128)}, u32[]{:S(2)}) copy-start(s32[64,128]{1,0:T(8,128)} %live_ref.5) | copy-start | bytes 98308
  10.2 36.6 %collective-permute-start.16 = (f32[5,8,256]{2,1,0:T(8,128)}, f32[5,8,256]{2,1,0:T(8,128)S(1)}, u32[]{:S(2)}, u32[]{:S(2)}) collective-permute-start(f32[5,8,256]{2,1,0:T(8,128)} %get-tuple-element.122), channel_id=1, source_target_pairs={{0,32},{32,64},{64,96},{96,0},{1,33},{33,65},{65,97},{97,1},{2,34}... | collective-permute-start | bytes 122888 | tf_op jit(solution)/shard_map/ppermute | solution.py:734
  12.3 32.5 %collective-permute-start.12 = (f32[8,128]{1,0:T(8,128)S(1)}, f32[8,128]{1,0:T(8,128)S(1)}, u32[]{:S(2)}, u32[]{:S(2)}) collective-permute-start(f32[8,128]{1,0:T(8,128)S(1)} %get-tuple-element.116), channel_id=1, source_target_pairs={{0,32},{32,64},{64,96},{96,0},{1,33},{33,65},{65,97},{97,1},{2,34}... | collective-permute-start | bytes 12296 | tf_op jit(solution)/shard_map/ppermute | solution.py:734
  13.7 31.2 %collective-permute-start.13 = (f32[8,128]{1,0:T(8,128)S(1)}, f32[8,128]{1,0:T(8,128)S(1)}, u32[]{:S(2)}, u32[]{:S(2)}) collective-permute-start(f32[8,128]{1,0:T(8,128)S(1)} %get-tuple-element.117), channel_id=1, source_target_pairs={{0,96},{32,0},{64,32},{96,64},{1,97},{33,1},{65,33},{97,65},{2,98}... | collective-permute-start | bytes 12296 | tf_op jit(solution)/shard_map/ppermute | solution.py:734
  15.0 27.0 %copy-start.12 = (f32[5,8,256]{2,1,0:T(8,128)S(1)}, f32[5,8,256]{2,1,0:T(8,128)}, u32[]{:S(2)}) copy-start(f32[5,8,256]{2,1,0:T(8,128)} %get-tuple-element.123) | copy-start | bytes 122884
  30.2 26.6 %copy-start.7 = (f32[12,12]{1,0:T(8,128)S(1)}, f32[12,12]{1,0:T(8,128)}, u32[]{:S(2)}) copy-start(f32[12,12]{1,0:T(8,128)} %stiff_ref.1) | copy-start | bytes 1732
  32.1 20.4 %all-to-all-start.1 = ((f32[128,1,384]{2,1,0:T(1,128)}), f32[128,1,384]{2,1,0:T(1,128)S(1)}, u32[]{:S(2)}, u32[]{:S(2)}) async-start(f32[128,1,384]{2,1,0:T(1,128)} %copy.53), calls=%async_computation.1 | async-start | bytes 393216 | tf_op jit(solution)/shard_map/all_to_all | solution.py:785
  42.1 26.5 %collective-permute-start.17 = (f32[5,8,256]{2,1,0:T(8,128)S(1)}, f32[5,8,256]{2,1,0:T(8,128)S(1)}, u32[]{:S(2)}, u32[]{:S(2)}) collective-permute-start(f32[5,8,256]{2,1,0:T(8,128)S(1)} %copy-done.12), channel_id=1, source_target_pairs={{0,96},{32,0},{64,32},{96,64},{1,97},{33,1},{65,33},{97,65},{2,98}... | collective-permute-start | bytes 122888 | tf_op jit(solution)/shard_map/ppermute | solution.py:734
  44.9 23.7 %copy-start.11 = (f32[5,32,256]{2,1,0:T(8,128)S(1)}, f32[5,32,256]{2,1,0:T(8,128)}, u32[]{:S(2)}) copy-start(f32[5,32,256]{2,1,0:T(8,128)} %get-tuple-element.121) | copy-start | bytes 491524
  45.0 11.9 %collective-permute-start.14 = (f32[8,128]{1,0:T(8,128)S(1)}, f32[8,128]{1,0:T(8,128)S(1)}, u32[]{:S(2)}, u32[]{:S(2)}) collective-permute-start(f32[8,128]{1,0:T(8,128)S(1)} %get-tuple-element.118), channel_id=1, source_target_pairs={{0,1},{1,2},{2,3},{3,4},{4,5},{5,6},{6,7},{7,8},{8,9},{9,10},{10,1... | collective-permute-start | bytes 12296 | tf_op jit(solution)/shard_map/ppermute | solution.py:734
  46.7 23.7 %copy-start.10 = (f32[5,32,256]{2,1,0:T(8,128)S(1)}, f32[5,32,256]{2,1,0:T(8,128)}, u32[]{:S(2)}) copy-start(f32[5,32,256]{2,1,0:T(8,128)} %get-tuple-element.124) | copy-start | bytes 491524
  46.8 10.1 %collective-permute-start.15 = (f32[8,128]{1,0:T(8,128)S(1)}, f32[8,128]{1,0:T(8,128)S(1)}, u32[]{:S(2)}, u32[]{:S(2)}) collective-permute-start(f32[8,128]{1,0:T(8,128)S(1)} %get-tuple-element.119), channel_id=1, source_target_pairs={{0,31},{1,0},{2,1},{3,2},{4,3},{5,4},{6,5},{7,6},{8,7},{9,8},{10,9... | collective-permute-start | bytes 12296 | tf_op jit(solution)/shard_map/ppermute | solution.py:734
  46.8 23.7 %copy-start.8 = (f32[5,8,256]{2,1,0:T(8,128)}, f32[5,8,256]{2,1,0:T(8,128)S(1)}, u32[]{:S(2)}) copy-start(f32[5,8,256]{2,1,0:T(8,128)S(1)} %collective-permute-done.16.xp_ref) | copy-start | bytes 122884
  64.1 15.7 %all-to-all-start.2 = ((f32[128,1,512]{2,1,0:T(1,128)}), f32[128,1,512]{2,1,0:T(1,128)S(1)}, u32[]{:S(2)}, u32[]{:S(2)}) async-start(f32[128,1,512]{2,1,0:T(1,128)} %copy.54), calls=%async_computation.2 | async-start | bytes 524288 | tf_op jit(solution)/shard_map/all_to_all | solution.py:785
  68.6 12.7 %copy-start.9 = (f32[5,8,256]{2,1,0:T(8,128)}, f32[5,8,256]{2,1,0:T(8,128)S(1)}, u32[]{:S(2)}) copy-start(f32[5,8,256]{2,1,0:T(8,128)S(1)} %collective-permute-done.17.xm_ref) | copy-start | bytes 122884
  68.7 11.1 %collective-permute-start.18 = (f32[5,32,256]{2,1,0:T(8,128)S(1)}, f32[5,32,256]{2,1,0:T(8,128)S(1)}, u32[]{:S(2)}, u32[]{:S(2)}) collective-permute-start(f32[5,32,256]{2,1,0:T(8,128)S(1)} %scatter.15), channel_id=1, source_target_pairs={{0,1},{1,2},{2,3},{3,4},{4,5},{5,6},{6,7},{7,8},{8,9},{9,10},{10,1... | collective-permute-start | bytes 491528 | tf_op jit(solution)/shard_map/ppermute | solution.py:734
  70.5 9.3 %collective-permute-start.19 = (f32[5,32,256]{2,1,0:T(8,128)S(1)}, f32[5,32,256]{2,1,0:T(8,128)S(1)}, u32[]{:S(2)}, u32[]{:S(2)}) collective-permute-start(f32[5,32,256]{2,1,0:T(8,128)S(1)} %scatter.19), channel_id=1, source_target_pairs={{0,31},{1,0},{2,1},{3,2},{4,3},{5,4},{6,5},{7,6},{8,7},{9,8},{10,9... | collective-permute-start | bytes 491528 | tf_op jit(solution)/shard_map/ppermute | solution.py:734
  79.8 1.5 %copy-start.5 = (f32[5,32,256]{2,1,0:T(8,128)}, f32[5,32,256]{2,1,0:T(8,128)S(1)}, u32[]{:S(2)}) copy-start(f32[5,32,256]{2,1,0:T(8,128)S(1)} %collective-permute-done.18.yp_ref) | copy-start | bytes 491524
  79.8 1.4 %copy-start.6 = (f32[5,32,256]{2,1,0:T(8,128)}, f32[5,32,256]{2,1,0:T(8,128)S(1)}, u32[]{:S(2)}) copy-start(f32[5,32,256]{2,1,0:T(8,128)S(1)} %collective-permute-done.19.ym_ref) | copy-start | bytes 491524

commit v3 on v2

--- a/solution.py
+++ b/solution.py
@@ -278,7 +278,7 @@
             read_ref[q, to, :] = relaxed
         return 0
 
-    lax.fori_loop(0, 32, line, 0)
+    lax.fori_loop(0, 32, line, 0, unroll=4)
     for i, q in enumerate(XP):
         xp_ref[i] = read_ref[q, 0:8, :]
     for i, q in enumerate(XM):
@@ -398,14 +398,6 @@
         compiler_params=pltpu.CompilerParams(vmem_limit_bytes=SMALL_LIMIT),
         name=name,
     )(*args)
-
-
-def static_rims(mass, modulus, live):
-    low, high = edge_call(edge_kernel, "edges", mass, modulus, live)
-    ulow = pass_on(low, "gx", 1)
-    uhigh = pass_on(high, "gx", -1)
-    low, high = edge_call(side_kernel, "sides", mass, modulus, live, ulow, uhigh)
-    return ulow, uhigh, pass_on(low, "gy", 1), pass_on(high, "gy", -1)
 
 
 def shell_kernel(
@@ -791,21 +783,27 @@
     owner_row = rec_owner.reshape(1, R)
     node_row = rec_node.reshape(1, R)
 
-    rims = static_rims(mass, modulus, live)
+    low, high = edge_call(edge_kernel, "edges", mass, modulus, live)
+    ulow = pass_on(low, "gx", 1)
+    uhigh = pass_on(high, "gx", -1)
     send, rank_row = loads_to_send(pops, weights, block_row, owner_row, node_row)
+    send, ulow, uhigh, pops = lax.optimization_barrier((send, ulow, uhigh, pops))
     recv = exchange(send)
+    low, high = edge_call(side_kernel, "sides", mass, modulus, live, ulow, uhigh)
+    rims = (ulow, uhigh, pass_on(low, "gy", 1), pass_on(high, "gy", -1))
 
     read, xp, xm, yp, ym = collide_and_run(pops)
     xp = pass_on(xp, "gx", 1)
     xm = pass_on(xm, "gx", -1)
+
+    force, rim = force_of(recv)
+    image, ret = shell_of(stiff, force, rim, mass, modulus, live, rims, recv)
+    ret, xp, xm = lax.optimization_barrier((ret, xp, xm))
+    back = exchange(ret)
     yp = yp.at[YP.index(7), 0].set(xp[XP.index(7), 0]).at[YP.index(10), 31].set(xm[XM.index(10), 0])
     ym = ym.at[YM.index(9), 0].set(xp[XP.index(9), 7]).at[YM.index(8), 31].set(xm[XM.index(8), 7])
     yp = pass_on(yp, "gy", 1)
     ym = pass_on(ym, "gy", -1)
-
-    force, rim = force_of(recv)
-    image, ret = shell_of(stiff, force, rim, mass, modulus, live, rims, recv)
-    back = exchange(ret)
 
     back, yp, ym = lax.optimization_barrier((back, yp, ym))
     pq, sound = scalars_of(back)

time: 95.9 us -> 92.7 us (0.967)
  waiting for transfers between devices: 14.9 us -> 9.09 us
  starting transfers between devices: 25.6 us -> 29.1 us
  Pallas kernels: 50 us -> 49 us
    all_to_all x2, waiting for transfers between devices: 14.9 us -> 9.07 us  [exchange(): return lax.all_to_all(x, ALL, 0, 0, tiled=True)]
    all_to_all x2, starting transfers between devices: 14.5 us -> 18.6 us  [exchange(): return lax.all_to_all(x, ALL, 0, 0, tiled=True)]
    pallas_call x1, Pallas kernels: 9.5 us -> 7.79 us  [collide_and_run(): pl.pallas_call(collide_kernel, out_shape=[jax.ShapeDtypeStruct((19, NB, N...]
  transfers between devices with their start and end apart: 10 -> 10, of which waited for: 2 -> 1; matrix products, arithmetic and copies ran while one was open for 3% -> 0% of each run, Pallas kernels for 27% -> 37%
where the time goes in v3:
time: 92.7 us; the launch traced here: 92.3 us
  Pallas kernels  49 us (53%)
  starting transfers between devices  29.1 us (31%)
  waiting for transfers between devices  9.09 us (10%)
  local copies, waits for them, and re-layouts  3.02 us (3%)
  between operations  1.76 us (2%)
    all_to_all x2, starting transfers between devices, exchange(): return lax.all_to_all(x, ALL, 0, 0, tiled=True)  18.6 us
    pallas_call x1, Pallas kernels, loads_to_send(): pl.pallas_call(load_kernel, grid=(MSTEPS + RSTEPS,), in_specs=[pl.BlockSp...  15.2 us
    pallas_call x1, Pallas kernels, outputs_of(): pl.pallas_call(next_kernel, grid=(RSTEPS + OSTEPS,), in_specs=[pl.BlockSp...  13.8 us
    ppermute x8, starting transfers between devices, pass_on(): lax.ppermute(x, axis, [(i, (i + shift) % count) for i in range(count)])  10.5 us
    all_to_all x2, waiting for transfers between devices, exchange(): return lax.all_to_all(x, ALL, 0, 0, tiled=True)  9.07 us
    pallas_call x1, Pallas kernels, collide_and_run(): pl.pallas_call(collide_kernel, out_shape=[jax.ShapeDtypeStruct((19, NB, N...  7.79 us
    pallas_call x1, Pallas kernels, shell_of(): pl.pallas_call(shell_kernel, in_specs=[pl.BlockSpec(memory_space=pltpu.SM...  6.29 us
    pallas_call x1, Pallas kernels, force_of(): pl.pallas_call(force_kernel, out_shape=[jax.ShapeDtypeStruct((3, NU, NV),...  4.32 us
  transfers between devices with their start and end apart: 10, of which 1 were waited for; matrix products, arithmetic and copies ran while one was open for 0% of the time, Pallas kernels for 37%

profile of v3, /device:TPU:1, one launch (start us, length us, event | category | flops | bytes accessed | tf_op | source)
XLA Modules:
  0.0 92.3 jit_solution(4635473298967651871)
XLA Ops:
  0.6 0.8 edges.1
  1.4 2.1 %collective-permute-start.12 = (f32[8,128]{1,0:T(8,128)S(1)}, f32[8,128]{1,0:T(8,128)S(1)}, u32[]{:S(2)}, u32[]{:S(2)}) collective-permute-start(f32[8,128]{1,0:T(8,128)S(1)} %get-tuple-element.121), channel_id=1, source_target_pairs={{0,32},{32,64},{64,96},{96,0},{1,33},{33,65},{65,97},{97,1},{2,34}... | collective-permute-start | bytes 12296 | tf_op jit(solution)/shard_map/ppermute | solution.py:726
  3.6 1.4 %collective-permute-start.13 = (f32[8,128]{1,0:T(8,128)S(1)}, f32[8,128]{1,0:T(8,128)S(1)}, u32[]{:S(2)}, u32[]{:S(2)}) collective-permute-start(f32[8,128]{1,0:T(8,128)S(1)} %get-tuple-element.122), channel_id=1, source_target_pairs={{0,96},{32,0},{64,32},{96,64},{1,97},{33,1},{65,33},{97,65},{2,98}... | collective-permute-start | bytes 12296 | tf_op jit(solution)/shard_map/ppermute | solution.py:726
  5.0 15.2 %loads.1 = (f32[128,384]{1,0:T(8,128)}, s32[1,4096]{1,0:T(1,128)}) custom-call(f32[19,256,256]{2,1,0:T(8,128)} %bitcast.64, f32[4096,256]{1,0:T(8,128)} %w_ref.3, s32[1,4096]{1,0:T(1,128)} %bitcast.83, s32[1,4096]{1,0:T(1,128)} %bitcast.78, s32[1,4096]{1,0:T(1,128)} %bitcast.81, s32[1,4096]{1,0:T(1,128)} %bitcast.79, s32[1,4096]{1,0:T(1,128)} %bitcast.82), custom_call_target="tpu_custom_call" | custom-call | tf_op jit(solution)/shard_map/loads/pallas_call | solution.py:214
  20.2 0.0 collective-permute-done.12.low_ref.ulow_ref
  20.2 0.0 collective-permute-done.13.high_ref.uhigh_ref
  20.2 1.8 %copy.53 = f32[128,1,384]{2,1,0:T(1,128)} copy(f32[128,1,384]{2,0,1:T(8,128)} %bitcast.77) | data formatting | bytes 393216 | tf_op jit(solution)/shard_map/all_to_all | solution.py:777
  22.0 10.0 %all-to-all-start.1 = ((f32[128,1,384]{2,1,0:T(1,128)}), f32[128,1,384]{2,1,0:T(1,128)S(1)}, u32[]{:S(2)}, u32[]{:S(2)}) async-start(f32[128,1,384]{2,1,0:T(1,128)} %copy.53), calls=%async_computation.1 | async-start | bytes 393216 | tf_op jit(solution)/shard_map/all_to_all | solution.py:777
  32.0 0.0 copy-start
  32.0 0.0 copy-start.3
  32.0 0.0 copy-start.4
  32.0 0.0 copy-start.7
  32.0 7.8 %collide.1 = (f32[19,256,256]{2,1,0:T(8,128)}, f32[5,8,256]{2,1,0:T(8,128)}, f32[5,8,256]{2,1,0:T(8,128)}, f32[5,32,256]{2,1,0:T(8,128)}, f32[5,32,256]{2,1,0:T(8,128)}) custom-call(f32[19,256,256]{2,1,0:T(8,128)} %bitcast.65), custom_call_target="tpu_custom_call" | custom-call | tf_op jit(solution)/shard_map/collide/pallas_call | solution.py:289
  39.8 1.4 %collective-permute-start.16 = (f32[5,8,256]{2,1,0:T(8,128)}, f32[5,8,256]{2,1,0:T(8,128)S(1)}, u32[]{:S(2)}, u32[]{:S(2)}) collective-permute-start(f32[5,8,256]{2,1,0:T(8,128)} %get-tuple-element.132), channel_id=1, source_target_pairs={{0,32},{32,64},{64,96},{96,0},{1,33},{33,65},{65,97},{97,1},{2,34}... | collective-permute-start | bytes 122888 | tf_op jit(solution)/shard_map/ppermute | solution.py:726
  41.2 1.3 %collective-permute-start.17 = (f32[5,8,256]{2,1,0:T(8,128)}, f32[5,8,256]{2,1,0:T(8,128)S(1)}, u32[]{:S(2)}, u32[]{:S(2)}) collective-permute-start(f32[5,8,256]{2,1,0:T(8,128)} %get-tuple-element.133), channel_id=1, source_target_pairs={{0,96},{32,0},{64,32},{96,64},{1,97},{33,1},{65,33},{97,65},{2,98}... | collective-permute-start | bytes 122888 | tf_op jit(solution)/shard_map/ppermute | solution.py:726
  42.5 0.0 copy-done
  42.5 0.0 copy-done.3
  42.5 0.0 copy-done.4
  42.5 0.1 sides.1
  42.6 0.0 copy-start.11
  42.6 2.3 %collective-permute-start.14 = (f32[8,128]{1,0:T(8,128)S(1)}, f32[8,128]{1,0:T(8,128)S(1)}, u32[]{:S(2)}, u32[]{:S(2)}) collective-permute-start(f32[8,128]{1,0:T(8,128)S(1)} %get-tuple-element.128), channel_id=1, source_target_pairs={{0,1},{1,2},{2,3},{3,4},{4,5},{5,6},{6,7},{7,8},{8,9},{9,10},{10,1... | collective-permute-start | bytes 12296 | tf_op jit(solution)/shard_map/ppermute | solution.py:726
  44.9 0.0 collective-permute-start.15
  44.9 0.0 all-to-all-done.1
  44.9 4.3 %force.1 = (f32[3,64,128]{2,1,0:T(8,128)S(1)}, f32[3,8,256]{2,1,0:T(8,128)S(1)}) custom-call(f32[128,384]{1,0:T(8,128)S(1)} %bitcast.66), custom_call_target="tpu_custom_call" | custom-call | tf_op jit(solution)/shard_map/force/pallas_call | solution.py:351
  49.2 0.0 collective-permute-done.14.vlow_ref
  49.3 0.0 collective-permute-done.15.vhigh_ref
  49.3 0.0 copy-done.7
  49.3 6.3 %shell.3 = (f32[3,64,128]{2,1,0:T(8,128)S(1)}, f32[128,512]{1,0:T(8,128)S(1)}) custom-call(f32[12,12]{1,0:T(8,128)S(1)} %copy-done.7, f32[3,64,128]{2,1,0:T(8,128)S(1)} %get-tuple-element.124.f_ref, f32[3,8,256]{2,1,0:T(8,128)S(1)} %get-tuple-element.125.rim_ref, f32[64,128]{1,0:T(8,128)S(1)} %copy-done.3, f32[64,128]{1,0:T(8,128)S(1)} %copy-done, ...), custom_call_target="tpu_custom_call" | custom-call | tf_op jit(solution)/shard_map/shell/pallas_call | solution.py:546
  55.6 0.0 collective-permute-done.16.xp_ref
  55.6 0.0 copy-start.8
  55.6 0.0 collective-permute-done.17.xm_ref
  55.6 0.0 copy-start.9
  55.6 1.0 %copy.54 = f32[128,1,512]{2,1,0:T(1,128)} copy(f32[128,1,512]{2,0,1:T(8,128)S(1)} %bitcast.63) | data formatting | bytes 524288 | tf_op jit(solution)/shard_map/all_to_all | solution.py:777
  56.6 8.7 %all-to-all-start.2 = ((f32[128,1,512]{2,1,0:T(1,128)}), f32[128,1,512]{2,1,0:T(1,128)S(1)}, u32[]{:S(2)}, u32[]{:S(2)}) async-start(f32[128,1,512]{2,1,0:T(1,128)} %copy.54), calls=%async_computation.2 | async-start | bytes 524288 | tf_op jit(solution)/shard_map/all_to_all | solution.py:777
  65.3 0.0 copy-done.11
  65.4 1.7 %collective-permute-start.18 = (f32[5,32,256]{2,1,0:T(8,128)S(1)}, f32[5,32,256]{2,1,0:T(8,128)S(1)}, u32[]{:S(2)}, u32[]{:S(2)}) collective-permute-start(f32[5,32,256]{2,1,0:T(8,128)S(1)} %scatter.15), channel_id=1, source_target_pairs={{0,1},{1,2},{2,3},{3,4},{4,5},{5,6},{6,7},{7,8},{8,9},{9,10},{10,1... | collective-permute-start | bytes 491528 | tf_op jit(solution)/shard_map/ppermute | solution.py:726
  67.1 0.0 copy-done.10
  67.1 0.3 collective-permute-start.19
  67.4 9.1 %all-to-all-done.2 = f32[128,1,512]{2,1,0:T(1,128)S(1)} async-done(((f32[128,1,512]{2,1,0:T(1,128)}), f32[128,1,512]{2,1,0:T(1,128)S(1)}, u32[]{:S(2)}, u32[]{:S(2)}) %all-to-all-start.2) | async-done | bytes 262176 | tf_op jit(solution)/shard_map/all_to_all | solution.py:777
  76.5 0.0 collective-permute-done.18.yp_ref
  76.5 0.0 copy-start.5
  76.5 0.0 collective-permute-done.19.ym_ref
  76.5 0.0 copy-start.6
  76.5 0.8 scalars.1
  77.9 0.0 copy-done.8
  78.0 0.0 copy-done.9
  78.0 0.3 conditional.1
  78.3 13.8 %outputs.1 = (f32[19,256,256]{2,1,0:T(8,128)}, f32[3,64,128]{2,1,0:T(8,128)}) custom-call(f32[2]{0:T(128)S(1)} %get-tuple-element.143.pq_ref, f32[128,512]{1,0:T(8,128)S(1)} %get-tuple-element.144.back_ref, f32[4096,256]{1,0:T(8,128)} %w_ref.3, s32[1,4096]{1,0:T(1,128)} %bitcast.84, s32[1,4096]{1,0:T(1,128)} %bitcast.80, ...), custom_call_target="tpu_custom_call" | custom-call | tf_op jit(solution)/shard_map/outputs/pallas_call | solution.py:691
  (10 shorter events, 0.2 us)
Async XLA Ops:
  1.4 18.8 %collective-permute-start.12 = (f32[8,128]{1,0:T(8,128)S(1)}, f32[8,128]{1,0:T(8,128)S(1)}, u32[]{:S(2)}, u32[]{:S(2)}) collective-permute-start(f32[8,128]{1,0:T(8,128)S(1)} %get-tuple-element.121), channel_id=1, source_target_pairs={{0,32},{32,64},{64,96},{96,0},{1,33},{33,65},{65,97},{97,1},{2,34}... | collective-permute-start | bytes 12296 | tf_op jit(solution)/shard_map/ppermute | solution.py:726
  3.6 16.7 %collective-permute-start.13 = (f32[8,128]{1,0:T(8,128)S(1)}, f32[8,128]{1,0:T(8,128)S(1)}, u32[]{:S(2)}, u32[]{:S(2)}) collective-permute-start(f32[8,128]{1,0:T(8,128)S(1)} %get-tuple-element.122), channel_id=1, source_target_pairs={{0,96},{32,0},{64,32},{96,64},{1,97},{33,1},{65,33},{97,65},{2,98}... | collective-permute-start | bytes 12296 | tf_op jit(solution)/shard_map/ppermute | solution.py:726
  22.0 22.9 %all-to-all-start.1 = ((f32[128,1,384]{2,1,0:T(1,128)}), f32[128,1,384]{2,1,0:T(1,128)S(1)}, u32[]{:S(2)}, u32[]{:S(2)}) async-start(f32[128,1,384]{2,1,0:T(1,128)} %copy.53), calls=%async_computation.1 | async-start | bytes 393216 | tf_op jit(solution)/shard_map/all_to_all | solution.py:777
  32.0 10.5 %copy-start = (f32[64,128]{1,0:T(8,128)S(1)}, f32[64,128]{1,0:T(8,128)}, u32[]{:S(2)}) copy-start(f32[64,128]{1,0:T(8,128)} %mod_ref.5) | copy-start | bytes 98308
  32.0 10.5 %copy-start.3 = (f32[64,128]{1,0:T(8,128)S(1)}, f32[64,128]{1,0:T(8,128)}, u32[]{:S(2)}) copy-start(f32[64,128]{1,0:T(8,128)} %mass_ref.5) | copy-start | bytes 98308
  32.0 10.5 %copy-start.4 = (s32[64,128]{1,0:T(8,128)S(1)}, s32[64,128]{1,0:T(8,128)}, u32[]{:S(2)}) copy-start(s32[64,128]{1,0:T(8,128)} %live_ref.5) | copy-start | bytes 98308
  32.0 17.3 %copy-start.7 = (f32[12,12]{1,0:T(8,128)S(1)}, f32[12,12]{1,0:T(8,128)}, u32[]{:S(2)}) copy-start(f32[12,12]{1,0:T(8,128)} %stiff_ref.1) | copy-start | bytes 1732
  39.8 15.8 %collective-permute-start.16 = (f32[5,8,256]{2,1,0:T(8,128)}, f32[5,8,256]{2,1,0:T(8,128)S(1)}, u32[]{:S(2)}, u32[]{:S(2)}) collective-permute-start(f32[5,8,256]{2,1,0:T(8,128)} %get-tuple-element.132), channel_id=1, source_target_pairs={{0,32},{32,64},{64,96},{96,0},{1,33},{33,65},{65,97},{97,1},{2,34}... | collective-permute-start | bytes 122888 | tf_op jit(solution)/shard_map/ppermute | solution.py:726
  41.2 14.4 %collective-permute-start.17 = (f32[5,8,256]{2,1,0:T(8,128)}, f32[5,8,256]{2,1,0:T(8,128)S(1)}, u32[]{:S(2)}, u32[]{:S(2)}) collective-permute-start(f32[5,8,256]{2,1,0:T(8,128)} %get-tuple-element.133), channel_id=1, source_target_pairs={{0,96},{32,0},{64,32},{96,64},{1,97},{33,1},{65,33},{97,65},{2,98}... | collective-permute-start | bytes 122888 | tf_op jit(solution)/shard_map/ppermute | solution.py:726
  42.6 22.6 %copy-start.11 = (f32[5,32,256]{2,1,0:T(8,128)S(1)}, f32[5,32,256]{2,1,0:T(8,128)}, u32[]{:S(2)}) copy-start(f32[5,32,256]{2,1,0:T(8,128)} %get-tuple-element.135) | copy-start | bytes 491524
  42.6 6.6 %collective-permute-start.14 = (f32[8,128]{1,0:T(8,128)S(1)}, f32[8,128]{1,0:T(8,128)S(1)}, u32[]{:S(2)}, u32[]{:S(2)}) collective-permute-start(f32[8,128]{1,0:T(8,128)S(1)} %get-tuple-element.128), channel_id=1, source_target_pairs={{0,1},{1,2},{2,3},{3,4},{4,5},{5,6},{6,7},{7,8},{8,9},{9,10},{10,1... | collective-permute-start | bytes 12296 | tf_op jit(solution)/shard_map/ppermute | solution.py:726
  44.9 22.2 %copy-start.10 = (f32[5,32,256]{2,1,0:T(8,128)S(1)}, f32[5,32,256]{2,1,0:T(8,128)}, u32[]{:S(2)}) copy-start(f32[5,32,256]{2,1,0:T(8,128)} %get-tuple-element.138) | copy-start | bytes 491524
  44.9 4.4 %collective-permute-start.15 = (f32[8,128]{1,0:T(8,128)S(1)}, f32[8,128]{1,0:T(8,128)S(1)}, u32[]{:S(2)}, u32[]{:S(2)}) collective-permute-start(f32[8,128]{1,0:T(8,128)S(1)} %get-tuple-element.129), channel_id=1, source_target_pairs={{0,31},{1,0},{2,1},{3,2},{4,3},{5,4},{6,5},{7,6},{8,7},{9,8},{10,9... | collective-permute-start | bytes 12296 | tf_op jit(solution)/shard_map/ppermute | solution.py:726
  55.6 22.4 %copy-start.8 = (f32[5,8,256]{2,1,0:T(8,128)}, f32[5,8,256]{2,1,0:T(8,128)S(1)}, u32[]{:S(2)}) copy-start(f32[5,8,256]{2,1,0:T(8,128)S(1)} %collective-permute-done.16.xp_ref) | copy-start | bytes 122884
  55.6 22.4 %copy-start.9 = (f32[5,8,256]{2,1,0:T(8,128)}, f32[5,8,256]{2,1,0:T(8,128)S(1)}, u32[]{:S(2)}) copy-start(f32[5,8,256]{2,1,0:T(8,128)S(1)} %collective-permute-done.17.xm_ref) | copy-start | bytes 122884
  56.6 19.9 %all-to-all-start.2 = ((f32[128,1,512]{2,1,0:T(1,128)}), f32[128,1,512]{2,1,0:T(1,128)S(1)}, u32[]{:S(2)}, u32[]{:S(2)}) async-start(f32[128,1,512]{2,1,0:T(1,128)} %copy.54), calls=%async_computation.2 | async-start | bytes 524288 | tf_op jit(solution)/shard_map/all_to_all | solution.py:777
  65.4 11.1 %collective-permute-start.18 = (f32[5,32,256]{2,1,0:T(8,128)S(1)}, f32[5,32,256]{2,1,0:T(8,128)S(1)}, u32[]{:S(2)}, u32[]{:S(2)}) collective-permute-start(f32[5,32,256]{2,1,0:T(8,128)S(1)} %scatter.15), channel_id=1, source_target_pairs={{0,1},{1,2},{2,3},{3,4},{4,5},{5,6},{6,7},{7,8},{8,9},{9,10},{10,1... | collective-permute-start | bytes 491528 | tf_op jit(solution)/shard_map/ppermute | solution.py:726
  67.1 9.4 %collective-permute-start.19 = (f32[5,32,256]{2,1,0:T(8,128)S(1)}, f32[5,32,256]{2,1,0:T(8,128)S(1)}, u32[]{:S(2)}, u32[]{:S(2)}) collective-permute-start(f32[5,32,256]{2,1,0:T(8,128)S(1)} %scatter.19), channel_id=1, source_target_pairs={{0,31},{1,0},{2,1},{3,2},{4,3},{5,4},{6,5},{7,6},{8,7},{9,8},{10,9... | collective-permute-start | bytes 491528 | tf_op jit(solution)/shard_map/ppermute | solution.py:726
  76.5 1.5 %copy-start.5 = (f32[5,32,256]{2,1,0:T(8,128)}, f32[5,32,256]{2,1,0:T(8,128)S(1)}, u32[]{:S(2)}) copy-start(f32[5,32,256]{2,1,0:T(8,128)S(1)} %collective-permute-done.18.yp_ref) | copy-start | bytes 491524
  76.5 1.4 %copy-start.6 = (f32[5,32,256]{2,1,0:T(8,128)}, f32[5,32,256]{2,1,0:T(8,128)S(1)}, u32[]{:S(2)}) copy-start(f32[5,32,256]{2,1,0:T(8,128)S(1)} %collective-permute-done.19.ym_ref) | copy-start | bytes 491524

commit v4 on v3

--- a/solution.py
+++ b/solution.py
@@ -78,13 +78,25 @@
     return lax.dot_general(a, b, (((1,), (0,)), ((), ())), preferred_element_type=F32)
 
 
-MSTEPS = 2
-MROWS = NB // MSTEPS
+CHUNKS = 4
+CROWS = NB // CHUNKS
 RSTEPS = R // RB
 
 
-def block_hot(row):
-    return jnp.where(iota((NB, RB), 0) == row, 1.0, 0.0).astype(BF16)
+def match(count, row):
+    lanes = row.shape[1]
+    column = iota((count, 128), 0).astype(F32).astype(BF16)
+    wanted = jnp.broadcast_to(row.astype(F32).astype(BF16), (count, lanes))
+    return jnp.concatenate([column] * (lanes // 128), axis=1) == wanted
+
+
+def hot(count, row):
+    shape = (count, row.shape[1])
+    return jnp.where(match(count, row), jnp.ones(shape, BF16), jnp.zeros(shape, BF16))
+
+
+def pick(mask, row):
+    return jnp.where(mask, jnp.broadcast_to(row, mask.shape), jnp.zeros(mask.shape, BF16))
 
 
 def rim_rows(own, node):
@@ -108,114 +120,115 @@
 
 
 def load_kernel(
-    pop_ref, w_ref, blk_ref, own_all_ref, node_all_ref, own_ref, node_ref, send_ref, rank_ref,
-    m_ref, mt_ref, tri_ref, carry_ref, dest_ref, code_ref, place_ref, over_ref,
+    pop_hbm, w_ref, blk_ref, own_all_ref, node_all_ref, own_ref, node_ref, send_ref, rank_ref, wt_ref,
+    pop_ref, sems, m_ref, mt_ref, tri_ref, carry_ref, dest_ref, code_ref, place_ref, over_ref, main_ref, rims_ref,
 ):
     step = pl.program_id(0)
 
+    def fetch(part):
+        rows = pl.ds(part * CROWS, CROWS)
+        return pltpu.make_async_copy(pop_hbm.at[:, rows, :], pop_ref.at[:, rows, :], sems.at[part])
+
     @pl.when(step == 0)
     def _():
+        for part in range(CHUNKS):
+            fetch(part).start()
         before = (iota((256, 256), 0) < iota((256, 256), 1)).astype(F32)
         tri_ref[:, 0:256] = before.astype(BF16)
         tri_ref[:, 256:512] = jnp.ones((256, 256), BF16)
         carry_ref[...] = jnp.zeros_like(carry_ref)
-        send_ref[...] = jnp.zeros_like(send_ref)
+        main_ref[...] = jnp.zeros_like(main_ref)
+        rims_ref[...] = jnp.zeros_like(rims_ref)
         over_ref[...] = jnp.zeros_like(over_ref)
         dests, codes = rim_rows(own_all_ref[...], node_all_ref[...])
         for i in range(3):
             dest_ref[i : i + 1, :] = dests[i]
             code_ref[i : i + 1, :] = codes[i].astype(F32)
-
-    for part in range(MSTEPS):
-
-        @pl.when(step == part)
-        def _():
-            def rows_of(i, _):
-                rows = pl.ds(pl.multiple_of(i * 8, 8), 8)
-                pops = [pop_ref[q, rows, :] for q in range(1, 19)]
-                for axis in range(3):
-                    total = None
-                    for q in range(1, 19):
-                        if DIRS[q][axis] != 0:
-                            term = pops[q - 1] if DIRS[q][axis] == 1 else -pops[q - 1]
-                            total = term if total is None else total + term
-                    m_ref[axis, rows, :] = total
-                return 0
-
-            lax.fori_loop(0, MROWS // 8, rows_of, 0, unroll=2)
+        for k in range(R // 256):
+            cols = slice(k * 256, (k + 1) * 256)
+            device = iota((ND, 256), 0)
+            hots = [device == own_all_ref[:, cols]] + [device == dest_ref[i : i + 1, cols] for i in range(3)]
+            main = jnp.where(hots[0], 1.0, 0.0).astype(BF16)
+            rims = jnp.where(hots[1] | hots[2] | hots[3], 1.0, 0.0).astype(BF16)
+            counts = dot(jnp.concatenate([main, rims], axis=0), tri_ref[...])
+            upto = counts[:, 0:256] + carry_ref[...]
+            carry_ref[...] += counts[:, 256:512]
+            rank = jnp.sum(jnp.where(hots[0], upto[0:ND], 0.0), axis=0, keepdims=True)
+            rank_ref[:, cols] = rank.astype(jnp.int32)
+            for i in range(3):
+                place = jnp.sum(jnp.where(hots[i + 1], upto[ND : 2 * ND], 0.0), axis=0, keepdims=True)
+                over_ref[...] = jnp.maximum(over_ref[...], place)
+                place_ref[i : i + 1, cols] = jnp.where(place < RIM - 1, place, 2.0 * RIM).astype(jnp.int32)
+
+        def rows_of(i, _):
+            rows = pl.ds(pl.multiple_of(i * 8, 8), 8)
+            pops = [pop_ref[q, rows, :] for q in range(1, 19)]
             for axis in range(3):
-                turned = m_ref[axis].T
-                high = turned.astype(BF16)
-                at = slice(axis * NK, (axis + 1) * NK)
-                mt_ref[at, part * MROWS : (part + 1) * MROWS] = high
-                low = (turned - high.astype(F32)).astype(BF16)
-                mt_ref[at, NB + part * MROWS : NB + (part + 1) * MROWS] = low
-            for k in range(R // 256 // MSTEPS):
-                start = (part * (R // 256 // MSTEPS) + k) * 256
-                cols = slice(start, start + 256)
-                device = iota((ND, 256), 0)
-                hots = [device == own_all_ref[:, cols]] + [device == dest_ref[i : i + 1, cols] for i in range(3)]
-                main = jnp.where(hots[0], 1.0, 0.0).astype(BF16)
-                rims = jnp.where(hots[1] | hots[2] | hots[3], 1.0, 0.0).astype(BF16)
-                counts = dot(jnp.concatenate([main, rims], axis=0), tri_ref[...])
-                upto = counts[:, 0:256] + carry_ref[...]
-                carry_ref[...] += counts[:, 256:512]
-                rank_ref[:, cols] = jnp.sum(jnp.where(hots[0], upto[0:ND], 0.0), axis=0, keepdims=True).astype(
-                    jnp.int32
-                )
-                for i in range(3):
-                    place = jnp.sum(jnp.where(hots[i + 1], upto[ND : 2 * ND], 0.0), axis=0, keepdims=True)
-                    over_ref[...] = jnp.maximum(over_ref[...], place)
-                    place_ref[i : i + 1, cols] = jnp.where(place < RIM - 1, place, 2.0 * RIM).astype(jnp.int32)
-
-    @pl.when(step >= MSTEPS)
+                total = None
+                for q in range(1, 19):
+                    if DIRS[q][axis] != 0:
+                        term = pops[q - 1] if DIRS[q][axis] == 1 else -pops[q - 1]
+                        total = term if total is None else total + term
+                m_ref[axis, rows, :] = total
+            return 0
+
+        for part in range(CHUNKS):
+            fetch(part).wait()
+            lax.fori_loop(part * CROWS // 8, (part + 1) * CROWS // 8, rows_of, 0, unroll=2)
+        for axis in range(3):
+            turned = m_ref[axis].T
+            high = turned.astype(BF16)
+            at = slice(axis * NK, (axis + 1) * NK)
+            mt_ref[at, 0:NB] = high
+            mt_ref[at, NB : 2 * NB] = (turned - high.astype(F32)).astype(BF16)
+
+    @pl.when(step >= 1)
     def _():
-        here = pl.ds(pl.multiple_of((step - MSTEPS) * RB, RB), RB)
+        here = pl.ds(pl.multiple_of((step - 1) * RB, RB), RB)
         w_t = w_ref[...].T
-        hot = block_hot(blk_ref[...])
-        picked = dot(mt_ref[...], jnp.concatenate([hot, hot], axis=0))
+        in_block = hot(NB, blk_ref[...])
+        picked = dot(mt_ref[...], jnp.concatenate([in_block, in_block], axis=0))
         values = [
             jnp.sum(picked[axis * NK : (axis + 1) * NK, :] * w_t, axis=0, keepdims=True) for axis in range(3)
         ]
-        parts = [halves(value) for value in values]
-        node = halves(node_ref[...].astype(F32))
-
-        def placed(in_slot, code):
-            both = [
-                jnp.concatenate(
-                    [jnp.where(in_slot, part[side], 0.0).astype(BF16) for part in parts + [code]], axis=0
-                )
-                for side in range(2)
-            ]
-            return jnp.concatenate(both, axis=1)
-
-        named = jnp.where(iota((ND, RB), 0) == own_ref[...], 1.0, 0.0).astype(BF16)
-        packed = placed(iota((CAP, RB), 0) == rank_ref[:, here], node)
-        send_ref[:, 0:MAIN] += dot_t(jnp.concatenate([named, named], axis=1), packed)
-        for i in range(3):
-            named = jnp.where(iota((ND, RB), 0) == dest_ref[i : i + 1, here], 1.0, 0.0).astype(BF16)
-            packed = placed(iota((RIM, RB), 0) == place_ref[i : i + 1, here], halves(code_ref[i : i + 1, here]))
-            send_ref[:, MAIN : MAIN + 4 * RIM] += dot_t(jnp.concatenate([named, named], axis=1), packed)
-
-    @pl.when(step == MSTEPS + RSTEPS - 1)
+
+        def sides(value):
+            return [side.astype(BF16) for side in halves(value)]
+
+        parts = [sides(value) for value in values]
+
+        def placed(count, slot, code):
+            mask = match(count, slot)
+            both = [pick(mask, part[side]) for side in range(2) for part in parts + [sides(code)]]
+            return jnp.concatenate(both, axis=0)
+
+        packed = placed(CAP, rank_ref[:, here], node_ref[...].astype(F32))
+        main_ref[...] += dot_t(packed, hot(ND, own_ref[...]))
+        packed = [placed(RIM, place_ref[i : i + 1, here], code_ref[i : i + 1, here]) for i in range(3)]
+        named = [hot(ND, dest_ref[i : i + 1, here]) for i in range(3)]
+        rims_ref[...] += dot_t(jnp.concatenate(packed, axis=1), jnp.concatenate(named, axis=1))
+        wt_ref[...] = w_t
+
+    @pl.when(step == RSTEPS)
     def _():
         most = jnp.max(over_ref[...], axis=1, keepdims=True)
         flag = jnp.where(most >= RIM - 1, 1.0, 0.0)
-        tail = send_ref[:, MAIN : MAIN + 4 * RIM]
-        send_ref[:, MAIN : MAIN + 4 * RIM] = jnp.where(iota((ND, 4 * RIM), 1) == 4 * RIM - 1, flag, tail)
+        send_ref[:, 0, 0:MAIN] = (main_ref[0:MAIN, :] + main_ref[MAIN : 2 * MAIN, :]).T
+        tail = (rims_ref[0 : 4 * RIM, :] + rims_ref[4 * RIM : 8 * RIM, :]).T
+        send_ref[:, 0, MAIN : MAIN + 4 * RIM] = jnp.where(iota((ND, 4 * RIM), 1) == 4 * RIM - 1, flag, tail)
 
 
 def loads_to_send(pops, weights, block_row, owner_row, node_row):
     def record(i):
-        return jnp.maximum(i - MSTEPS, 0)
+        return jnp.maximum(i - 1, 0)
 
     row_spec = pl.BlockSpec((1, RB), lambda i: (0, record(i)))
     all_rows = pl.BlockSpec((1, R), lambda i: (0, 0))
     return pl.pallas_call(
         load_kernel,
-        grid=(MSTEPS + RSTEPS,),
+        grid=(1 + RSTEPS,),
         in_specs=[
-            pl.BlockSpec((19, MROWS, NK), lambda i: (0, jnp.minimum(i, MSTEPS - 1), 0)),
+            pl.BlockSpec(memory_space=pl.ANY),
             pl.BlockSpec((RB, NK), lambda i: (record(i), 0)),
             row_spec,
             all_rows,
@@ -223,13 +236,20 @@
             row_spec,
             row_spec,
         ],
-        out_specs=[pl.BlockSpec((ND, MAIN + 4 * RIM), lambda i: (0, 0)), all_rows],
+        out_specs=[
+            pl.BlockSpec((ND, 1, MAIN + 4 * RIM), lambda i: (0, 0, 0)),
+            all_rows,
+            pl.BlockSpec((NK, RB), lambda i: (0, record(i))),
+        ],
         out_shape=[
-            jax.ShapeDtypeStruct((ND, MAIN + 4 * RIM), F32),
+            jax.ShapeDtypeStruct((ND, 1, MAIN + 4 * RIM), F32),
             jax.ShapeDtypeStruct((1, R), jnp.int32),
+            jax.ShapeDtypeStruct((NK, R), F32),
         ],
         scratch_shapes=[
-            pltpu.VMEM((3, MROWS, NK), F32),
+            pltpu.VMEM((19, NB, NK), F32),
+            pltpu.SemaphoreType.DMA((CHUNKS,)),
+            pltpu.VMEM((3, NB, NK), F32),
             pltpu.VMEM((3 * NK, 2 * NB), BF16),
             pltpu.VMEM((256, 512), BF16),
             pltpu.VMEM((2 * ND, 256), F32),
@@ -237,6 +257,8 @@
             pltpu.VMEM((8, R), F32),
             pltpu.VMEM((8, R), jnp.int32),
             pltpu.VMEM((1, 256), F32),
+            pltpu.VMEM((2 * MAIN, ND), F32),
+            pltpu.VMEM((8 * RIM, ND), F32),
         ],
         compiler_params=pltpu.CompilerParams(vmem_limit_bytes=VMEM_LIMIT),
         name="loads",
@@ -306,7 +328,7 @@
 
 
 def force_kernel(recv_ref, f_ref, rim_ref, u_ref, v_ref, hl_ref, ru_ref, rv_ref, rhl_ref):
-    recv_t = recv_ref[...].T
+    recv_t = recv_ref[:, 0, :].T
     u_ref[...], v_ref[...] = node_rows(recv_t)
     high, low = halves(recv_t[0 : 3 * CAP, :])
     hl_ref[0 : 3 * CAP, :] = high
@@ -505,7 +527,7 @@
     for i in range(4):
         whole = jnp.sum(jnp.sum(sums[i], axis=0, keepdims=True), axis=1, keepdims=True)
         moments = jnp.where(lane == i, whole, moments)
-    over = jnp.max(recv_ref[:, MAIN + 4 * RIM - 1 : MAIN + 4 * RIM], axis=0, keepdims=True)
+    over = jnp.max(recv_ref[:, 0, MAIN + 3 * RIM :], axis=0, keepdims=True)[:, RIM - 1 :]
     moments = jnp.where(lane == 4, over, moments)
 
     for c in range(3):
@@ -513,7 +535,7 @@
             high = field.astype(BF16)
             fy_ref[part * NU : (part + 1) * NU, 0:NV] = high
             fy_ref[part * NU : (part + 1) * NU, NV : 2 * NV] = (field - high.astype(F32)).astype(BF16)
-    u_ref[...], v_ref[...] = node_rows(recv_ref[:, 0:MAIN].T)
+    u_ref[...], v_ref[...] = node_rows(recv_ref[:, 0, 0:MAIN].T)
     u_of = iota((NU, ND), 0)
     v_of = iota((NV, ND), 0)
 
@@ -537,8 +559,8 @@
         return 0
 
     lax.fori_loop(0, CAP // 8, chunk, 0)
-    ret_ref[:, 0 : 6 * CAP] = rt_ref[...].T
-    ret_ref[:, 6 * CAP : 8 * CAP] = jnp.broadcast_to(moments, (ND, 128))
+    ret_ref[:, 0, 0 : 6 * CAP] = rt_ref[...].T
+    ret_ref[:, 0, 6 * CAP : 8 * CAP] = jnp.broadcast_to(moments, (ND, 128))
 
 
 def shell_of(stiff, force, rim, mass, modulus, live, rims, recv):
@@ -549,7 +571,7 @@
         out_specs=[vmem, vmem],
         out_shape=[
             jax.ShapeDtypeStruct((3, NU, NV), F32),
-            jax.ShapeDtypeStruct((ND, 8 * CAP), F32),
+            jax.ShapeDtypeStruct((ND, 1, 8 * CAP), F32),
         ],
         scratch_shapes=[
             pltpu.VMEM((6, EU, EV), F32),
@@ -567,7 +589,7 @@
 
 
 def scalar_kernel(part_ref, pq_ref, sound_ref):
-    row = jnp.sum(part_ref[...], axis=0, keepdims=True)
+    row = jnp.sum(part_ref[:, 0, :], axis=0, keepdims=True)
     lane = iota((1, 128), 1)
     m0, m1, m2, m3, over = [
         jnp.sum(jnp.where(lane == i, row, 0.0), axis=1, keepdims=True) for i in range(5)
@@ -596,29 +618,37 @@
     return pl.pallas_call(
         scalar_kernel,
         grid=(1,),
-        in_specs=[pl.BlockSpec((ND, 128), lambda i: (0, 3))],
+        in_specs=[pl.BlockSpec((ND, 1, 128), lambda i: (0, 0, 3))],
         out_specs=[smem, smem],
         out_shape=[jax.ShapeDtypeStruct((2,), F32), jax.ShapeDtypeStruct((1,), jnp.int32)],
         name="scalars",
     )(back)
 
 
-XS = 4
+OB = 2048
+OREC = R // OB
+XS = 8
 OSTEPS = 32 // XS
 
 
 def next_kernel(
     pq_ref, back_ref, w_ref, blk_ref, own_ref, rank_ref, f_ref, y_ref, read_ref, xp_ref, xm_ref, yp_ref, ym_ref,
     next_ref, disp_ref,
-    x_ref, turned_ref, force_ref,
+    x_ref, turned_ref, force_ref, buf_ref, sems,
 ):
     step = pl.program_id(0)
 
+    def fetch(slab):
+        rows = pl.ds(pl.multiple_of(slab * XS * 8, XS * 8), XS * 8)
+        return pltpu.make_async_copy(read_ref.at[:, rows, :], buf_ref.at[:, rows, :], sems.at[slab])
+
     @pl.when(step == 0)
     def _():
+        for slab in range(OSTEPS):
+            fetch(slab).start()
         p = pq_ref[0]
         q = pq_ref[1]
-        back = p * back_ref[:, 0 : 3 * CAP] + q * back_ref[:, 3 * CAP : 6 * CAP]
+        back = p * back_ref[:, 0, 0 : 3 * CAP] + q * back_ref[:, 0, 3 * CAP : 6 * CAP]
         turned = back.T * COUPLING
         high = turned.astype(BF16)
         x_ref[:, 0:ND] = high
@@ -626,12 +656,12 @@
         disp_ref[...] = p * f_ref[...] + q * y_ref[...]
         turned_ref[...] = jnp.zeros_like(turned_ref)
 
-    @pl.when(step < RSTEPS)
+    @pl.when(step < OREC)
     def _():
-        named = jnp.where(iota((ND, RB), 0) == own_ref[...], 1.0, 0.0).astype(BF16)
+        named = hot(ND, own_ref[...])
         picked = dot(x_ref[...], jnp.concatenate([named, named], axis=0))
-        in_slot = iota((CAP, RB), 0) == rank_ref[...]
-        w_t = w_ref[...].T
+        in_slot = iota((CAP, OB), 0) == rank_ref[...]
+        w_t = w_ref[...]
         highs, lows = [], []
         for c in range(3):
             moved = jnp.sum(
@@ -641,27 +671,29 @@
             high = part.astype(BF16)
             highs.append(high)
             lows.append((part - high.astype(F32)).astype(BF16))
-        hot = block_hot(blk_ref[...])
+        in_block = hot(NB, blk_ref[...])
         parts = jnp.concatenate([jnp.concatenate(highs, axis=0), jnp.concatenate(lows, axis=0)], axis=1)
-        turned_ref[...] += dot_t(parts, jnp.concatenate([hot, hot], axis=1))
-
-    @pl.when(step == RSTEPS)
+        turned_ref[...] += dot_t(parts, jnp.concatenate([in_block, in_block], axis=1))
+
+    @pl.when(step == OREC)
     def _():
         for c in range(3):
             force_ref[c * NB : (c + 1) * NB, :] = turned_ref[c * NK : (c + 1) * NK, :].T
 
-    @pl.when(step >= RSTEPS)
+    @pl.when(step >= OREC)
     def _():
-        slab = step - RSTEPS
+        slab = step - OREC
+        fetch(slab).wait()
         sub = iota((8, NK), 0)
         for xx in range(XS):
             x = slab * XS + xx
+            rows = pl.ds(pl.multiple_of(x * 8, 8), 8)
             forcing = [
                 force_ref[pl.ds(pl.multiple_of(c * NB + x * 8, 8), 8), :] for c in range(3)
             ]
             for q in range(19):
                 cx, cy, _ = DIRS[q]
-                value = read_ref[q, xx * 8 : (xx + 1) * 8, :]
+                value = buf_ref[q, rows, :]
                 if cx == 1 and xx == 0:
                     value = jnp.where(x == 0, xp_ref[XP.index(q)], value)
                 if cx == -1 and xx == XS - 1:
@@ -678,29 +710,29 @@
 
 def outputs_of(pq, back, weights, block_row, owner_row, rank_row, force, image, read, xp, xm, yp, ym):
     def record(i):
-        return jnp.minimum(i, RSTEPS - 1)
+        return jnp.minimum(i, OREC - 1)
 
     def slab(i):
-        return jnp.maximum(i - RSTEPS, 0)
-
-    row_spec = pl.BlockSpec((1, RB), lambda i: (0, record(i)))
+        return jnp.maximum(i - OREC, 0)
+
+    row_spec = pl.BlockSpec((1, OB), lambda i: (0, record(i)))
     patch = pl.BlockSpec((3, NU, NV), lambda i: (0, 0, 0))
     lines = pl.BlockSpec((19, XS * 8, NK), lambda i: (0, slab(i), 0))
     x_face = pl.BlockSpec((5, 8, NK), lambda i: (0, 0, 0))
     y_face = pl.BlockSpec((5, 32, NK), lambda i: (0, 0, 0))
     return pl.pallas_call(
         next_kernel,
-        grid=(RSTEPS + OSTEPS,),
+        grid=(OREC + OSTEPS,),
         in_specs=[
             pl.BlockSpec(memory_space=pltpu.SMEM),
-            pl.BlockSpec((ND, 8 * CAP), lambda i: (0, 0)),
-            pl.BlockSpec((RB, NK), lambda i: (record(i), 0)),
+            pl.BlockSpec((ND, 1, 8 * CAP), lambda i: (0, 0, 0)),
+            pl.BlockSpec((NK, OB), lambda i: (0, record(i))),
             row_spec,
             row_spec,
             row_spec,
             patch,
             patch,
-            lines,
+            pl.BlockSpec(memory_space=pl.ANY),
             x_face,
             x_face,
             y_face,
@@ -715,6 +747,8 @@
             pltpu.VMEM((3 * CAP, 2 * ND), BF16),
             pltpu.VMEM((3 * NK, NB), F32),
             pltpu.VMEM((3 * NB, NK), F32),
+            pltpu.VMEM((19, NB, NK), F32),
+            pltpu.SemaphoreType.DMA((OSTEPS,)),
         ],
         compiler_params=pltpu.CompilerParams(vmem_limit_bytes=VMEM_LIMIT),
         name="outputs",
@@ -786,7 +820,7 @@
     low, high = edge_call(edge_kernel, "edges", mass, modulus, live)
     ulow = pass_on(low, "gx", 1)
     uhigh = pass_on(high, "gx", -1)
-    send, rank_row = loads_to_send(pops, weights, block_row, owner_row, node_row)
+    send, rank_row, turned = loads_to_send(pops, weights, block_row, owner_row, node_row)
     send, ulow, uhigh, pops = lax.optimization_barrier((send, ulow, uhigh, pops))
     recv = exchange(send)
     low, high = edge_call(side_kernel, "sides", mass, modulus, live, ulow, uhigh)
@@ -830,7 +864,7 @@
     )
 
     populations_next, displacement = outputs_of(
-        pq, back, weights, block_row, owner_row, rank_row, force, image, read, xp, xm, yp, ym
+        pq, back, turned, block_row, owner_row, rank_row, force, image, read, xp, xm, yp, ym
     )
     return populations_next.reshape(19, 32, 8, NK), displacement
 

time: 92.7 us -> 84 us (0.906)
  Pallas kernels: 49 us -> 43.4 us
  local copies, waits for them, and re-layouts: 3.02 us -> 0.22 us
    pallas_call x3, Pallas kernels: 29.8 us -> 23.3 us  [the longest x1 12.9 us: loads_to_send(): pl.pallas_call(load_kernel, grid=(1 + RSTEPS,), in_specs=[pl.BlockSpec(me...]
    all_to_all x2, waiting for transfers between devices: 9.07 us -> 4.04 us  [exchange(): return lax.all_to_all(x, ALL, 0, 0, tiled=True)]
    ppermute x8, waiting for transfers between devices: 0.02 us -> 5.04 us  [pass_on(): lax.ppermute(x, axis, [(i, (i + shift) % count) for i in range(count)])]
    all_to_all x2 -> x0, local copies, waits for them, and re-layouts: 2.78 us -> none  [exchange(): return lax.all_to_all(x, ALL, 0, 0, tiled=True)]
  transfers between devices with their start and end apart: 10 -> 10, of which waited for: 1 -> 3; matrix products, arithmetic and copies ran while one was open for 0% -> 0% of each run, Pallas kernels for 37% -> 38%
where the time goes in v4:
time: 84 us; the launch traced here: 83.7 us
  Pallas kernels  43.4 us (52%)
  starting transfers between devices  29.1 us (35%)
  waiting for transfers between devices  9.08 us (11%)
  between operations  1.68 us (2%)
    all_to_all x2, starting transfers between devices, exchange(): return lax.all_to_all(x, ALL, 0, 0, tiled=True)  18.6 us
    pallas_call x1, Pallas kernels, loads_to_send(): pl.pallas_call(load_kernel, grid=(1 + RSTEPS,), in_specs=[pl.BlockSpec(me...  12.9 us
    ppermute x8, starting transfers between devices, pass_on(): lax.ppermute(x, axis, [(i, (i + shift) % count) for i in range(count)])  10.5 us
    pallas_call x1, Pallas kernels, outputs_of(): pl.pallas_call(next_kernel, grid=(OREC + OSTEPS,), in_specs=[pl.BlockSpec...  9.63 us
    pallas_call x1, Pallas kernels, collide_and_run(): pl.pallas_call(collide_kernel, out_shape=[jax.ShapeDtypeStruct((19, NB, N...  7.78 us
    pallas_call x1, Pallas kernels, shell_of(): pl.pallas_call(shell_kernel, in_specs=[pl.BlockSpec(memory_space=pltpu.SM...  7 us
    ppermute x8, waiting for transfers between devices, pass_on(): lax.ppermute(x, axis, [(i, (i + shift) % count) for i in range(count)])  5.04 us
    pallas_call x1, Pallas kernels, force_of(): pl.pallas_call(force_kernel, out_shape=[jax.ShapeDtypeStruct((3, NU, NV),...  4.35 us
  transfers between devices with their start and end apart: 10, of which 3 were waited for; matrix products, arithmetic and copies ran while one was open for 0% of the time, Pallas kernels for 38%

profile of v4, /device:TPU:1, one launch (start us, length us, event | category | flops | bytes accessed | tf_op | source)
XLA Modules:
  0.0 83.7 jit_solution(1939378261985922123)
XLA Ops:
  0.6 0.8 edges.1
  1.4 2.1 %collective-permute-start.12 = (f32[8,128]{1,0:T(8,128)S(1)}, f32[8,128]{1,0:T(8,128)S(1)}, u32[]{:S(2)}, u32[]{:S(2)}) collective-permute-start(f32[8,128]{1,0:T(8,128)S(1)} %get-tuple-element.122), channel_id=1, source_target_pairs={{0,32},{32,64},{64,96},{96,0},{1,33},{33,65},{65,97},{97,1},{2,34}... | collective-permute-start | bytes 12296 | tf_op jit(solution)/shard_map/ppermute | solution.py:760
  3.6 1.4 %collective-permute-start.13 = (f32[8,128]{1,0:T(8,128)S(1)}, f32[8,128]{1,0:T(8,128)S(1)}, u32[]{:S(2)}, u32[]{:S(2)}) collective-permute-start(f32[8,128]{1,0:T(8,128)S(1)} %get-tuple-element.123), channel_id=1, source_target_pairs={{0,96},{32,0},{64,32},{96,64},{1,97},{33,1},{65,33},{97,65},{2,98}... | collective-permute-start | bytes 12296 | tf_op jit(solution)/shard_map/ppermute | solution.py:760
  5.0 12.9 %loads.1 = (f32[128,1,384]{2,1,0:T(1,128)}, s32[1,4096]{1,0:T(1,128)}, f32[256,4096]{1,0:T(8,128)}) custom-call(f32[19,256,256]{2,1,0:T(8,128)} %bitcast.50, f32[4096,256]{1,0:T(8,128)} %w_ref.1, s32[1,4096]{1,0:T(1,128)} %bitcast.62, s32[1,4096]{1,0:T(1,128)} %bitcast.57, s32[1,4096]{1,0:T(1,128)} %bitcast.60, s32[1,4096]{1,0:T(1,128)} %bitcast.58, ...), custom_call_target="tpu_custom_call" | custom-call | tf_op jit(solution)/shard_map/loads/pallas_call | solution.py:227
  17.9 0.0 collective-permute-done.12.low_ref.ulow_ref
  17.9 0.0 collective-permute-done.13.high_ref.uhigh_ref
  17.9 10.0 %all-to-all-start.1 = ((f32[128,1,384]{2,1,0:T(1,128)}), f32[128,1,384]{2,1,0:T(1,128)S(1)}, u32[]{:S(2)}, u32[]{:S(2)}) async-start(f32[128,1,384]{2,1,0:T(1,128)} %get-tuple-element.124), calls=%async_computation.1 | async-start | bytes 393216 | tf_op jit(solution)/shard_map/all_to_all | solution.py:811
  27.9 0.0 copy-start
  27.9 0.0 copy-start.3
  27.9 0.0 copy-start.4
  27.9 0.0 copy-start.7
  27.9 7.8 %collide.1 = (f32[19,256,256]{2,1,0:T(8,128)}, f32[5,8,256]{2,1,0:T(8,128)}, f32[5,8,256]{2,1,0:T(8,128)}, f32[5,32,256]{2,1,0:T(8,128)}, f32[5,32,256]{2,1,0:T(8,128)}) custom-call(f32[19,256,256]{2,1,0:T(8,128)} %bitcast.51), custom_call_target="tpu_custom_call" | custom-call | tf_op jit(solution)/shard_map/collide/pallas_call | solution.py:311
  35.7 0.0 copy-start.11
  35.7 0.0 copy-start.10
  35.7 1.4 %collective-permute-start.16 = (f32[5,8,256]{2,1,0:T(8,128)}, f32[5,8,256]{2,1,0:T(8,128)S(1)}, u32[]{:S(2)}, u32[]{:S(2)}) collective-permute-start(f32[5,8,256]{2,1,0:T(8,128)} %get-tuple-element.133), channel_id=1, source_target_pairs={{0,32},{32,64},{64,96},{96,0},{1,33},{33,65},{65,97},{97,1},{2,34}... | collective-permute-start | bytes 122888 | tf_op jit(solution)/shard_map/ppermute | solution.py:760
  37.1 1.3 %collective-permute-start.17 = (f32[5,8,256]{2,1,0:T(8,128)}, f32[5,8,256]{2,1,0:T(8,128)S(1)}, u32[]{:S(2)}, u32[]{:S(2)}) collective-permute-start(f32[5,8,256]{2,1,0:T(8,128)} %get-tuple-element.134), channel_id=1, source_target_pairs={{0,96},{32,0},{64,32},{96,64},{1,97},{33,1},{65,33},{97,65},{2,98}... | collective-permute-start | bytes 122888 | tf_op jit(solution)/shard_map/ppermute | solution.py:760
  38.5 0.0 copy-done
  38.5 0.0 copy-done.3
  38.5 0.0 copy-done.4
  38.5 0.1 sides.1
  38.6 2.2 %collective-permute-start.14 = (f32[8,128]{1,0:T(8,128)S(1)}, f32[8,128]{1,0:T(8,128)S(1)}, u32[]{:S(2)}, u32[]{:S(2)}) collective-permute-start(f32[8,128]{1,0:T(8,128)S(1)} %get-tuple-element.129), channel_id=1, source_target_pairs={{0,1},{1,2},{2,3},{3,4},{4,5},{5,6},{6,7},{7,8},{8,9},{9,10},{10,1... | collective-permute-start | bytes 12296 | tf_op jit(solution)/shard_map/ppermute | solution.py:760
  40.8 0.0 collective-permute-start.15
  40.8 0.0 all-to-all-done.1.recv_ref
  40.8 4.4 %force.1 = (f32[3,64,128]{2,1,0:T(8,128)S(1)}, f32[3,8,256]{2,1,0:T(8,128)S(1)}) custom-call(f32[128,1,384]{2,1,0:T(1,128)S(1)} %all-to-all-done.1.recv_ref), custom_call_target="tpu_custom_call" | custom-call | tf_op jit(solution)/shard_map/force/pallas_call | solution.py:373
  45.2 0.0 collective-permute-done.14.vlow_ref
  45.2 0.0 collective-permute-done.15.vhigh_ref
  45.2 0.0 copy-done.7
  45.2 7.0 %shell.3 = (f32[3,64,128]{2,1,0:T(8,128)S(1)}, f32[128,1,512]{2,1,0:T(1,128)}) custom-call(f32[12,12]{1,0:T(8,128)S(1)} %copy-done.7, f32[3,64,128]{2,1,0:T(8,128)S(1)} %get-tuple-element.125.f_ref, f32[3,8,256]{2,1,0:T(8,128)S(1)} %get-tuple-element.126.rim_ref, f32[64,128]{1,0:T(8,128)S(1)} %copy-done.3, f32[64,128]{1,0:T(8,128)S(1)} %copy-done, ...), custom_call_target="tpu_custom_call" | custom-call | tf_op jit(solution)/shard_map/shell/pallas_call | solution.py:568
  52.2 0.0 collective-permute-done.16.xp_ref
  52.2 0.0 copy-start.8
  52.2 0.0 collective-permute-done.17.xm_ref
  52.2 0.0 copy-start.9
  52.2 8.7 %all-to-all-start.2 = ((f32[128,1,512]{2,1,0:T(1,128)}), f32[128,1,512]{2,1,0:T(1,128)S(1)}, u32[]{:S(2)}, u32[]{:S(2)}) async-start(f32[128,1,512]{2,1,0:T(1,128)} %get-tuple-element.135), calls=%async_computation.2 | async-start | bytes 524288 | tf_op jit(solution)/shard_map/all_to_all | solution.py:811
  60.9 0.0 copy-done.11
  61.0 1.7 %collective-permute-start.18 = (f32[5,32,256]{2,1,0:T(8,128)S(1)}, f32[5,32,256]{2,1,0:T(8,128)S(1)}, u32[]{:S(2)}, u32[]{:S(2)}) collective-permute-start(f32[5,32,256]{2,1,0:T(8,128)S(1)} %scatter.15), channel_id=1, source_target_pairs={{0,1},{1,2},{2,3},{3,4},{4,5},{5,6},{6,7},{7,8},{8,9},{9,10},{10,1... | collective-permute-start | bytes 491528 | tf_op jit(solution)/shard_map/ppermute | solution.py:760
  62.7 0.0 copy-done.10
  62.8 0.3 collective-permute-start.19
  63.0 2.3 %collective-permute-done.18.yp_ref = f32[5,32,256]{2,1,0:T(8,128)S(1)} collective-permute-done((f32[5,32,256]{2,1,0:T(8,128)S(1)}, f32[5,32,256]{2,1,0:T(8,128)S(1)}, u32[]{:S(2)}, u32[]{:S(2)}) %collective-permute-start.18) | collective-permute-done | bytes 163872 | tf_op jit(solution)/shard_map/ppermute | solution.py:760
  65.3 0.0 copy-start.5
  65.3 2.8 %collective-permute-done.19.ym_ref = f32[5,32,256]{2,1,0:T(8,128)S(1)} collective-permute-done((f32[5,32,256]{2,1,0:T(8,128)S(1)}, f32[5,32,256]{2,1,0:T(8,128)S(1)}, u32[]{:S(2)}, u32[]{:S(2)}) %collective-permute-start.19) | collective-permute-done | bytes 163872 | tf_op jit(solution)/shard_map/ppermute | solution.py:760
  68.1 4.0 %all-to-all-done.2.part_ref = f32[128,1,512]{2,1,0:T(1,128)S(1)} async-done(((f32[128,1,512]{2,1,0:T(1,128)}), f32[128,1,512]{2,1,0:T(1,128)S(1)}, u32[]{:S(2)}, u32[]{:S(2)}) %all-to-all-start.2) | async-done | bytes 262176 | tf_op jit(solution)/shard_map/all_to_all | solution.py:811
  72.1 0.8 %scalars.1 = (f32[2]{0:T(128)S(1)}, s32[1]{0:T(128)}) custom-call(f32[128,1,512]{2,1,0:T(1,128)S(1)} %all-to-all-done.2.part_ref), custom_call_target="tpu_custom_call" | custom-call | tf_op jit(solution)/shard_map/scalars/pallas_call | solution.py:618
  73.6 0.0 copy-done.8
  73.6 0.0 copy-done.9
  73.6 0.0 copy-done.5
  73.6 0.0 copy-done.6
  73.6 0.3 conditional.1
  73.9 9.6 %outputs.1 = (f32[19,256,256]{2,1,0:T(8,128)}, f32[3,64,128]{2,1,0:T(8,128)}) custom-call(f32[2]{0:T(128)S(1)} %get-tuple-element.144.pq_ref, f32[128,1,512]{2,1,0:T(1,128)S(1)} %get-tuple-element.145.back_ref, f32[256,4096]{1,0:T(8,128)} %get-tuple-element.146.w_ref, s32[1,4096]{1,0:T(1,128)} %bitcast.63, s32[1,4096]{1,0:T(1,128)} %bitcast.59, ...), custom_call_target="tpu_custom_call" | custom-call | tf_op jit(solution)/shard_map/outputs/pallas_call | solution.py:723
  (7 shorter events, 0.2 us)
Async XLA Ops:
  1.4 16.4 %collective-permute-start.12 = (f32[8,128]{1,0:T(8,128)S(1)}, f32[8,128]{1,0:T(8,128)S(1)}, u32[]{:S(2)}, u32[]{:S(2)}) collective-permute-start(f32[8,128]{1,0:T(8,128)S(1)} %get-tuple-element.122), channel_id=1, source_target_pairs={{0,32},{32,64},{64,96},{96,0},{1,33},{33,65},{65,97},{97,1},{2,34}... | collective-permute-start | bytes 12296 | tf_op jit(solution)/shard_map/ppermute | solution.py:760
  3.6 14.3 %collective-permute-start.13 = (f32[8,128]{1,0:T(8,128)S(1)}, f32[8,128]{1,0:T(8,128)S(1)}, u32[]{:S(2)}, u32[]{:S(2)}) collective-permute-start(f32[8,128]{1,0:T(8,128)S(1)} %get-tuple-element.123), channel_id=1, source_target_pairs={{0,96},{32,0},{64,32},{96,64},{1,97},{33,1},{65,33},{97,65},{2,98}... | collective-permute-start | bytes 12296 | tf_op jit(solution)/shard_map/ppermute | solution.py:760
  17.9 22.9 %all-to-all-start.1 = ((f32[128,1,384]{2,1,0:T(1,128)}), f32[128,1,384]{2,1,0:T(1,128)S(1)}, u32[]{:S(2)}, u32[]{:S(2)}) async-start(f32[128,1,384]{2,1,0:T(1,128)} %get-tuple-element.124), calls=%async_computation.1 | async-start | bytes 393216 | tf_op jit(solution)/shard_map/all_to_all | solution.py:811
  27.9 10.6 %copy-start = (f32[64,128]{1,0:T(8,128)S(1)}, f32[64,128]{1,0:T(8,128)}, u32[]{:S(2)}) copy-start(f32[64,128]{1,0:T(8,128)} %mod_ref.5) | copy-start | bytes 98308
  27.9 10.6 %copy-start.3 = (f32[64,128]{1,0:T(8,128)S(1)}, f32[64,128]{1,0:T(8,128)}, u32[]{:S(2)}) copy-start(f32[64,128]{1,0:T(8,128)} %mass_ref.5) | copy-start | bytes 98308
  27.9 10.6 %copy-start.4 = (s32[64,128]{1,0:T(8,128)S(1)}, s32[64,128]{1,0:T(8,128)}, u32[]{:S(2)}) copy-start(s32[64,128]{1,0:T(8,128)} %live_ref.5) | copy-start | bytes 98308
  27.9 17.3 %copy-start.7 = (f32[12,12]{1,0:T(8,128)S(1)}, f32[12,12]{1,0:T(8,128)}, u32[]{:S(2)}) copy-start(f32[12,12]{1,0:T(8,128)} %stiff_ref.1) | copy-start | bytes 1732
  35.7 25.2 %copy-start.11 = (f32[5,32,256]{2,1,0:T(8,128)S(1)}, f32[5,32,256]{2,1,0:T(8,128)}, u32[]{:S(2)}) copy-start(f32[5,32,256]{2,1,0:T(8,128)} %get-tuple-element.136) | copy-start | bytes 491524
  35.7 27.0 %copy-start.10 = (f32[5,32,256]{2,1,0:T(8,128)S(1)}, f32[5,32,256]{2,1,0:T(8,128)}, u32[]{:S(2)}) copy-start(f32[5,32,256]{2,1,0:T(8,128)} %get-tuple-element.139) | copy-start | bytes 491524
  35.7 16.5 %collective-permute-start.16 = (f32[5,8,256]{2,1,0:T(8,128)}, f32[5,8,256]{2,1,0:T(8,128)S(1)}, u32[]{:S(2)}, u32[]{:S(2)}) collective-permute-start(f32[5,8,256]{2,1,0:T(8,128)} %get-tuple-element.133), channel_id=1, source_target_pairs={{0,32},{32,64},{64,96},{96,0},{1,33},{33,65},{65,97},{97,1},{2,34}... | collective-permute-start | bytes 122888 | tf_op jit(solution)/shard_map/ppermute | solution.py:760
  37.1 15.1 %collective-permute-start.17 = (f32[5,8,256]{2,1,0:T(8,128)}, f32[5,8,256]{2,1,0:T(8,128)S(1)}, u32[]{:S(2)}, u32[]{:S(2)}) collective-permute-start(f32[5,8,256]{2,1,0:T(8,128)} %get-tuple-element.134), channel_id=1, source_target_pairs={{0,96},{32,0},{64,32},{96,64},{1,97},{33,1},{65,33},{97,65},{2,98}... | collective-permute-start | bytes 122888 | tf_op jit(solution)/shard_map/ppermute | solution.py:760
  38.6 6.6 %collective-permute-start.14 = (f32[8,128]{1,0:T(8,128)S(1)}, f32[8,128]{1,0:T(8,128)S(1)}, u32[]{:S(2)}, u32[]{:S(2)}) collective-permute-start(f32[8,128]{1,0:T(8,128)S(1)} %get-tuple-element.129), channel_id=1, source_target_pairs={{0,1},{1,2},{2,3},{3,4},{4,5},{5,6},{6,7},{7,8},{8,9},{9,10},{10,1... | collective-permute-start | bytes 12296 | tf_op jit(solution)/shard_map/ppermute | solution.py:760
  40.8 4.4 %collective-permute-start.15 = (f32[8,128]{1,0:T(8,128)S(1)}, f32[8,128]{1,0:T(8,128)S(1)}, u32[]{:S(2)}, u32[]{:S(2)}) collective-permute-start(f32[8,128]{1,0:T(8,128)S(1)} %get-tuple-element.130), channel_id=1, source_target_pairs={{0,31},{1,0},{2,1},{3,2},{4,3},{5,4},{6,5},{7,6},{8,7},{9,8},{10,9... | collective-permute-start | bytes 12296 | tf_op jit(solution)/shard_map/ppermute | solution.py:760
  52.2 21.4 %copy-start.8 = (f32[5,8,256]{2,1,0:T(8,128)}, f32[5,8,256]{2,1,0:T(8,128)S(1)}, u32[]{:S(2)}) copy-start(f32[5,8,256]{2,1,0:T(8,128)S(1)} %collective-permute-done.16.xp_ref) | copy-start | bytes 122884
  52.2 21.4 %copy-start.9 = (f32[5,8,256]{2,1,0:T(8,128)}, f32[5,8,256]{2,1,0:T(8,128)S(1)}, u32[]{:S(2)}) copy-start(f32[5,8,256]{2,1,0:T(8,128)S(1)} %collective-permute-done.17.xm_ref) | copy-start | bytes 122884
  52.2 19.9 %all-to-all-start.2 = ((f32[128,1,512]{2,1,0:T(1,128)}), f32[128,1,512]{2,1,0:T(1,128)S(1)}, u32[]{:S(2)}, u32[]{:S(2)}) async-start(f32[128,1,512]{2,1,0:T(1,128)} %get-tuple-element.135), calls=%async_computation.2 | async-start | bytes 524288 | tf_op jit(solution)/shard_map/all_to_all | solution.py:811
  61.0 4.3 %collective-permute-start.18 = (f32[5,32,256]{2,1,0:T(8,128)S(1)}, f32[5,32,256]{2,1,0:T(8,128)S(1)}, u32[]{:S(2)}, u32[]{:S(2)}) collective-permute-start(f32[5,32,256]{2,1,0:T(8,128)S(1)} %scatter.15), channel_id=1, source_target_pairs={{0,1},{1,2},{2,3},{3,4},{4,5},{5,6},{6,7},{7,8},{8,9},{9,10},{10,1... | collective-permute-start | bytes 491528 | tf_op jit(solution)/shard_map/ppermute | solution.py:760
  62.8 5.3 %collective-permute-start.19 = (f32[5,32,256]{2,1,0:T(8,128)S(1)}, f32[5,32,256]{2,1,0:T(8,128)S(1)}, u32[]{:S(2)}, u32[]{:S(2)}) collective-permute-start(f32[5,32,256]{2,1,0:T(8,128)S(1)} %scatter.19), channel_id=1, source_target_pairs={{0,31},{1,0},{2,1},{3,2},{4,3},{5,4},{6,5},{7,6},{8,7},{9,8},{10,9... | collective-permute-start | bytes 491528 | tf_op jit(solution)/shard_map/ppermute | solution.py:760
  65.3 8.3 %copy-start.5 = (f32[5,32,256]{2,1,0:T(8,128)}, f32[5,32,256]{2,1,0:T(8,128)S(1)}, u32[]{:S(2)}) copy-start(f32[5,32,256]{2,1,0:T(8,128)S(1)} %collective-permute-done.18.yp_ref) | copy-start | bytes 491524
  68.1 5.6 %copy-start.6 = (f32[5,32,256]{2,1,0:T(8,128)}, f32[5,32,256]{2,1,0:T(8,128)S(1)}, u32[]{:S(2)}) copy-start(f32[5,32,256]{2,1,0:T(8,128)S(1)} %collective-permute-done.19.ym_ref) | copy-start | bytes 491524

commit v5 on v4

--- a/solution.py
+++ b/solution.py
@@ -78,6 +78,40 @@
     return lax.dot_general(a, b, (((1,), (0,)), ((), ())), preferred_element_type=F32)
 
 
+def relaxed_of(pops, wanted):
+    density = pops[0]
+    for q in range(1, 19):
+        density = density + pops[q]
+    inverse = 1.0 / density
+    velocity = []
+    for axis in range(3):
+        total = None
+        for q in range(1, 19):
+            if DIRS[q][axis] != 0:
+                term = pops[q] if DIRS[q][axis] == 1 else -pops[q]
+                total = term if total is None else total + term
+        velocity.append(total * inverse)
+    squared = velocity[0] * velocity[0] + velocity[1] * velocity[1] + velocity[2] * velocity[2]
+    base = 1.0 - 1.5 * squared
+    result = []
+    for q in wanted:
+        along = combine(velocity, DIRS[q])
+        bracket = base if along is None else base + along * (3.0 + 4.5 * along)
+        relaxed = pops[q] - RATE * (pops[q] - (WEIGHTS[q] * density) * bracket)
+        if DIRS[q][2] != 0:
+            relaxed = pltpu.roll(relaxed, 1 if DIRS[q][2] == 1 else NK - 1, 1)
+        result.append(relaxed)
+    return result
+
+
+def turned_y(value, cy):
+    return value if cy == 0 else pltpu.roll(value, 1 if cy == 1 else 7, 0)
+
+
+XMSG = 48
+YMSG = 168
+
+
 CHUNKS = 4
 CROWS = NB // CHUNKS
 RSTEPS = R // RB
@@ -120,7 +154,8 @@
 
 
 def load_kernel(
-    pop_hbm, w_ref, blk_ref, own_all_ref, node_all_ref, own_ref, node_ref, send_ref, rank_ref, wt_ref,
+    pop_hbm, w_ref, blk_ref, own_all_ref, node_all_ref, own_ref, node_ref, mass_ref, mod_ref, live_ref,
+    send_ref, rank_ref, wt_ref, xp_ref, xm_ref, yp_ref, ym_ref,
     pop_ref, sems, m_ref, mt_ref, tri_ref, carry_ref, dest_ref, code_ref, place_ref, over_ref, main_ref, rims_ref,
 ):
     step = pl.program_id(0)
@@ -175,6 +210,31 @@
         for part in range(CHUNKS):
             fetch(part).wait()
             lax.fori_loop(part * CROWS // 8, (part + 1) * CROWS // 8, rows_of, 0, unroll=2)
+        for face_ref, dirs, x in ((xp_ref, XP, 31), (xm_ref, XM, 0)):
+            values = relaxed_of([pop_ref[q, x * 8 : x * 8 + 8, :] for q in range(19)], dirs)
+            for i, q in enumerate(dirs):
+                face_ref[i * 8 : i * 8 + 8, :] = turned_y(values[i], DIRS[q][1])
+            face_ref[40:XMSG, :] = jnp.zeros((XMSG - 40, NK), F32)
+        for i, field in enumerate([mass_ref[...], mod_ref[...], live_ref[...].astype(F32)]):
+            xp_ref[40 + i : 41 + i, 0:NV] = field[NU - 1 : NU, :]
+            xm_ref[40 + 2 * i : 42 + 2 * i, 0:NV] = field[0:2, :]
+        sub = iota((8, NK), 0)
+        for face_ref, dirs, y in ((yp_ref, YP, 7), (ym_ref, YM, 0)):
+            for part in range(4):
+                pops = []
+                for q in range(19):
+                    tile = None
+                    for i in range(8):
+                        row = jnp.broadcast_to(pop_ref[q, pl.ds(part * 64 + i * 8 + y, 1), :], (8, NK))
+                        tile = row if tile is None else jnp.where(sub == i, row, tile)
+                    pops.append(tile)
+                values = relaxed_of(pops, dirs)
+                for i in range(5):
+                    face_ref[i * 32 + part * 8 : i * 32 + part * 8 + 8, :] = values[i]
+            for i, q in enumerate(dirs):
+                if DIRS[q][0] != 0:
+                    face = face_ref[i * 32 : i * 32 + 32, :]
+                    face_ref[i * 32 : i * 32 + 32, :] = pltpu.roll(face, 1 if DIRS[q][0] == 1 else 31, 0)
         for axis in range(3):
             turned = m_ref[axis].T
             high = turned.astype(BF16)
@@ -218,12 +278,16 @@
         send_ref[:, 0, MAIN : MAIN + 4 * RIM] = jnp.where(iota((ND, 4 * RIM), 1) == 4 * RIM - 1, flag, tail)
 
 
-def loads_to_send(pops, weights, block_row, owner_row, node_row):
+def loads_to_send(pops, weights, block_row, owner_row, node_row, mass, modulus, live):
     def record(i):
         return jnp.maximum(i - 1, 0)
 
     row_spec = pl.BlockSpec((1, RB), lambda i: (0, record(i)))
     all_rows = pl.BlockSpec((1, R), lambda i: (0, 0))
+
+    def whole(*shape):
+        return pl.BlockSpec(shape, lambda i: (0, 0))
+
     return pl.pallas_call(
         load_kernel,
         grid=(1 + RSTEPS,),
@@ -235,16 +299,27 @@
             all_rows,
             row_spec,
             row_spec,
+            whole(NU, NV),
+            whole(NU, NV),
+            whole(NU, NV),
         ],
         out_specs=[
             pl.BlockSpec((ND, 1, MAIN + 4 * RIM), lambda i: (0, 0, 0)),
             all_rows,
             pl.BlockSpec((NK, RB), lambda i: (0, record(i))),
+            whole(XMSG, NK),
+            whole(XMSG, NK),
+            whole(160, NK),
+            whole(160, NK),
         ],
         out_shape=[
             jax.ShapeDtypeStruct((ND, 1, MAIN + 4 * RIM), F32),
             jax.ShapeDtypeStruct((1, R), jnp.int32),
             jax.ShapeDtypeStruct((NK, R), F32),
+            jax.ShapeDtypeStruct((XMSG, NK), F32),
+            jax.ShapeDtypeStruct((XMSG, NK), F32),
+            jax.ShapeDtypeStruct((160, NK), F32),
+            jax.ShapeDtypeStruct((160, NK), F32),
         ],
         scratch_shapes=[
             pltpu.VMEM((19, NB, NK), F32),
@@ -262,60 +337,60 @@
         ],
         compiler_params=pltpu.CompilerParams(vmem_limit_bytes=VMEM_LIMIT),
         name="loads",
-    )(pops, weights, block_row, owner_row, node_row, owner_row, node_row)
-
-
-def collide_kernel(pop_ref, read_ref, xp_ref, xm_ref, yp_ref, ym_ref):
+    )(pops, weights, block_row, owner_row, node_row, owner_row, node_row, mass, modulus, live)
+
+
+LINES = 8
+
+
+def collide_kernel(pop_hbm, out_hbm, pop_ref, read_ref, in_sems, out_sems):
+    chunks = 32 // LINES
+
+    def fetch(part):
+        rows = pl.ds(part * LINES * 8, LINES * 8)
+        return pltpu.make_async_copy(pop_hbm.at[:, rows, :], pop_ref.at[:, rows, :], in_sems.at[part])
+
+    def store(part):
+        first = max(part * LINES - 1, 0) * 8
+        last = NB if part == chunks - 1 else (part * LINES + LINES - 1) * 8
+        rows = pl.ds(first, last - first)
+        kept = pl.ds(first + 8, last - first)
+        return pltpu.make_async_copy(read_ref.at[:, kept, :], out_hbm.at[:, rows, :], out_sems.at[part])
+
     def line(x, _):
         rows = pl.ds(pl.multiple_of(x * 8, 8), 8)
-        pops = [pop_ref[q, rows, :] for q in range(19)]
-        density = pops[0]
-        for q in range(1, 19):
-            density = density + pops[q]
-        inverse = 1.0 / density
-        velocity = []
-        for axis in range(3):
-            total = None
-            for q in range(1, 19):
-                if DIRS[q][axis] != 0:
-                    term = pops[q] if DIRS[q][axis] == 1 else -pops[q]
-                    total = term if total is None else total + term
-            velocity.append(total * inverse)
-        squared = velocity[0] * velocity[0] + velocity[1] * velocity[1] + velocity[2] * velocity[2]
-        base = 1.0 - 1.5 * squared
+        values = relaxed_of([pop_ref[q, rows, :] for q in range(19)], range(19))
         for q in range(19):
-            cx, cy, cz = DIRS[q]
-            along = combine(velocity, DIRS[q])
-            bracket = base if along is None else base + along * (3.0 + 4.5 * along)
-            relaxed = pops[q] - RATE * (pops[q] - (WEIGHTS[q] * density) * bracket)
-            if cz != 0:
-                relaxed = pltpu.roll(relaxed, 1 if cz == 1 else NK - 1, 1)
-            if cy != 0:
-                relaxed = pltpu.roll(relaxed, 1 if cy == 1 else 7, 0)
-            if cy == 1:
-                yp_ref[YP.index(q), pl.ds(lax.rem(x + cx + 32, 32), 1), :] = relaxed[0:1, :]
-            if cy == -1:
-                ym_ref[YM.index(q), pl.ds(lax.rem(x + cx + 32, 32), 1), :] = relaxed[7:8, :]
-            to = pl.ds(pl.multiple_of(lax.rem(x + cx + 32, 32) * 8, 8), 8)
-            read_ref[q, to, :] = relaxed
+            cx, cy, _ = DIRS[q]
+            to = pl.ds(pl.multiple_of((x + cx + 1) * 8, 8), 8)
+            read_ref[q, to, :] = turned_y(values[q], cy)
         return 0
 
-    lax.fori_loop(0, 32, line, 0, unroll=4)
-    for i, q in enumerate(XP):
-        xp_ref[i] = read_ref[q, 0:8, :]
-    for i, q in enumerate(XM):
-        xm_ref[i] = read_ref[q, NB - 8 : NB, :]
+    for part in range(chunks):
+        fetch(part).start()
+    for q in XP:
+        read_ref[q, 8:16, :] = jnp.zeros((8, NK), F32)
+    for q in XM:
+        read_ref[q, NB : NB + 8, :] = jnp.zeros((8, NK), F32)
+    for part in range(chunks):
+        fetch(part).wait()
+        lax.fori_loop(part * LINES, (part + 1) * LINES, line, 0, unroll=4)
+        store(part).start()
+    for part in range(chunks):
+        store(part).wait()
 
 
 def collide_and_run(pops):
     return pl.pallas_call(
         collide_kernel,
-        out_shape=[
-            jax.ShapeDtypeStruct((19, NB, NK), F32),
-            jax.ShapeDtypeStruct((5, 8, NK), F32),
-            jax.ShapeDtypeStruct((5, 8, NK), F32),
-            jax.ShapeDtypeStruct((5, 32, NK), F32),
-            jax.ShapeDtypeStruct((5, 32, NK), F32),
+        in_specs=[pl.BlockSpec(memory_space=pl.ANY)],
+        out_specs=pl.BlockSpec(memory_space=pl.ANY),
+        out_shape=jax.ShapeDtypeStruct((19, NB, NK), F32),
+        scratch_shapes=[
+            pltpu.VMEM((19, NB, NK), F32),
+            pltpu.VMEM((19, NB + 16, NK), F32),
+            pltpu.SemaphoreType.DMA((32 // LINES,)),
+            pltpu.SemaphoreType.DMA((32 // LINES,)),
         ],
         compiler_params=pltpu.CompilerParams(vmem_limit_bytes=VMEM_LIMIT),
         name="collide",
@@ -386,40 +461,41 @@
     )(recv)
 
 
-def edge_kernel(mass_ref, mod_ref, live_ref, low_ref, high_ref):
-    low_ref[...] = jnp.zeros_like(low_ref)
-    high_ref[...] = jnp.zeros_like(high_ref)
+def rim_tile(i, low, high):
+    sub = iota((8, 128), 0)
+    tile = jnp.where(sub == 0, high[2 * i : 2 * i + 1, :], 0.0)
+    tile = jnp.where(sub == 1, high[2 * i + 1 : 2 * i + 2, :], tile)
+    return jnp.where(sub == 7, low[i : i + 1, :], tile)
+
+
+def side_kernel(mass_ref, mod_ref, live_ref, xp_ref, xm_ref, yp_ref, ym_ref, to_p_ref, to_m_ref):
+    to_p_ref[0:160, :] = yp_ref[...]
+    to_m_ref[0:160, :] = ym_ref[...]
+    for q, line, from_ref in ((7, 0, xp_ref), (10, 31, xm_ref)):
+        face = (XP if line == 0 else XM).index(q) * 8
+        at = YP.index(q) * 32 + line
+        to_p_ref[at : at + 1, :] = from_ref[face : face + 1, :]
+    for q, line, from_ref in ((9, 0, xp_ref), (8, 31, xm_ref)):
+        face = (XP if line == 0 else XM).index(q) * 8 + 7
+        at = YM.index(q) * 32 + line
+        to_m_ref[at : at + 1, :] = from_ref[face : face + 1, :]
+    to_p_ref[160:YMSG, :] = jnp.zeros((YMSG - 160, NK), F32)
+    to_m_ref[160:YMSG, :] = jnp.zeros((YMSG - 160, NK), F32)
+    low, high = xp_ref[40:XMSG, 0:NV], xm_ref[40:XMSG, 0:NV]
     for i, field in enumerate([mass_ref[...], mod_ref[...], live_ref[...].astype(F32)]):
-        low_ref[i : i + 1, :] = field[NU - 1 : NU, :]
-        high_ref[2 * i : 2 * i + 2, :] = field[0:2, :]
-
-
-def rim_tile(i, low_ref, high_ref):
-    sub = iota((8, 128), 0)
-    tile = jnp.where(sub == 0, high_ref[2 * i : 2 * i + 1, :], 0.0)
-    tile = jnp.where(sub == 1, high_ref[2 * i + 1 : 2 * i + 2, :], tile)
-    return jnp.where(sub == 7, low_ref[i : i + 1, :], tile)
-
-
-def side_kernel(mass_ref, mod_ref, live_ref, low_ref, high_ref, to_low_ref, to_high_ref):
-    to_low_ref[...] = jnp.zeros_like(to_low_ref)
-    to_high_ref[...] = jnp.zeros_like(to_high_ref)
-    for i, field in enumerate([mass_ref[...], mod_ref[...], live_ref[...].astype(F32)]):
-        whole = jnp.concatenate(
-            [field, rim_tile(i, low_ref, high_ref), jnp.zeros((128 - EU, 128), F32)], axis=0
-        )
-        turned = whole.T
-        to_low_ref[i : i + 1, :] = turned[127:128, :]
-        to_high_ref[2 * i : 2 * i + 2, :] = turned[0:2, :]
-
-
-def edge_call(kernel, name, *args):
+        tall = jnp.concatenate([field, rim_tile(i, low, high), jnp.zeros((128 - EU, 128), F32)], axis=0)
+        turned = tall.T
+        to_p_ref[160 + i : 161 + i, 0:128] = turned[127:128, :]
+        to_m_ref[160 + 2 * i : 162 + 2 * i, 0:128] = turned[0:2, :]
+
+
+def sides_of(mass, modulus, live, xp, xm, yp, ym):
     return pl.pallas_call(
-        kernel,
-        out_shape=[jax.ShapeDtypeStruct((8, 128), F32), jax.ShapeDtypeStruct((8, 128), F32)],
+        side_kernel,
+        out_shape=[jax.ShapeDtypeStruct((YMSG, NK), F32), jax.ShapeDtypeStruct((YMSG, NK), F32)],
         compiler_params=pltpu.CompilerParams(vmem_limit_bytes=SMALL_LIMIT),
-        name=name,
-    )(*args)
+        name="sides",
+    )(mass, modulus, live, xp, xm, yp, ym)
 
 
 def shell_kernel(
@@ -437,9 +513,11 @@
 
     for i, field in enumerate([mass_ref[...], mod_ref[...], live_ref[...].astype(F32)]):
         e_ref[3 + i, 0:NU, 0:NV] = field
-        e_ref[3 + i, NU:EU, 0:NV] = rim_tile(i, ulow_ref, uhigh_ref)
+        e_ref[3 + i, NU:EU, 0:NV] = rim_tile(i, ulow_ref[:, 0:NV], uhigh_ref[:, 0:NV])
         side = columns(
-            vhigh_ref[2 * i : 2 * i + 1, :], vhigh_ref[2 * i + 1 : 2 * i + 2, :], vlow_ref[i : i + 1, :]
+            vhigh_ref[2 * i : 2 * i + 1, 0:128],
+            vhigh_ref[2 * i + 1 : 2 * i + 2, 0:128],
+            vlow_ref[i : i + 1, 0:128],
         )
         e_ref[3 + i, :, NV:EV] = side[0:EU, :]
     wide = iota((8, EV), 0)
@@ -567,7 +645,12 @@
     vmem = pl.BlockSpec(memory_space=pltpu.VMEM)
     return pl.pallas_call(
         shell_kernel,
-        in_specs=[pl.BlockSpec(memory_space=pltpu.SMEM)] + [vmem] * 10,
+        grid=(1,),
+        in_specs=[pl.BlockSpec(memory_space=pltpu.SMEM)]
+        + [vmem] * 5
+        + [pl.BlockSpec((8, NK), lambda i: (5, 0))] * 2
+        + [pl.BlockSpec((8, NK), lambda i: (20, 0))] * 2
+        + [vmem],
         out_specs=[vmem, vmem],
         out_shape=[
             jax.ShapeDtypeStruct((3, NU, NV), F32),
@@ -695,13 +778,13 @@
                 cx, cy, _ = DIRS[q]
                 value = buf_ref[q, rows, :]
                 if cx == 1 and xx == 0:
-                    value = jnp.where(x == 0, xp_ref[XP.index(q)], value)
+                    value = jnp.where(x == 0, xp_ref[XP.index(q) * 8 : XP.index(q) * 8 + 8, :], value)
                 if cx == -1 and xx == XS - 1:
-                    value = jnp.where(x == 31, xm_ref[XM.index(q)], value)
+                    value = jnp.where(x == 31, xm_ref[XM.index(q) * 8 : XM.index(q) * 8 + 8, :], value)
                 if cy == 1:
-                    value = jnp.where(sub == 0, yp_ref[YP.index(q), pl.ds(x, 1), :], value)
+                    value = jnp.where(sub == 0, yp_ref[pl.ds(YP.index(q) * 32 + x, 1), :], value)
                 if cy == -1:
-                    value = jnp.where(sub == 7, ym_ref[YM.index(q), pl.ds(x, 1), :], value)
+                    value = jnp.where(sub == 7, ym_ref[pl.ds(YM.index(q) * 32 + x, 1), :], value)
                 along = combine(forcing, DIRS[q])
                 if along is not None:
                     value = value + (3.0 * WEIGHTS[q]) * along
@@ -718,8 +801,8 @@
     row_spec = pl.BlockSpec((1, OB), lambda i: (0, record(i)))
     patch = pl.BlockSpec((3, NU, NV), lambda i: (0, 0, 0))
     lines = pl.BlockSpec((19, XS * 8, NK), lambda i: (0, slab(i), 0))
-    x_face = pl.BlockSpec((5, 8, NK), lambda i: (0, 0, 0))
-    y_face = pl.BlockSpec((5, 32, NK), lambda i: (0, 0, 0))
+    x_face = pl.BlockSpec((40, NK), lambda i: (0, 0))
+    y_face = pl.BlockSpec((160, NK), lambda i: (0, 0))
     return pl.pallas_call(
         next_kernel,
         grid=(OREC + OSTEPS,),
@@ -817,29 +900,23 @@
     owner_row = rec_owner.reshape(1, R)
     node_row = rec_node.reshape(1, R)
 
-    low, high = edge_call(edge_kernel, "edges", mass, modulus, live)
-    ulow = pass_on(low, "gx", 1)
-    uhigh = pass_on(high, "gx", -1)
-    send, rank_row, turned = loads_to_send(pops, weights, block_row, owner_row, node_row)
-    send, ulow, uhigh, pops = lax.optimization_barrier((send, ulow, uhigh, pops))
-    recv = exchange(send)
-    low, high = edge_call(side_kernel, "sides", mass, modulus, live, ulow, uhigh)
-    rims = (ulow, uhigh, pass_on(low, "gy", 1), pass_on(high, "gy", -1))
-
-    read, xp, xm, yp, ym = collide_and_run(pops)
+    send, rank_row, turned, xp, xm, yp, ym = loads_to_send(
+        pops, weights, block_row, owner_row, node_row, mass, modulus, live
+    )
     xp = pass_on(xp, "gx", 1)
     xm = pass_on(xm, "gx", -1)
+    recv = exchange(send)
+    yp, ym = sides_of(mass, modulus, live, xp, xm, yp, ym)
+    yp = pass_on(yp, "gy", 1)
+    ym = pass_on(ym, "gy", -1)
+    rims = (xp, xm, yp, ym)
 
     force, rim = force_of(recv)
     image, ret = shell_of(stiff, force, rim, mass, modulus, live, rims, recv)
-    ret, xp, xm = lax.optimization_barrier((ret, xp, xm))
+    ret, pops = lax.optimization_barrier((ret, pops))
     back = exchange(ret)
-    yp = yp.at[YP.index(7), 0].set(xp[XP.index(7), 0]).at[YP.index(10), 31].set(xm[XM.index(10), 0])
-    ym = ym.at[YM.index(9), 0].set(xp[XP.index(9), 7]).at[YM.index(8), 31].set(xm[XM.index(8), 7])
-    yp = pass_on(yp, "gy", 1)
-    ym = pass_on(ym, "gy", -1)
-
-    back, yp, ym = lax.optimization_barrier((back, yp, ym))
+    read = collide_and_run(pops)
+    back, read = lax.optimization_barrier((back, read))
     pq, sound = scalars_of(back)
 
     def quick(operands):

time: 84 us -> 78.2 us (0.931)
  starting transfers between devices: 29.1 us -> 19.9 us
  waiting for transfers between devices: 9.08 us -> 12.6 us
  Pallas kernels: 43.4 us -> 41 us
  local copies, waits for them, and re-layouts: 0.22 us -> 2.55 us
    all_to_all x2, waiting for transfers between devices: 4.04 us -> 12.6 us  [exchange(): return lax.all_to_all(x, ALL, 0, 0, tiled=True)]
    ppermute x8 -> x4, starting transfers between devices: 10.5 us -> 5.43 us  [pass_on(): lax.ppermute(x, axis, [(i, (i + shift) % count) for i in range(count)])]
    ppermute x8 -> x4, waiting for transfers between devices: 5.04 us -> 0.01 us  [pass_on(): lax.ppermute(x, axis, [(i, (i + shift) % count) for i in range(count)])]
    all_to_all x2, starting transfers between devices: 18.6 us -> 14.5 us  [exchange(): return lax.all_to_all(x, ALL, 0, 0, tiled=True)]
    pallas_call x4 -> x3, Pallas kernels: 15.7 us -> 12.4 us  [the longest x1 7 us: shell_of(): pl.pallas_call(shell_kernel, grid=(1,), in_specs=[pl.BlockSpec(memory_spa...]
    unnamed x20 -> x12, local copies, waits for them, and re-layouts: 0.05 us -> 1.84 us
    pallas_call x1, Pallas kernels: 12.9 us -> 13.9 us  [loads_to_send(): pl.pallas_call(load_kernel, grid=(1 + RSTEPS,), in_specs=[pl.BlockSpec(me...]
  transfers between devices with their start and end apart: 10 -> 6, of which waited for: 3 -> 2; matrix products, arithmetic and copies ran while one was open for 0% -> 0% of each run, Pallas kernels for 38% -> 12%
where the time goes in v5:
time: 78.2 us; the launch traced here: 77.9 us
  Pallas kernels  41 us (52%)
  starting transfers between devices  19.9 us (25%)
  waiting for transfers between devices  12.6 us (16%)
  local copies, waits for them, and re-layouts  2.55 us (3%)
  between operations  1.62 us (2%)
    all_to_all x2, starting transfers between devices, exchange(): return lax.all_to_all(x, ALL, 0, 0, tiled=True)  14.5 us
    pallas_call x1, Pallas kernels, loads_to_send(): pl.pallas_call(load_kernel, grid=(1 + RSTEPS,), in_specs=[pl.BlockSpec(me...  13.9 us
    all_to_all x2, waiting for transfers between devices, exchange(): return lax.all_to_all(x, ALL, 0, 0, tiled=True)  12.6 us
    pallas_call x1, Pallas kernels, outputs_of(): pl.pallas_call(next_kernel, grid=(OREC + OSTEPS,), in_specs=[pl.BlockSpec...  9.54 us
    pallas_call x1, Pallas kernels, shell_of(): pl.pallas_call(shell_kernel, grid=(1,), in_specs=[pl.BlockSpec(memory_spa...  7 us
    ppermute x4, starting transfers between devices, pass_on(): lax.ppermute(x, axis, [(i, (i + shift) % count) for i in range(count)])  5.43 us
    pallas_call x1, Pallas kernels, collide_and_run(): pl.pallas_call(collide_kernel, in_specs=[pl.BlockSpec(memory_space=pl.ANY...  5.25 us
    pallas_call x1, Pallas kernels, force_of(): pl.pallas_call(force_kernel, out_shape=[jax.ShapeDtypeStruct((3, NU, NV),...  4.35 us
  transfers between devices with their start and end apart: 6, of which 2 were waited for; matrix products, arithmetic and copies ran while one was open for 0% of the time, Pallas kernels for 12%

profile of v5, /device:TPU:1, one launch (start us, length us, event | category | flops | bytes accessed | tf_op | source)
XLA Modules:
  0.0 77.9 jit_solution(12868286477186960424)
XLA Ops:
  0.6 0.0 copy-start.2
  0.6 0.0 copy-start.5
  0.7 0.0 copy-start.6
  0.7 13.9 %loads.1 = (f32[128,1,384]{2,1,0:T(1,128)}, s32[1,4096]{1,0:T(1,128)}, f32[256,4096]{1,0:T(8,128)}, f32[48,256]{1,0:T(8,128)}, f32[48,256]{1,0:T(8,128)}, /*index=5*/f32[160,256]{1,0:T(8,128)}, f32[160,256]{1,0:T(8,128)}) custom-call(f32[19,256,256]{2,1,0:T(8,128)} %bitcast.50, f32[4096,256]{1,0:T(8,128)} %w_ref.1, s32[1,4096]{1,0:T(1,128)} %bitcast.62, ...), custom_call_target="tpu_custom_call" | custom-call | tf_op jit(solution)/shard_map/loads/pallas_call | solution.py:291
  14.6 0.0 copy-start.7
  14.6 2.2 %collective-permute-start.12 = (f32[48,256]{1,0:T(8,128)}, f32[48,256]{1,0:T(8,128)S(1)}, u32[]{:S(2)}, u32[]{:S(2)}) collective-permute-start(f32[48,256]{1,0:T(8,128)} %get-tuple-element.67), channel_id=1, source_target_pairs={{0,32},{32,64},{64,96},{96,0},{1,33},{33,65},{65,97},{97,1},{2,34}... | collective-permute-start | bytes 147464 | tf_op jit(solution)/shard_map/ppermute | solution.py:843
  16.8 1.5 %collective-permute-start.13 = (f32[48,256]{1,0:T(8,128)}, f32[48,256]{1,0:T(8,128)S(1)}, u32[]{:S(2)}, u32[]{:S(2)}) collective-permute-start(f32[48,256]{1,0:T(8,128)} %get-tuple-element.68), channel_id=1, source_target_pairs={{0,96},{32,0},{64,32},{96,64},{1,97},{33,1},{65,33},{97,65},{2,98}... | collective-permute-start | bytes 147464 | tf_op jit(solution)/shard_map/ppermute | solution.py:843
  18.3 9.9 %all-to-all-start.1 = ((f32[128,1,384]{2,1,0:T(1,128)}), f32[128,1,384]{2,1,0:T(1,128)S(1)}, u32[]{:S(2)}, u32[]{:S(2)}) async-start(f32[128,1,384]{2,1,0:T(1,128)} %get-tuple-element.64), calls=%async_computation.1 | async-start | bytes 393216 | tf_op jit(solution)/shard_map/all_to_all | solution.py:894
  28.2 0.0 collective-permute-done.12.xp_ref.ulow_ref
  28.2 0.0 collective-permute-done.13.xm_ref.uhigh_ref
  28.2 0.0 copy-done.2
  28.3 0.0 copy-done.5
  28.3 0.0 copy-done.6
  28.3 0.0 copy-start
  28.3 0.9 %copy-done = f32[160,256]{1,0:T(8,128)S(1)} copy-done((f32[160,256]{1,0:T(8,128)S(1)}, f32[160,256]{1,0:T(8,128)}, u32[]{:S(2)}) %copy-start) | copy-done | bytes 163864
  29.2 0.0 copy-start.1
  29.2 0.9 %copy-done.1 = f32[160,256]{1,0:T(8,128)S(1)} copy-done((f32[160,256]{1,0:T(8,128)S(1)}, f32[160,256]{1,0:T(8,128)}, u32[]{:S(2)}) %copy-start.1) | copy-done | bytes 163864
  30.1 0.1 sides.1
  30.2 1.7 %collective-permute-start.14 = (f32[168,256]{1,0:T(8,128)S(1)}, f32[168,256]{1,0:T(8,128)S(1)}, u32[]{:S(2)}, u32[]{:S(2)}) collective-permute-start(f32[168,256]{1,0:T(8,128)S(1)} %get-tuple-element.71), channel_id=1, source_target_pairs={{0,1},{1,2},{2,3},{3,4},{4,5},{5,6},{6,7},{7,8},{8,9},{9,10},{10,1... | collective-permute-start | bytes 516104 | tf_op jit(solution)/shard_map/ppermute | solution.py:843
  31.9 0.0 collective-permute-start.15
  31.9 6.9 %all-to-all-done.1.recv_ref = f32[128,1,384]{2,1,0:T(1,128)S(1)} async-done(((f32[128,1,384]{2,1,0:T(1,128)}), f32[128,1,384]{2,1,0:T(1,128)S(1)}, u32[]{:S(2)}, u32[]{:S(2)}) %all-to-all-start.1) | async-done | bytes 196640 | tf_op jit(solution)/shard_map/all_to_all | solution.py:894
  38.9 4.3 %force.1 = (f32[3,64,128]{2,1,0:T(8,128)S(1)}, f32[3,8,256]{2,1,0:T(8,128)S(1)}) custom-call(f32[128,1,384]{2,1,0:T(1,128)S(1)} %all-to-all-done.1.recv_ref), custom_call_target="tpu_custom_call" | custom-call | tf_op jit(solution)/shard_map/force/pallas_call | solution.py:448
  43.2 0.0 collective-permute-done.14.vlow_ref.yp_ref
  43.2 0.0 collective-permute-done.15.vhigh_ref.ym_ref
  43.3 0.0 copy-done.7
  43.3 7.0 %shell.3 = (f32[3,64,128]{2,1,0:T(8,128)S(1)}, f32[128,1,512]{2,1,0:T(1,128)}) custom-call(f32[12,12]{1,0:T(8,128)S(1)} %copy-done.7, f32[3,64,128]{2,1,0:T(8,128)S(1)} %get-tuple-element.65.f_ref, f32[3,8,256]{2,1,0:T(8,128)S(1)} %get-tuple-element.66.rim_ref, f32[64,128]{1,0:T(8,128)S(1)} %copy-done.5, f32[64,128]{1,0:T(8,128)S(1)} %copy-done.2, ...), custom_call_target="tpu_custom_call" | custom-call | tf_op jit(solution)/shard_map/shell/pallas_call | solution.py:646
  50.3 4.6 %all-to-all-start.2 = ((f32[128,1,512]{2,1,0:T(1,128)}), f32[128,1,512]{2,1,0:T(1,128)S(1)}, u32[]{:S(2)}, u32[]{:S(2)}) async-start(f32[128,1,512]{2,1,0:T(1,128)} %get-tuple-element.74), calls=%async_computation.2 | async-start | bytes 524288 | tf_op jit(solution)/shard_map/all_to_all | solution.py:894
  54.9 5.2 %collide.1.read_ref = f32[19,256,256]{2,1,0:T(8,128)} custom-call(f32[19,256,256]{2,1,0:T(8,128)} %bitcast.51), custom_call_target="tpu_custom_call" | custom-call | tf_op jit(solution)/shard_map/collide/pallas_call | solution.py:384
  60.1 5.7 %all-to-all-done.2.part_ref = f32[128,1,512]{2,1,0:T(1,128)S(1)} async-done(((f32[128,1,512]{2,1,0:T(1,128)}), f32[128,1,512]{2,1,0:T(1,128)S(1)}, u32[]{:S(2)}, u32[]{:S(2)}) %all-to-all-start.2) | async-done | bytes 262176 | tf_op jit(solution)/shard_map/all_to_all | solution.py:894
  65.8 0.8 %scalars.1 = (f32[2]{0:T(128)S(1)}, s32[1]{0:T(128)}) custom-call(f32[128,1,512]{2,1,0:T(1,128)S(1)} %all-to-all-done.2.part_ref), custom_call_target="tpu_custom_call" | custom-call | tf_op jit(solution)/shard_map/scalars/pallas_call | solution.py:701
  67.3 0.9 %conditional.1 = (f32[2]{0:T(128)S(1)}, f32[3,64,128]{2,1,0:T(8,128)S(1)}, f32[128,1,512]{2,1,0:T(1,128)}) conditional(s32[]{:T(128)} %bitcast.22, (f32[3,64,128]{2,1,0:T(8,128)S(1)}, f32[12,12]{1,0:T(8,128)S(1)}, f32[64,128]{1,0:T(8,128)S(1)}, f32[64,128]{1,0:T(8,128)S(1)}, s32[64,128]{1,0:T(8,128)S(1)}, /*index=5*/f32[48,256]{1,0:T(8,128)S(1)}, ...), branch_computations={%region_0.0_spmd, %region_9.0_spmd} | conditional | flops 15798779 | bytes 9198656 | solution.py:939
  67.5 0.7 copy.69
  68.2 9.5 %outputs.1 = (f32[19,256,256]{2,1,0:T(8,128)}, f32[3,64,128]{2,1,0:T(8,128)}) custom-call(f32[2]{0:T(128)S(1)} %get-tuple-element.80.pq_ref, f32[128,1,512]{2,1,0:T(1,128)} %get-tuple-element.81.back_ref, f32[256,4096]{1,0:T(8,128)} %get-tuple-element.82.w_ref, s32[1,4096]{1,0:T(1,128)} %bitcast.63, s32[1,4096]{1,0:T(1,128)} %bitcast.59, ...), custom_call_target="tpu_custom_call" | custom-call | tf_op jit(solution)/shard_map/outputs/pallas_call | solution.py:806
Async XLA Ops:
  0.6 27.6 %copy-start.2 = (f32[64,128]{1,0:T(8,128)S(1)}, f32[64,128]{1,0:T(8,128)}, u32[]{:S(2)}) copy-start(f32[64,128]{1,0:T(8,128)} %mod_ref.5) | copy-start | bytes 98308
  0.6 27.6 %copy-start.5 = (f32[64,128]{1,0:T(8,128)S(1)}, f32[64,128]{1,0:T(8,128)}, u32[]{:S(2)}) copy-start(f32[64,128]{1,0:T(8,128)} %mass_ref.5) | copy-start | bytes 98308
  0.7 27.6 %copy-start.6 = (s32[64,128]{1,0:T(8,128)S(1)}, s32[64,128]{1,0:T(8,128)}, u32[]{:S(2)}) copy-start(s32[64,128]{1,0:T(8,128)} %live_ref.5) | copy-start | bytes 98308
  14.6 28.7 %copy-start.7 = (f32[12,12]{1,0:T(8,128)S(1)}, f32[12,12]{1,0:T(8,128)}, u32[]{:S(2)}) copy-start(f32[12,12]{1,0:T(8,128)} %stiff_ref.1) | copy-start | bytes 1732
  14.6 13.6 %collective-permute-start.12 = (f32[48,256]{1,0:T(8,128)}, f32[48,256]{1,0:T(8,128)S(1)}, u32[]{:S(2)}, u32[]{:S(2)}) collective-permute-start(f32[48,256]{1,0:T(8,128)} %get-tuple-element.67), channel_id=1, source_target_pairs={{0,32},{32,64},{64,96},{96,0},{1,33},{33,65},{65,97},{97,1},{2,34}... | collective-permute-start | bytes 147464 | tf_op jit(solution)/shard_map/ppermute | solution.py:843
  16.8 11.4 %collective-permute-start.13 = (f32[48,256]{1,0:T(8,128)}, f32[48,256]{1,0:T(8,128)S(1)}, u32[]{:S(2)}, u32[]{:S(2)}) collective-permute-start(f32[48,256]{1,0:T(8,128)} %get-tuple-element.68), channel_id=1, source_target_pairs={{0,96},{32,0},{64,32},{96,64},{1,97},{33,1},{65,33},{97,65},{2,98}... | collective-permute-start | bytes 147464 | tf_op jit(solution)/shard_map/ppermute | solution.py:843
  18.3 20.5 %all-to-all-start.1 = ((f32[128,1,384]{2,1,0:T(1,128)}), f32[128,1,384]{2,1,0:T(1,128)S(1)}, u32[]{:S(2)}, u32[]{:S(2)}) async-start(f32[128,1,384]{2,1,0:T(1,128)} %get-tuple-element.64), calls=%async_computation.1 | async-start | bytes 393216 | tf_op jit(solution)/shard_map/all_to_all | solution.py:894
  28.3 0.9 %copy-start = (f32[160,256]{1,0:T(8,128)S(1)}, f32[160,256]{1,0:T(8,128)}, u32[]{:S(2)}) copy-start(f32[160,256]{1,0:T(8,128)} %get-tuple-element.69.yp_ref) | copy-start | bytes 491524
  29.2 0.9 %copy-start.1 = (f32[160,256]{1,0:T(8,128)S(1)}, f32[160,256]{1,0:T(8,128)}, u32[]{:S(2)}) copy-start(f32[160,256]{1,0:T(8,128)} %get-tuple-element.70.ym_ref) | copy-start | bytes 491524
  30.2 13.0 %collective-permute-start.14 = (f32[168,256]{1,0:T(8,128)S(1)}, f32[168,256]{1,0:T(8,128)S(1)}, u32[]{:S(2)}, u32[]{:S(2)}) collective-permute-start(f32[168,256]{1,0:T(8,128)S(1)} %get-tuple-element.71), channel_id=1, source_target_pairs={{0,1},{1,2},{2,3},{3,4},{4,5},{5,6},{6,7},{7,8},{8,9},{9,10},{10,1... | collective-permute-start | bytes 516104 | tf_op jit(solution)/shard_map/ppermute | solution.py:843
  31.9 11.3 %collective-permute-start.15 = (f32[168,256]{1,0:T(8,128)S(1)}, f32[168,256]{1,0:T(8,128)S(1)}, u32[]{:S(2)}, u32[]{:S(2)}) collective-permute-start(f32[168,256]{1,0:T(8,128)S(1)} %get-tuple-element.72), channel_id=1, source_target_pairs={{0,31},{1,0},{2,1},{3,2},{4,3},{5,4},{6,5},{7,6},{8,7},{9,8},{10,9... | collective-permute-start | bytes 516104 | tf_op jit(solution)/shard_map/ppermute | solution.py:843
  50.3 15.5 %all-to-all-start.2 = ((f32[128,1,512]{2,1,0:T(1,128)}), f32[128,1,512]{2,1,0:T(1,128)S(1)}, u32[]{:S(2)}, u32[]{:S(2)}) async-start(f32[128,1,512]{2,1,0:T(1,128)} %get-tuple-element.74), calls=%async_computation.2 | async-start | bytes 524288 | tf_op jit(solution)/shard_map/all_to_all | solution.py:894

commit v6 on v5

--- a/solution.py
+++ b/solution.py
@@ -154,15 +154,19 @@
 
 
 def load_kernel(
-    pop_hbm, w_ref, blk_ref, own_all_ref, node_all_ref, own_ref, node_ref, mass_ref, mod_ref, live_ref,
+    pop_hbm, w_hbm, blk_ref, own_all_ref, node_all_ref, own_ref, node_ref, mass_ref, mod_ref, live_ref,
     send_ref, rank_ref, wt_ref, xp_ref, xm_ref, yp_ref, ym_ref,
-    pop_ref, sems, m_ref, mt_ref, tri_ref, carry_ref, dest_ref, code_ref, place_ref, over_ref, main_ref, rims_ref,
+    pop_ref, sems, w_ref, w_sems, m_ref, mt_ref, tri_ref, carry_ref, dest_ref, code_ref, place_ref, over_ref, main_ref, rims_ref,
 ):
     step = pl.program_id(0)
 
     def fetch(part):
         rows = pl.ds(part * CROWS, CROWS)
         return pltpu.make_async_copy(pop_hbm.at[:, rows, :], pop_ref.at[:, rows, :], sems.at[part])
+
+    def fetch_w(part):
+        rows = pl.ds(pl.multiple_of(part * RB, RB), RB)
+        return pltpu.make_async_copy(w_hbm.at[rows, :], w_ref.at[rows, :], w_sems.at[part])
 
     @pl.when(step == 0)
     def _():
@@ -207,20 +211,12 @@
                 m_ref[axis, rows, :] = total
             return 0
 
+        sub = iota((8, NK), 0)
         for part in range(CHUNKS):
             fetch(part).wait()
+            fetch_w(part).start()
             lax.fori_loop(part * CROWS // 8, (part + 1) * CROWS // 8, rows_of, 0, unroll=2)
-        for face_ref, dirs, x in ((xp_ref, XP, 31), (xm_ref, XM, 0)):
-            values = relaxed_of([pop_ref[q, x * 8 : x * 8 + 8, :] for q in range(19)], dirs)
-            for i, q in enumerate(dirs):
-                face_ref[i * 8 : i * 8 + 8, :] = turned_y(values[i], DIRS[q][1])
-            face_ref[40:XMSG, :] = jnp.zeros((XMSG - 40, NK), F32)
-        for i, field in enumerate([mass_ref[...], mod_ref[...], live_ref[...].astype(F32)]):
-            xp_ref[40 + i : 41 + i, 0:NV] = field[NU - 1 : NU, :]
-            xm_ref[40 + 2 * i : 42 + 2 * i, 0:NV] = field[0:2, :]
-        sub = iota((8, NK), 0)
-        for face_ref, dirs, y in ((yp_ref, YP, 7), (ym_ref, YM, 0)):
-            for part in range(4):
+            for face_ref, dirs, y in ((yp_ref, YP, 7), (ym_ref, YM, 0)):
                 pops = []
                 for q in range(19):
                     tile = None
@@ -231,10 +227,19 @@
                 values = relaxed_of(pops, dirs)
                 for i in range(5):
                     face_ref[i * 32 + part * 8 : i * 32 + part * 8 + 8, :] = values[i]
+        for face_ref, dirs in ((yp_ref, YP), (ym_ref, YM)):
             for i, q in enumerate(dirs):
                 if DIRS[q][0] != 0:
                     face = face_ref[i * 32 : i * 32 + 32, :]
                     face_ref[i * 32 : i * 32 + 32, :] = pltpu.roll(face, 1 if DIRS[q][0] == 1 else 31, 0)
+        for face_ref, dirs, x in ((xp_ref, XP, 31), (xm_ref, XM, 0)):
+            values = relaxed_of([pop_ref[q, x * 8 : x * 8 + 8, :] for q in range(19)], dirs)
+            for i, q in enumerate(dirs):
+                face_ref[i * 8 : i * 8 + 8, :] = turned_y(values[i], DIRS[q][1])
+            face_ref[40:XMSG, :] = jnp.zeros((XMSG - 40, NK), F32)
+        for i, field in enumerate([mass_ref[...], mod_ref[...], live_ref[...].astype(F32)]):
+            xp_ref[40 + i : 41 + i, 0:NV] = field[NU - 1 : NU, :]
+            xm_ref[40 + 2 * i : 42 + 2 * i, 0:NV] = field[0:2, :]
         for axis in range(3):
             turned = m_ref[axis].T
             high = turned.astype(BF16)
@@ -245,7 +250,8 @@
     @pl.when(step >= 1)
     def _():
         here = pl.ds(pl.multiple_of((step - 1) * RB, RB), RB)
-        w_t = w_ref[...].T
+        fetch_w(step - 1).wait()
+        w_t = w_ref[here, :].T
         in_block = hot(NB, blk_ref[...])
         picked = dot(mt_ref[...], jnp.concatenate([in_block, in_block], axis=0))
         values = [
@@ -292,8 +298,8 @@
         load_kernel,
         grid=(1 + RSTEPS,),
         in_specs=[
-            pl.BlockSpec(memory_space=pl.ANY),
-            pl.BlockSpec((RB, NK), lambda i: (record(i), 0)),
+            pl.BlockSpec(memory_space=pltpu.HBM),
+            pl.BlockSpec(memory_space=pltpu.HBM),
             row_spec,
             all_rows,
             all_rows,
@@ -324,6 +330,8 @@
         scratch_shapes=[
             pltpu.VMEM((19, NB, NK), F32),
             pltpu.SemaphoreType.DMA((CHUNKS,)),
+            pltpu.VMEM((R, NK), F32),
+            pltpu.SemaphoreType.DMA((RSTEPS,)),
             pltpu.VMEM((3, NB, NK), F32),
             pltpu.VMEM((3 * NK, 2 * NB), BF16),
             pltpu.VMEM((256, 512), BF16),
@@ -383,8 +391,8 @@
 def collide_and_run(pops):
     return pl.pallas_call(
         collide_kernel,
-        in_specs=[pl.BlockSpec(memory_space=pl.ANY)],
-        out_specs=pl.BlockSpec(memory_space=pl.ANY),
+        in_specs=[pl.BlockSpec(memory_space=pltpu.HBM)],
+        out_specs=pl.BlockSpec(memory_space=pltpu.HBM),
         out_shape=jax.ShapeDtypeStruct((19, NB, NK), F32),
         scratch_shapes=[
             pltpu.VMEM((19, NB, NK), F32),
@@ -399,7 +407,7 @@
 
 def node_rows(recv_t):
     node = recv_t[3 * CAP : MAIN, :].astype(jnp.int32)
-    return node >> 7, node & 127
+    return node >> 8, node & 255
 
 
 def force_kernel(recv_ref, f_ref, rim_ref, u_ref, v_ref, hl_ref, ru_ref, rv_ref, rhl_ref):
@@ -416,32 +424,28 @@
     rhl_ref[3 * RIM : 6 * RIM, :] = low
 
     def chunk_of(rows_ref, cols_ref, vals_ref, slots, height, width):
-        u_of = iota((height, ND), 0)
-        v_of = iota((width, ND), 0)
-
         def chunk(i, acc):
             at = pl.multiple_of(i * 8, 8)
             u8 = rows_ref[pl.ds(at, 8), :]
             v8 = cols_ref[pl.ds(at, 8), :]
-            vals = [vals_ref[pl.ds(pl.multiple_of(part * slots + at, 8), 8), :] for part in range(6)]
+            vals = [vals_ref[pl.ds(pl.multiple_of(part * slots + at, 8), 8), :].astype(BF16) for part in range(6)]
             lhs, rhs = [], []
             for r in range(8):
-                here = u_of == u8[r : r + 1, :]
-                lhs.append(
-                    jnp.concatenate([jnp.where(here, vals[part][r : r + 1, :], 0.0) for part in range(6)], axis=0)
-                    .astype(BF16)
-                )
-                rhs.append(jnp.where(v_of == v8[r : r + 1, :], 1.0, 0.0).astype(BF16))
+                here = match(max(height, 16), u8[r : r + 1, :])
+                lhs.append(jnp.concatenate([pick(here, vals[part][r : r + 1, :]) for part in range(6)], axis=0))
+                rhs.append(hot(width, v8[r : r + 1, :]))
             return acc + dot_t(jnp.concatenate(lhs, axis=1), jnp.concatenate(rhs, axis=1))
 
-        return lax.fori_loop(0, slots // 8, chunk, jnp.zeros((6 * height, width), F32))
-
-    acc = chunk_of(u_ref, v_ref, hl_ref, CAP, NU, NV)
+        return lax.fori_loop(0, slots // 8, chunk, jnp.zeros((6 * max(height, 16), width), F32), unroll=2)
+
+    acc = chunk_of(u_ref, v_ref, hl_ref, CAP, NU // 2, 2 * NV)
     for c in range(3):
-        f_ref[c] = acc[c * NU : (c + 1) * NU, :] + acc[(3 + c) * NU : (4 + c) * NU, :]
+        pair = acc[c * 32 : (c + 1) * 32, :] + acc[(3 + c) * 32 : (4 + c) * 32, :]
+        f_ref[c, pl.ds(0, 32, stride=2), :] = pair[:, 0:NV]
+        f_ref[c, pl.ds(1, 32, stride=2), :] = pair[:, NV : 2 * NV]
     acc = chunk_of(ru_ref, rv_ref, rhl_ref, RIM, 8, EV)
     for c in range(3):
-        rim_ref[c] = acc[c * 8 : (c + 1) * 8, :] + acc[(3 + c) * 8 : (4 + c) * 8, :]
+        rim_ref[c] = acc[c * 16 : c * 16 + 8, :] + acc[(3 + c) * 16 : (3 + c) * 16 + 8, :]
 
 
 def force_of(recv):
@@ -493,7 +497,7 @@
     return pl.pallas_call(
         side_kernel,
         out_shape=[jax.ShapeDtypeStruct((YMSG, NK), F32), jax.ShapeDtypeStruct((YMSG, NK), F32)],
-        compiler_params=pltpu.CompilerParams(vmem_limit_bytes=SMALL_LIMIT),
+        compiler_params=pltpu.CompilerParams(vmem_limit_bytes=VMEM_LIMIT),
         name="sides",
     )(mass, modulus, live, xp, xm, yp, ym)
 
@@ -609,34 +613,34 @@
     moments = jnp.where(lane == 4, over, moments)
 
     for c in range(3):
-        for part, field in ((c, f_ref[c]), (3 + c, y_ref[c])):
-            high = field.astype(BF16)
-            fy_ref[part * NU : (part + 1) * NU, 0:NV] = high
-            fy_ref[part * NU : (part + 1) * NU, NV : 2 * NV] = (field - high.astype(F32)).astype(BF16)
+        for part, field in ((c, f_ref), (3 + c, y_ref)):
+            rows = slice(part * 32, part * 32 + 32)
+            for odd in range(2):
+                value = field[c, pl.ds(odd, 32, stride=2), :]
+                high = value.astype(BF16)
+                fy_ref[rows, odd * NV : (odd + 1) * NV] = high
+                fy_ref[rows, (2 + odd) * NV : (3 + odd) * NV] = (value - high.astype(F32)).astype(BF16)
     u_ref[...], v_ref[...] = node_rows(recv_ref[:, 0, 0:MAIN].T)
-    u_of = iota((NU, ND), 0)
-    v_of = iota((NV, ND), 0)
+    u_of = iota((NU // 2, ND), 0)
 
     def chunk(i, _):
         at = pl.multiple_of(i * 8, 8)
         u8 = u_ref[pl.ds(at, 8), :]
         v8 = v_ref[pl.ds(at, 8), :]
-        rhs = jnp.concatenate(
-            [jnp.where(v_of == v8[r : r + 1, :], 1.0, 0.0).astype(BF16) for r in range(8)], axis=1
-        )
+        rhs = jnp.concatenate([hot(2 * NV, v8[r : r + 1, :]) for r in range(8)], axis=1)
         picked = dot(fy_ref[...], jnp.concatenate([rhs, rhs], axis=0))
         tiles = [jnp.zeros((8, ND), F32) for _ in range(6)]
         for r in range(8):
             here = u_of == u8[r : r + 1, :]
             for part in range(6):
-                block = picked[part * NU : (part + 1) * NU, r * ND : (r + 1) * ND]
+                block = picked[part * 32 : (part + 1) * 32, r * ND : (r + 1) * ND]
                 row = jnp.sum(jnp.where(here, block, 0.0), axis=0, keepdims=True)
                 tiles[part] = jnp.where(sub == r, row, tiles[part])
         for part in range(6):
             rt_ref[pl.ds(pl.multiple_of(part * CAP + at, 8), 8), :] = tiles[part]
         return 0
 
-    lax.fori_loop(0, CAP // 8, chunk, 0)
+    lax.fori_loop(0, CAP // 8, chunk, 0, unroll=2)
     ret_ref[:, 0, 0 : 6 * CAP] = rt_ref[...].T
     ret_ref[:, 0, 6 * CAP : 8 * CAP] = jnp.broadcast_to(moments, (ND, 128))
 
@@ -661,7 +665,7 @@
             pltpu.VMEM((12, EU, EV), F32),
             pltpu.VMEM((12, EU, EV), F32),
             pltpu.VMEM((3, EU, EV), F32),
-            pltpu.VMEM((6 * NU, 2 * NV), BF16),
+            pltpu.VMEM((6 * NU // 2, 4 * NV), BF16),
             pltpu.VMEM((CAP, ND), jnp.int32),
             pltpu.VMEM((CAP, ND), jnp.int32),
             pltpu.VMEM((6 * CAP, ND), F32),
@@ -704,6 +708,7 @@
         in_specs=[pl.BlockSpec((ND, 1, 128), lambda i: (0, 0, 3))],
         out_specs=[smem, smem],
         out_shape=[jax.ShapeDtypeStruct((2,), F32), jax.ShapeDtypeStruct((1,), jnp.int32)],
+        compiler_params=pltpu.CompilerParams(vmem_limit_bytes=VMEM_LIMIT),
         name="scalars",
     )(back)
 
@@ -815,7 +820,7 @@
             row_spec,
             patch,
             patch,
-            pl.BlockSpec(memory_space=pl.ANY),
+            pl.BlockSpec(memory_space=pltpu.HBM),
             x_face,
             x_face,
             y_face,

time: 78.2 us -> 76.7 us (0.981)
  local copies, waits for them, and re-layouts: 2.55 us -> 0.04 us
  starting transfers between devices: 19.9 us -> 21.1 us
    unnamed x12 -> x8, local copies, waits for them, and re-layouts: 1.84 us -> 0.02 us
    pallas_call x1, Pallas kernels: 0.12 us -> 1.84 us  [sides_of(): pl.pallas_call(side_kernel, out_shape=[jax.ShapeDtypeStruct((YMSG, NK), F...]
    all_to_all x2, starting transfers between devices: 14.5 us -> 15.7 us  [exchange(): return lax.all_to_all(x, ALL, 0, 0, tiled=True)]
    pallas_call x1, Pallas kernels: 4.35 us -> 3.09 us  [force_of(): pl.pallas_call(force_kernel, out_shape=[jax.ShapeDtypeStruct((3, NU, NV),...]
  transfers between devices with their start and end apart: 6 -> 6, of which waited for: 2 -> 2; matrix products, arithmetic and copies ran while one was open for 0% -> 0% of each run, Pallas kernels for 12% -> 13%
where the time goes in v6:
time: 76.7 us; the launch traced here: 76.4 us
  Pallas kernels  40.6 us (53%)
  starting transfers between devices  21.1 us (28%)
  waiting for transfers between devices  12.8 us (17%)
  between operations  1.61 us (2%)
    all_to_all x2, starting transfers between devices, exchange(): return lax.all_to_all(x, ALL, 0, 0, tiled=True)  15.7 us
    pallas_call x1, Pallas kernels, loads_to_send(): pl.pallas_call(load_kernel, grid=(1 + RSTEPS,), in_specs=[pl.BlockSpec(me...  13.8 us
    all_to_all x2, waiting for transfers between devices, exchange(): return lax.all_to_all(x, ALL, 0, 0, tiled=True)  12.8 us
    pallas_call x1, Pallas kernels, outputs_of(): pl.pallas_call(next_kernel, grid=(OREC + OSTEPS,), in_specs=[pl.BlockSpec...  9.52 us
    pallas_call x1, Pallas kernels, shell_of(): pl.pallas_call(shell_kernel, grid=(1,), in_specs=[pl.BlockSpec(memory_spa...  6.3 us
    ppermute x4, starting transfers between devices, pass_on(): lax.ppermute(x, axis, [(i, (i + shift) % count) for i in range(count)])  5.35 us
    pallas_call x1, Pallas kernels, collide_and_run(): pl.pallas_call(collide_kernel, in_specs=[pl.BlockSpec(memory_space=pltpu....  5.25 us
    pallas_call x1, Pallas kernels, force_of(): pl.pallas_call(force_kernel, out_shape=[jax.ShapeDtypeStruct((3, NU, NV),...  3.09 us
  transfers between devices with their start and end apart: 6, of which 2 were waited for; matrix products, arithmetic and copies ran while one was open for 0% of the time, Pallas kernels for 13%

profile of v6, /device:TPU:1, one launch (start us, length us, event | category | flops | bytes accessed | tf_op | source)
XLA Modules:
  0.0 76.4 jit_solution(334221457842985084)
XLA Ops:
  0.6 0.0 copy-start
  0.6 0.0 copy-start.3
  0.7 0.0 copy-start.6
  0.7 13.8 %loads.1 = (f32[128,1,384]{2,1,0:T(1,128)}, s32[1,4096]{1,0:T(1,128)}, f32[256,4096]{1,0:T(8,128)}, f32[48,256]{1,0:T(8,128)}, f32[48,256]{1,0:T(8,128)}, /*index=5*/f32[160,256]{1,0:T(8,128)}, f32[160,256]{1,0:T(8,128)}) custom-call(f32[19,256,256]{2,1,0:T(8,128)} %bitcast.50, f32[4096,256]{1,0:T(8,128)} %w_hbm.1, s32[1,4096]{1,0:T(1,128)} %bitcast.62, ...), custom_call_target="tpu_custom_call" | custom-call | tf_op jit(solution)/shard_map/loads/pallas_call | solution.py:297
  14.4 0.0 copy-start.7
  14.5 2.2 %collective-permute-start.12 = (f32[48,256]{1,0:T(8,128)}, f32[48,256]{1,0:T(8,128)S(1)}, u32[]{:S(2)}, u32[]{:S(2)}) collective-permute-start(f32[48,256]{1,0:T(8,128)} %get-tuple-element.67), channel_id=1, source_target_pairs={{0,32},{32,64},{64,96},{96,0},{1,33},{33,65},{65,97},{97,1},{2,34}... | collective-permute-start | bytes 147464 | tf_op jit(solution)/shard_map/ppermute | solution.py:848
  16.6 1.5 %collective-permute-start.13 = (f32[48,256]{1,0:T(8,128)}, f32[48,256]{1,0:T(8,128)S(1)}, u32[]{:S(2)}, u32[]{:S(2)}) collective-permute-start(f32[48,256]{1,0:T(8,128)} %get-tuple-element.68), channel_id=1, source_target_pairs={{0,96},{32,0},{64,32},{96,64},{1,97},{33,1},{65,33},{97,65},{2,98}... | collective-permute-start | bytes 147464 | tf_op jit(solution)/shard_map/ppermute | solution.py:848
  18.2 9.9 %all-to-all-start.1 = ((f32[128,1,384]{2,1,0:T(1,128)}), f32[128,1,384]{2,1,0:T(1,128)S(1)}, u32[]{:S(2)}, u32[]{:S(2)}) async-start(f32[128,1,384]{2,1,0:T(1,128)} %get-tuple-element.64), calls=%async_computation.1 | async-start | bytes 393216 | tf_op jit(solution)/shard_map/all_to_all | solution.py:899
  28.1 0.0 collective-permute-done.12.xp_ref.ulow_ref
  28.1 0.0 collective-permute-done.13.xm_ref.uhigh_ref
  28.1 0.0 copy-done
  28.1 0.0 copy-done.3
  28.1 0.0 copy-done.6
  28.1 1.8 %sides.1 = (f32[168,256]{1,0:T(8,128)}, f32[168,256]{1,0:T(8,128)}) custom-call(f32[64,128]{1,0:T(8,128)S(1)} %copy-done.3, f32[64,128]{1,0:T(8,128)S(1)} %copy-done, s32[64,128]{1,0:T(8,128)S(1)} %copy-done.6, f32[48,256]{1,0:T(8,128)S(1)} %collective-permute-done.12.xp_ref.ulow_ref, f32[48,256]{1,0:T(8,128)S(1)} %collective-permute-done.13.xm_ref.uhigh_ref, ...), custom_call_target="tpu_custom_call" | custom-call | tf_op jit(solution)/shard_map/sides/pallas_call | solution.py:497
  29.9 1.6 %collective-permute-start.14 = (f32[168,256]{1,0:T(8,128)}, f32[168,256]{1,0:T(8,128)S(1)}, u32[]{:S(2)}, u32[]{:S(2)}) collective-permute-start(f32[168,256]{1,0:T(8,128)} %get-tuple-element.71), channel_id=1, source_target_pairs={{0,1},{1,2},{2,3},{3,4},{4,5},{5,6},{6,7},{7,8},{8,9},{9,10},{10,1... | collective-permute-start | bytes 516104 | tf_op jit(solution)/shard_map/ppermute | solution.py:848
  31.6 0.0 collective-permute-start.15
  31.6 7.1 %all-to-all-done.1.recv_ref = f32[128,1,384]{2,1,0:T(1,128)S(1)} async-done(((f32[128,1,384]{2,1,0:T(1,128)}), f32[128,1,384]{2,1,0:T(1,128)S(1)}, u32[]{:S(2)}, u32[]{:S(2)}) %all-to-all-start.1) | async-done | bytes 196640 | tf_op jit(solution)/shard_map/all_to_all | solution.py:899
  38.7 3.1 %force.1 = (f32[3,64,128]{2,1,0:T(8,128)S(1)}, f32[3,8,256]{2,1,0:T(8,128)S(1)}) custom-call(f32[128,1,384]{2,1,0:T(1,128)S(1)} %all-to-all-done.1.recv_ref), custom_call_target="tpu_custom_call" | custom-call | tf_op jit(solution)/shard_map/force/pallas_call | solution.py:452
  41.8 0.0 collective-permute-done.14.vlow_ref.yp_ref
  41.8 0.0 collective-permute-done.15.vhigh_ref.ym_ref
  41.8 0.0 copy-done.7
  41.8 6.3 %shell.3 = (f32[3,64,128]{2,1,0:T(8,128)S(1)}, f32[128,1,512]{2,1,0:T(1,128)}) custom-call(f32[12,12]{1,0:T(8,128)S(1)} %copy-done.7, f32[3,64,128]{2,1,0:T(8,128)S(1)} %get-tuple-element.65.f_ref, f32[3,8,256]{2,1,0:T(8,128)S(1)} %get-tuple-element.66.rim_ref, f32[64,128]{1,0:T(8,128)S(1)} %copy-done.3, f32[64,128]{1,0:T(8,128)S(1)} %copy-done, ...), custom_call_target="tpu_custom_call" | custom-call | tf_op jit(solution)/shard_map/shell/pallas_call | solution.py:650
  48.1 5.9 %all-to-all-start.2 = ((f32[128,1,512]{2,1,0:T(1,128)}), f32[128,1,512]{2,1,0:T(1,128)S(1)}, u32[]{:S(2)}, u32[]{:S(2)}) async-start(f32[128,1,512]{2,1,0:T(1,128)} %get-tuple-element.74), calls=%async_computation.2 | async-start | bytes 524288 | tf_op jit(solution)/shard_map/all_to_all | solution.py:899
  54.0 5.2 %collide.1.read_ref = f32[19,256,256]{2,1,0:T(8,128)} custom-call(f32[19,256,256]{2,1,0:T(8,128)} %bitcast.51), custom_call_target="tpu_custom_call" | custom-call | tf_op jit(solution)/shard_map/collide/pallas_call | solution.py:392
  59.3 5.7 %all-to-all-done.2.part_ref = f32[128,1,512]{2,1,0:T(1,128)S(1)} async-done(((f32[128,1,512]{2,1,0:T(1,128)}), f32[128,1,512]{2,1,0:T(1,128)S(1)}, u32[]{:S(2)}, u32[]{:S(2)}) %all-to-all-start.2) | async-done | bytes 262176 | tf_op jit(solution)/shard_map/all_to_all | solution.py:899
  64.9 0.8 %scalars.1 = (f32[2]{0:T(128)S(1)}, s32[1]{0:T(128)}) custom-call(f32[128,1,512]{2,1,0:T(1,128)S(1)} %all-to-all-done.2.part_ref), custom_call_target="tpu_custom_call" | custom-call | tf_op jit(solution)/shard_map/scalars/pallas_call | solution.py:705
  66.4 0.3 conditional.1
  66.7 9.5 %outputs.1 = (f32[19,256,256]{2,1,0:T(8,128)}, f32[3,64,128]{2,1,0:T(8,128)}) custom-call(f32[2]{0:T(128)S(1)} %get-tuple-element.80.pq_ref, f32[128,1,512]{2,1,0:T(1,128)S(1)} %get-tuple-element.81.back_ref, f32[256,4096]{1,0:T(8,128)} %get-tuple-element.82.w_ref, s32[1,4096]{1,0:T(1,128)} %bitcast.63, s32[1,4096]{1,0:T(1,128)} %bitcast.59, ...), custom_call_target="tpu_custom_call" | custom-call | tf_op jit(solution)/shard_map/outputs/pallas_call | solution.py:811
  (1 shorter events, 0.0 us)
Async XLA Ops:
  0.6 27.4 %copy-start = (f32[64,128]{1,0:T(8,128)S(1)}, f32[64,128]{1,0:T(8,128)}, u32[]{:S(2)}) copy-start(f32[64,128]{1,0:T(8,128)} %mod_ref.5) | copy-start | bytes 98308
  0.6 27.4 %copy-start.3 = (f32[64,128]{1,0:T(8,128)S(1)}, f32[64,128]{1,0:T(8,128)}, u32[]{:S(2)}) copy-start(f32[64,128]{1,0:T(8,128)} %mass_ref.5) | copy-start | bytes 98308
  0.7 27.4 %copy-start.6 = (s32[64,128]{1,0:T(8,128)S(1)}, s32[64,128]{1,0:T(8,128)}, u32[]{:S(2)}) copy-start(s32[64,128]{1,0:T(8,128)} %live_ref.5) | copy-start | bytes 98308
  14.4 27.4 %copy-start.7 = (f32[12,12]{1,0:T(8,128)S(1)}, f32[12,12]{1,0:T(8,128)}, u32[]{:S(2)}) copy-start(f32[12,12]{1,0:T(8,128)} %stiff_ref.1) | copy-start | bytes 1732
  14.5 13.6 %collective-permute-start.12 = (f32[48,256]{1,0:T(8,128)}, f32[48,256]{1,0:T(8,128)S(1)}, u32[]{:S(2)}, u32[]{:S(2)}) collective-permute-start(f32[48,256]{1,0:T(8,128)} %get-tuple-element.67), channel_id=1, source_target_pairs={{0,32},{32,64},{64,96},{96,0},{1,33},{33,65},{65,97},{97,1},{2,34}... | collective-permute-start | bytes 147464 | tf_op jit(solution)/shard_map/ppermute | solution.py:848
  16.6 11.4 %collective-permute-start.13 = (f32[48,256]{1,0:T(8,128)}, f32[48,256]{1,0:T(8,128)S(1)}, u32[]{:S(2)}, u32[]{:S(2)}) collective-permute-start(f32[48,256]{1,0:T(8,128)} %get-tuple-element.68), channel_id=1, source_target_pairs={{0,96},{32,0},{64,32},{96,64},{1,97},{33,1},{65,33},{97,65},{2,98}... | collective-permute-start | bytes 147464 | tf_op jit(solution)/shard_map/ppermute | solution.py:848
  18.2 20.5 %all-to-all-start.1 = ((f32[128,1,384]{2,1,0:T(1,128)}), f32[128,1,384]{2,1,0:T(1,128)S(1)}, u32[]{:S(2)}, u32[]{:S(2)}) async-start(f32[128,1,384]{2,1,0:T(1,128)} %get-tuple-element.64), calls=%async_computation.1 | async-start | bytes 393216 | tf_op jit(solution)/shard_map/all_to_all | solution.py:899
  29.9 11.9 %collective-permute-start.14 = (f32[168,256]{1,0:T(8,128)}, f32[168,256]{1,0:T(8,128)S(1)}, u32[]{:S(2)}, u32[]{:S(2)}) collective-permute-start(f32[168,256]{1,0:T(8,128)} %get-tuple-element.71), channel_id=1, source_target_pairs={{0,1},{1,2},{2,3},{3,4},{4,5},{5,6},{6,7},{7,8},{8,9},{9,10},{10,1... | collective-permute-start | bytes 516104 | tf_op jit(solution)/shard_map/ppermute | solution.py:848
  31.6 10.2 %collective-permute-start.15 = (f32[168,256]{1,0:T(8,128)}, f32[168,256]{1,0:T(8,128)S(1)}, u32[]{:S(2)}, u32[]{:S(2)}) collective-permute-start(f32[168,256]{1,0:T(8,128)} %get-tuple-element.72), channel_id=1, source_target_pairs={{0,31},{1,0},{2,1},{3,2},{4,3},{5,4},{6,5},{7,6},{8,7},{9,8},{10,9... | collective-permute-start | bytes 516104 | tf_op jit(solution)/shard_map/ppermute | solution.py:848
  48.1 16.8 %all-to-all-start.2 = ((f32[128,1,512]{2,1,0:T(1,128)}), f32[128,1,512]{2,1,0:T(1,128)S(1)}, u32[]{:S(2)}, u32[]{:S(2)}) async-start(f32[128,1,512]{2,1,0:T(1,128)} %get-tuple-element.74), calls=%async_computation.2 | async-start | bytes 524288 | tf_op jit(solution)/shard_map/all_to_all | solution.py:899

commit v7 on v6

--- a/solution.py
+++ b/solution.py
@@ -436,7 +436,7 @@
                 rhs.append(hot(width, v8[r : r + 1, :]))
             return acc + dot_t(jnp.concatenate(lhs, axis=1), jnp.concatenate(rhs, axis=1))
 
-        return lax.fori_loop(0, slots // 8, chunk, jnp.zeros((6 * max(height, 16), width), F32), unroll=2)
+        return lax.fori_loop(0, slots // 8, chunk, jnp.zeros((6 * max(height, 16), width), F32), unroll=4)
 
     acc = chunk_of(u_ref, v_ref, hl_ref, CAP, NU // 2, 2 * NV)
     for c in range(3):
@@ -567,7 +567,7 @@
             g_ref[k, rows, :] = scale * total
         return 0
 
-    lax.fori_loop(0, EU // 8, cells, 0)
+    lax.fori_loop(0, EU // 8, cells, 0, unroll=3)
     mass = e_ref[3]
     for c in range(3):
         spread = g_ref[c] + down(g_ref[3 + c])
@@ -603,7 +603,7 @@
         return tuple(s + m for s, m in zip(sums, (m0, m1, m2, m3)))
 
     zero = jnp.zeros((8, NV), F32)
-    sums = lax.fori_loop(0, NU // 8, energy, (zero, zero, zero, zero))
+    sums = lax.fori_loop(0, NU // 8, energy, (zero, zero, zero, zero), unroll=2)
     lane = iota((1, 128), 1)
     moments = jnp.zeros((1, 128), F32)
     for i in range(4):
@@ -640,7 +640,7 @@
             rt_ref[pl.ds(pl.multiple_of(part * CAP + at, 8), 8), :] = tiles[part]
         return 0
 
-    lax.fori_loop(0, CAP // 8, chunk, 0, unroll=2)
+    lax.fori_loop(0, CAP // 8, chunk, 0, unroll=8)
     ret_ref[:, 0, 0 : 6 * CAP] = rt_ref[...].T
     ret_ref[:, 0, 6 * CAP : 8 * CAP] = jnp.broadcast_to(moments, (ND, 128))
 

time: 76.7 us -> 75.9 us (0.990)
  Pallas kernels: 40.6 us -> 39.4 us
where the time goes in v7:
time: 75.9 us; the launch traced here: 75.6 us
  Pallas kernels  39.4 us (52%)
  starting transfers between devices  21.6 us (28%)
  waiting for transfers between devices  12.8 us (17%)
  between operations  1.62 us (2%)
    all_to_all x2, starting transfers between devices, exchange(): return lax.all_to_all(x, ALL, 0, 0, tiled=True)  16.2 us
    pallas_call x1, Pallas kernels, loads_to_send(): pl.pallas_call(load_kernel, grid=(1 + RSTEPS,), in_specs=[pl.BlockSpec(me...  13.8 us
    all_to_all x2, waiting for transfers between devices, exchange(): return lax.all_to_all(x, ALL, 0, 0, tiled=True)  12.8 us
    pallas_call x1, Pallas kernels, outputs_of(): pl.pallas_call(next_kernel, grid=(OREC + OSTEPS,), in_specs=[pl.BlockSpec...  9.51 us
    pallas_call x1, Pallas kernels, shell_of(): pl.pallas_call(shell_kernel, grid=(1,), in_specs=[pl.BlockSpec(memory_spa...  5.55 us
    ppermute x4, starting transfers between devices, pass_on(): lax.ppermute(x, axis, [(i, (i + shift) % count) for i in range(count)])  5.35 us
    pallas_call x1, Pallas kernels, collide_and_run(): pl.pallas_call(collide_kernel, in_specs=[pl.BlockSpec(memory_space=pltpu....  5.25 us
    pallas_call x1, Pallas kernels, force_of(): pl.pallas_call(force_kernel, out_shape=[jax.ShapeDtypeStruct((3, NU, NV),...  2.62 us
  transfers between devices with their start and end apart: 6, of which 2 were waited for; matrix products, arithmetic and copies ran while one was open for 0% of the time, Pallas kernels for 13%

profile of v7, /device:TPU:1, one launch (start us, length us, event | category | flops | bytes accessed | tf_op | source)
XLA Modules:
  0.0 75.6 jit_solution(12914763183334315546)
XLA Ops:
  0.6 0.0 copy-start
  0.6 0.0 copy-start.3
  0.7 0.0 copy-start.6
  0.7 13.8 %loads.1 = (f32[128,1,384]{2,1,0:T(1,128)}, s32[1,4096]{1,0:T(1,128)}, f32[256,4096]{1,0:T(8,128)}, f32[48,256]{1,0:T(8,128)}, f32[48,256]{1,0:T(8,128)}, /*index=5*/f32[160,256]{1,0:T(8,128)}, f32[160,256]{1,0:T(8,128)}) custom-call(f32[19,256,256]{2,1,0:T(8,128)} %bitcast.50, f32[4096,256]{1,0:T(8,128)} %w_hbm.1, s32[1,4096]{1,0:T(1,128)} %bitcast.62, ...), custom_call_target="tpu_custom_call" | custom-call | tf_op jit(solution)/shard_map/loads/pallas_call | solution.py:297
  14.4 0.0 copy-start.7
  14.5 2.2 %collective-permute-start.12 = (f32[48,256]{1,0:T(8,128)}, f32[48,256]{1,0:T(8,128)S(1)}, u32[]{:S(2)}, u32[]{:S(2)}) collective-permute-start(f32[48,256]{1,0:T(8,128)} %get-tuple-element.67), channel_id=1, source_target_pairs={{0,32},{32,64},{64,96},{96,0},{1,33},{33,65},{65,97},{97,1},{2,34}... | collective-permute-start | bytes 147464 | tf_op jit(solution)/shard_map/ppermute | solution.py:848
  16.6 1.5 %collective-permute-start.13 = (f32[48,256]{1,0:T(8,128)}, f32[48,256]{1,0:T(8,128)S(1)}, u32[]{:S(2)}, u32[]{:S(2)}) collective-permute-start(f32[48,256]{1,0:T(8,128)} %get-tuple-element.68), channel_id=1, source_target_pairs={{0,96},{32,0},{64,32},{96,64},{1,97},{33,1},{65,33},{97,65},{2,98}... | collective-permute-start | bytes 147464 | tf_op jit(solution)/shard_map/ppermute | solution.py:848
  18.2 9.9 %all-to-all-start.1 = ((f32[128,1,384]{2,1,0:T(1,128)}), f32[128,1,384]{2,1,0:T(1,128)S(1)}, u32[]{:S(2)}, u32[]{:S(2)}) async-start(f32[128,1,384]{2,1,0:T(1,128)} %get-tuple-element.64), calls=%async_computation.1 | async-start | bytes 393216 | tf_op jit(solution)/shard_map/all_to_all | solution.py:899
  28.1 0.0 collective-permute-done.12.xp_ref.ulow_ref
  28.1 0.0 collective-permute-done.13.xm_ref.uhigh_ref
  28.1 0.0 copy-done
  28.1 0.0 copy-done.3
  28.1 0.0 copy-done.6
  28.1 1.8 %sides.1 = (f32[168,256]{1,0:T(8,128)}, f32[168,256]{1,0:T(8,128)}) custom-call(f32[64,128]{1,0:T(8,128)S(1)} %copy-done.3, f32[64,128]{1,0:T(8,128)S(1)} %copy-done, s32[64,128]{1,0:T(8,128)S(1)} %copy-done.6, f32[48,256]{1,0:T(8,128)S(1)} %collective-permute-done.12.xp_ref.ulow_ref, f32[48,256]{1,0:T(8,128)S(1)} %collective-permute-done.13.xm_ref.uhigh_ref, ...), custom_call_target="tpu_custom_call" | custom-call | tf_op jit(solution)/shard_map/sides/pallas_call | solution.py:497
  29.9 1.6 %collective-permute-start.14 = (f32[168,256]{1,0:T(8,128)}, f32[168,256]{1,0:T(8,128)S(1)}, u32[]{:S(2)}, u32[]{:S(2)}) collective-permute-start(f32[168,256]{1,0:T(8,128)} %get-tuple-element.71), channel_id=1, source_target_pairs={{0,1},{1,2},{2,3},{3,4},{4,5},{5,6},{6,7},{7,8},{8,9},{9,10},{10,1... | collective-permute-start | bytes 516104 | tf_op jit(solution)/shard_map/ppermute | solution.py:848
  31.6 0.0 collective-permute-start.15
  31.6 7.1 %all-to-all-done.1.recv_ref = f32[128,1,384]{2,1,0:T(1,128)S(1)} async-done(((f32[128,1,384]{2,1,0:T(1,128)}), f32[128,1,384]{2,1,0:T(1,128)S(1)}, u32[]{:S(2)}, u32[]{:S(2)}) %all-to-all-start.1) | async-done | bytes 196640 | tf_op jit(solution)/shard_map/all_to_all | solution.py:899
  38.7 2.6 %force.1 = (f32[3,64,128]{2,1,0:T(8,128)S(1)}, f32[3,8,256]{2,1,0:T(8,128)S(1)}) custom-call(f32[128,1,384]{2,1,0:T(1,128)S(1)} %all-to-all-done.1.recv_ref), custom_call_target="tpu_custom_call" | custom-call | tf_op jit(solution)/shard_map/force/pallas_call | solution.py:452
  41.3 0.0 collective-permute-done.14.vlow_ref.yp_ref
  41.3 0.0 collective-permute-done.15.vhigh_ref.ym_ref
  41.3 0.0 copy-done.7
  41.4 5.6 %shell.3 = (f32[3,64,128]{2,1,0:T(8,128)S(1)}, f32[128,1,512]{2,1,0:T(1,128)}) custom-call(f32[12,12]{1,0:T(8,128)S(1)} %copy-done.7, f32[3,64,128]{2,1,0:T(8,128)S(1)} %get-tuple-element.65.f_ref, f32[3,8,256]{2,1,0:T(8,128)S(1)} %get-tuple-element.66.rim_ref, f32[64,128]{1,0:T(8,128)S(1)} %copy-done.3, f32[64,128]{1,0:T(8,128)S(1)} %copy-done, ...), custom_call_target="tpu_custom_call" | custom-call | tf_op jit(solution)/shard_map/shell/pallas_call | solution.py:650
  46.9 6.3 %all-to-all-start.2 = ((f32[128,1,512]{2,1,0:T(1,128)}), f32[128,1,512]{2,1,0:T(1,128)S(1)}, u32[]{:S(2)}, u32[]{:S(2)}) async-start(f32[128,1,512]{2,1,0:T(1,128)} %get-tuple-element.74), calls=%async_computation.2 | async-start | bytes 524288 | tf_op jit(solution)/shard_map/all_to_all | solution.py:899
  53.2 5.2 %collide.1.read_ref = f32[19,256,256]{2,1,0:T(8,128)} custom-call(f32[19,256,256]{2,1,0:T(8,128)} %bitcast.51), custom_call_target="tpu_custom_call" | custom-call | tf_op jit(solution)/shard_map/collide/pallas_call | solution.py:392
  58.5 5.7 %all-to-all-done.2.part_ref = f32[128,1,512]{2,1,0:T(1,128)S(1)} async-done(((f32[128,1,512]{2,1,0:T(1,128)}), f32[128,1,512]{2,1,0:T(1,128)S(1)}, u32[]{:S(2)}, u32[]{:S(2)}) %all-to-all-start.2) | async-done | bytes 262176 | tf_op jit(solution)/shard_map/all_to_all | solution.py:899
  64.2 0.8 %scalars.1 = (f32[2]{0:T(128)S(1)}, s32[1]{0:T(128)}) custom-call(f32[128,1,512]{2,1,0:T(1,128)S(1)} %all-to-all-done.2.part_ref), custom_call_target="tpu_custom_call" | custom-call | tf_op jit(solution)/shard_map/scalars/pallas_call | solution.py:705
  65.7 0.3 conditional.1
  65.9 9.5 %outputs.1 = (f32[19,256,256]{2,1,0:T(8,128)}, f32[3,64,128]{2,1,0:T(8,128)}) custom-call(f32[2]{0:T(128)S(1)} %get-tuple-element.80.pq_ref, f32[128,1,512]{2,1,0:T(1,128)S(1)} %get-tuple-element.81.back_ref, f32[256,4096]{1,0:T(8,128)} %get-tuple-element.82.w_ref, s32[1,4096]{1,0:T(1,128)} %bitcast.63, s32[1,4096]{1,0:T(1,128)} %bitcast.59, ...), custom_call_target="tpu_custom_call" | custom-call | tf_op jit(solution)/shard_map/outputs/pallas_call | solution.py:811
  (1 shorter events, 0.0 us)
Async XLA Ops:
  0.6 27.4 %copy-start = (f32[64,128]{1,0:T(8,128)S(1)}, f32[64,128]{1,0:T(8,128)}, u32[]{:S(2)}) copy-start(f32[64,128]{1,0:T(8,128)} %mod_ref.5) | copy-start | bytes 98308
  0.6 27.4 %copy-start.3 = (f32[64,128]{1,0:T(8,128)S(1)}, f32[64,128]{1,0:T(8,128)}, u32[]{:S(2)}) copy-start(f32[64,128]{1,0:T(8,128)} %mass_ref.5) | copy-start | bytes 98308
  0.7 27.4 %copy-start.6 = (s32[64,128]{1,0:T(8,128)S(1)}, s32[64,128]{1,0:T(8,128)}, u32[]{:S(2)}) copy-start(s32[64,128]{1,0:T(8,128)} %live_ref.5) | copy-start | bytes 98308
  14.4 26.9 %copy-start.7 = (f32[12,12]{1,0:T(8,128)S(1)}, f32[12,12]{1,0:T(8,128)}, u32[]{:S(2)}) copy-start(f32[12,12]{1,0:T(8,128)} %stiff_ref.1) | copy-start | bytes 1732
  14.5 13.6 %collective-permute-start.12 = (f32[48,256]{1,0:T(8,128)}, f32[48,256]{1,0:T(8,128)S(1)}, u32[]{:S(2)}, u32[]{:S(2)}) collective-permute-start(f32[48,256]{1,0:T(8,128)} %get-tuple-element.67), channel_id=1, source_target_pairs={{0,32},{32,64},{64,96},{96,0},{1,33},{33,65},{65,97},{97,1},{2,34}... | collective-permute-start | bytes 147464 | tf_op jit(solution)/shard_map/ppermute | solution.py:848
  16.6 11.4 %collective-permute-start.13 = (f32[48,256]{1,0:T(8,128)}, f32[48,256]{1,0:T(8,128)S(1)}, u32[]{:S(2)}, u32[]{:S(2)}) collective-permute-start(f32[48,256]{1,0:T(8,128)} %get-tuple-element.68), channel_id=1, source_target_pairs={{0,96},{32,0},{64,32},{96,64},{1,97},{33,1},{65,33},{97,65},{2,98}... | collective-permute-start | bytes 147464 | tf_op jit(solution)/shard_map/ppermute | solution.py:848
  18.2 20.5 %all-to-all-start.1 = ((f32[128,1,384]{2,1,0:T(1,128)}), f32[128,1,384]{2,1,0:T(1,128)S(1)}, u32[]{:S(2)}, u32[]{:S(2)}) async-start(f32[128,1,384]{2,1,0:T(1,128)} %get-tuple-element.64), calls=%async_computation.1 | async-start | bytes 393216 | tf_op jit(solution)/shard_map/all_to_all | solution.py:899
  29.9 11.4 %collective-permute-start.14 = (f32[168,256]{1,0:T(8,128)}, f32[168,256]{1,0:T(8,128)S(1)}, u32[]{:S(2)}, u32[]{:S(2)}) collective-permute-start(f32[168,256]{1,0:T(8,128)} %get-tuple-element.71), channel_id=1, source_target_pairs={{0,1},{1,2},{2,3},{3,4},{4,5},{5,6},{6,7},{7,8},{8,9},{9,10},{10,1... | collective-permute-start | bytes 516104 | tf_op jit(solution)/shard_map/ppermute | solution.py:848
  31.6 9.8 %collective-permute-start.15 = (f32[168,256]{1,0:T(8,128)}, f32[168,256]{1,0:T(8,128)S(1)}, u32[]{:S(2)}, u32[]{:S(2)}) collective-permute-start(f32[168,256]{1,0:T(8,128)} %get-tuple-element.72), channel_id=1, source_target_pairs={{0,31},{1,0},{2,1},{3,2},{4,3},{5,4},{6,5},{7,6},{8,7},{9,8},{10,9... | collective-permute-start | bytes 516104 | tf_op jit(solution)/shard_map/ppermute | solution.py:848
  46.9 17.3 %all-to-all-start.2 = ((f32[128,1,512]{2,1,0:T(1,128)}), f32[128,1,512]{2,1,0:T(1,128)S(1)}, u32[]{:S(2)}, u32[]{:S(2)}) async-start(f32[128,1,512]{2,1,0:T(1,128)} %get-tuple-element.74), calls=%async_computation.2 | async-start | bytes 524288 | tf_op jit(solution)/shard_map/all_to_all | solution.py:899

commit v8 on v7

--- a/solution.py
+++ b/solution.py
@@ -215,7 +215,7 @@
         for part in range(CHUNKS):
             fetch(part).wait()
             fetch_w(part).start()
-            lax.fori_loop(part * CROWS // 8, (part + 1) * CROWS // 8, rows_of, 0, unroll=2)
+            lax.fori_loop(part * CROWS // 8, (part + 1) * CROWS // 8, rows_of, 0, unroll=4)
             for face_ref, dirs, y in ((yp_ref, YP, 7), (ym_ref, YM, 0)):
                 pops = []
                 for q in range(19):
@@ -715,7 +715,7 @@
 
 OB = 2048
 OREC = R // OB
-XS = 8
+XS = 16
 OSTEPS = 32 // XS
 
 

time: 75.9 us -> 75.6 us (level)
  no operation moved by 1% of the time
where the time goes in v8:
time: 75.6 us; the launch traced here: 75.3 us
  Pallas kernels  39.1 us (52%)
  starting transfers between devices  21.6 us (29%)
  waiting for transfers between devices  12.8 us (17%)
  between operations  1.62 us (2%)
    all_to_all x2, starting transfers between devices, exchange(): return lax.all_to_all(x, ALL, 0, 0, tiled=True)  16.2 us
    pallas_call x1, Pallas kernels, loads_to_send(): pl.pallas_call(load_kernel, grid=(1 + RSTEPS,), in_specs=[pl.BlockSpec(me...  13.7 us
    all_to_all x2, waiting for transfers between devices, exchange(): return lax.all_to_all(x, ALL, 0, 0, tiled=True)  12.8 us
    pallas_call x1, Pallas kernels, outputs_of(): pl.pallas_call(next_kernel, grid=(OREC + OSTEPS,), in_specs=[pl.BlockSpec...  9.25 us
    pallas_call x1, Pallas kernels, shell_of(): pl.pallas_call(shell_kernel, grid=(1,), in_specs=[pl.BlockSpec(memory_spa...  5.55 us
    ppermute x4, starting transfers between devices, pass_on(): lax.ppermute(x, axis, [(i, (i + shift) % count) for i in range(count)])  5.35 us
    pallas_call x1, Pallas kernels, collide_and_run(): pl.pallas_call(collide_kernel, in_specs=[pl.BlockSpec(memory_space=pltpu....  5.25 us
    pallas_call x1, Pallas kernels, force_of(): pl.pallas_call(force_kernel, out_shape=[jax.ShapeDtypeStruct((3, NU, NV),...  2.63 us
  transfers between devices with their start and end apart: 6, of which 2 were waited for; matrix products, arithmetic and copies ran while one was open for 0% of the time, Pallas kernels for 13%

profile of v8, /device:TPU:1, one launch (start us, length us, event | category | flops | bytes accessed | tf_op | source)
XLA Modules:
  0.0 75.3 jit_solution(799338951857889372)
XLA Ops:
  0.6 0.0 copy-start
  0.6 0.0 copy-start.3
  0.7 0.0 copy-start.6
  0.7 13.7 %loads.1 = (f32[128,1,384]{2,1,0:T(1,128)}, s32[1,4096]{1,0:T(1,128)}, f32[256,4096]{1,0:T(8,128)}, f32[48,256]{1,0:T(8,128)}, f32[48,256]{1,0:T(8,128)}, /*index=5*/f32[160,256]{1,0:T(8,128)}, f32[160,256]{1,0:T(8,128)}) custom-call(f32[19,256,256]{2,1,0:T(8,128)} %bitcast.50, f32[4096,256]{1,0:T(8,128)} %w_hbm.1, s32[1,4096]{1,0:T(1,128)} %bitcast.62, ...), custom_call_target="tpu_custom_call" | custom-call | tf_op jit(solution)/shard_map/loads/pallas_call | solution.py:297
  14.4 0.0 copy-start.7
  14.4 2.2 %collective-permute-start.12 = (f32[48,256]{1,0:T(8,128)}, f32[48,256]{1,0:T(8,128)S(1)}, u32[]{:S(2)}, u32[]{:S(2)}) collective-permute-start(f32[48,256]{1,0:T(8,128)} %get-tuple-element.67), channel_id=1, source_target_pairs={{0,32},{32,64},{64,96},{96,0},{1,33},{33,65},{65,97},{97,1},{2,34}... | collective-permute-start | bytes 147464 | tf_op jit(solution)/shard_map/ppermute | solution.py:848
  16.6 1.5 %collective-permute-start.13 = (f32[48,256]{1,0:T(8,128)}, f32[48,256]{1,0:T(8,128)S(1)}, u32[]{:S(2)}, u32[]{:S(2)}) collective-permute-start(f32[48,256]{1,0:T(8,128)} %get-tuple-element.68), channel_id=1, source_target_pairs={{0,96},{32,0},{64,32},{96,64},{1,97},{33,1},{65,33},{97,65},{2,98}... | collective-permute-start | bytes 147464 | tf_op jit(solution)/shard_map/ppermute | solution.py:848
  18.1 9.9 %all-to-all-start.1 = ((f32[128,1,384]{2,1,0:T(1,128)}), f32[128,1,384]{2,1,0:T(1,128)S(1)}, u32[]{:S(2)}, u32[]{:S(2)}) async-start(f32[128,1,384]{2,1,0:T(1,128)} %get-tuple-element.64), calls=%async_computation.1 | async-start | bytes 393216 | tf_op jit(solution)/shard_map/all_to_all | solution.py:899
  28.0 0.0 collective-permute-done.12.xp_ref.ulow_ref
  28.0 0.0 collective-permute-done.13.xm_ref.uhigh_ref
  28.0 0.0 copy-done
  28.0 0.0 copy-done.3
  28.0 0.0 copy-done.6
  28.0 1.8 %sides.1 = (f32[168,256]{1,0:T(8,128)}, f32[168,256]{1,0:T(8,128)}) custom-call(f32[64,128]{1,0:T(8,128)S(1)} %copy-done.3, f32[64,128]{1,0:T(8,128)S(1)} %copy-done, s32[64,128]{1,0:T(8,128)S(1)} %copy-done.6, f32[48,256]{1,0:T(8,128)S(1)} %collective-permute-done.12.xp_ref.ulow_ref, f32[48,256]{1,0:T(8,128)S(1)} %collective-permute-done.13.xm_ref.uhigh_ref, ...), custom_call_target="tpu_custom_call" | custom-call | tf_op jit(solution)/shard_map/sides/pallas_call | solution.py:497
  29.9 1.6 %collective-permute-start.14 = (f32[168,256]{1,0:T(8,128)}, f32[168,256]{1,0:T(8,128)S(1)}, u32[]{:S(2)}, u32[]{:S(2)}) collective-permute-start(f32[168,256]{1,0:T(8,128)} %get-tuple-element.71), channel_id=1, source_target_pairs={{0,1},{1,2},{2,3},{3,4},{4,5},{5,6},{6,7},{7,8},{8,9},{9,10},{10,1... | collective-permute-start | bytes 516104 | tf_op jit(solution)/shard_map/ppermute | solution.py:848
  31.5 0.0 collective-permute-start.15
  31.5 7.1 %all-to-all-done.1.recv_ref = f32[128,1,384]{2,1,0:T(1,128)S(1)} async-done(((f32[128,1,384]{2,1,0:T(1,128)}), f32[128,1,384]{2,1,0:T(1,128)S(1)}, u32[]{:S(2)}, u32[]{:S(2)}) %all-to-all-start.1) | async-done | bytes 196640 | tf_op jit(solution)/shard_map/all_to_all | solution.py:899
  38.6 2.6 %force.1 = (f32[3,64,128]{2,1,0:T(8,128)S(1)}, f32[3,8,256]{2,1,0:T(8,128)S(1)}) custom-call(f32[128,1,384]{2,1,0:T(1,128)S(1)} %all-to-all-done.1.recv_ref), custom_call_target="tpu_custom_call" | custom-call | tf_op jit(solution)/shard_map/force/pallas_call | solution.py:452
  41.3 0.0 collective-permute-done.14.vlow_ref.yp_ref
  41.3 0.0 collective-permute-done.15.vhigh_ref.ym_ref
  41.3 0.0 copy-done.7
  41.3 5.6 %shell.3 = (f32[3,64,128]{2,1,0:T(8,128)S(1)}, f32[128,1,512]{2,1,0:T(1,128)}) custom-call(f32[12,12]{1,0:T(8,128)S(1)} %copy-done.7, f32[3,64,128]{2,1,0:T(8,128)S(1)} %get-tuple-element.65.f_ref, f32[3,8,256]{2,1,0:T(8,128)S(1)} %get-tuple-element.66.rim_ref, f32[64,128]{1,0:T(8,128)S(1)} %copy-done.3, f32[64,128]{1,0:T(8,128)S(1)} %copy-done, ...), custom_call_target="tpu_custom_call" | custom-call | tf_op jit(solution)/shard_map/shell/pallas_call | solution.py:650
  46.8 6.3 %all-to-all-start.2 = ((f32[128,1,512]{2,1,0:T(1,128)}), f32[128,1,512]{2,1,0:T(1,128)S(1)}, u32[]{:S(2)}, u32[]{:S(2)}) async-start(f32[128,1,512]{2,1,0:T(1,128)} %get-tuple-element.74), calls=%async_computation.2 | async-start | bytes 524288 | tf_op jit(solution)/shard_map/all_to_all | solution.py:899
  53.2 5.2 %collide.1.read_ref = f32[19,256,256]{2,1,0:T(8,128)} custom-call(f32[19,256,256]{2,1,0:T(8,128)} %bitcast.51), custom_call_target="tpu_custom_call" | custom-call | tf_op jit(solution)/shard_map/collide/pallas_call | solution.py:392
  58.4 5.7 %all-to-all-done.2.part_ref = f32[128,1,512]{2,1,0:T(1,128)S(1)} async-done(((f32[128,1,512]{2,1,0:T(1,128)}), f32[128,1,512]{2,1,0:T(1,128)S(1)}, u32[]{:S(2)}, u32[]{:S(2)}) %all-to-all-start.2) | async-done | bytes 262176 | tf_op jit(solution)/shard_map/all_to_all | solution.py:899
  64.1 0.8 %scalars.1 = (f32[2]{0:T(128)S(1)}, s32[1]{0:T(128)}) custom-call(f32[128,1,512]{2,1,0:T(1,128)S(1)} %all-to-all-done.2.part_ref), custom_call_target="tpu_custom_call" | custom-call | tf_op jit(solution)/shard_map/scalars/pallas_call | solution.py:705
  65.6 0.3 conditional.1
  65.9 9.3 %outputs.1 = (f32[19,256,256]{2,1,0:T(8,128)}, f32[3,64,128]{2,1,0:T(8,128)}) custom-call(f32[2]{0:T(128)S(1)} %get-tuple-element.80.pq_ref, f32[128,1,512]{2,1,0:T(1,128)S(1)} %get-tuple-element.81.back_ref, f32[256,4096]{1,0:T(8,128)} %get-tuple-element.82.w_ref, s32[1,4096]{1,0:T(1,128)} %bitcast.63, s32[1,4096]{1,0:T(1,128)} %bitcast.59, ...), custom_call_target="tpu_custom_call" | custom-call | tf_op jit(solution)/shard_map/outputs/pallas_call | solution.py:811
  (1 shorter events, 0.0 us)
Async XLA Ops:
  0.6 27.4 %copy-start = (f32[64,128]{1,0:T(8,128)S(1)}, f32[64,128]{1,0:T(8,128)}, u32[]{:S(2)}) copy-start(f32[64,128]{1,0:T(8,128)} %mod_ref.5) | copy-start | bytes 98308
  0.6 27.4 %copy-start.3 = (f32[64,128]{1,0:T(8,128)S(1)}, f32[64,128]{1,0:T(8,128)}, u32[]{:S(2)}) copy-start(f32[64,128]{1,0:T(8,128)} %mass_ref.5) | copy-start | bytes 98308
  0.7 27.4 %copy-start.6 = (s32[64,128]{1,0:T(8,128)S(1)}, s32[64,128]{1,0:T(8,128)}, u32[]{:S(2)}) copy-start(s32[64,128]{1,0:T(8,128)} %live_ref.5) | copy-start | bytes 98308
  14.4 26.9 %copy-start.7 = (f32[12,12]{1,0:T(8,128)S(1)}, f32[12,12]{1,0:T(8,128)}, u32[]{:S(2)}) copy-start(f32[12,12]{1,0:T(8,128)} %stiff_ref.1) | copy-start | bytes 1732
  14.4 13.6 %collective-permute-start.12 = (f32[48,256]{1,0:T(8,128)}, f32[48,256]{1,0:T(8,128)S(1)}, u32[]{:S(2)}, u32[]{:S(2)}) collective-permute-start(f32[48,256]{1,0:T(8,128)} %get-tuple-element.67), channel_id=1, source_target_pairs={{0,32},{32,64},{64,96},{96,0},{1,33},{33,65},{65,97},{97,1},{2,34}... | collective-permute-start | bytes 147464 | tf_op jit(solution)/shard_map/ppermute | solution.py:848
  16.6 11.4 %collective-permute-start.13 = (f32[48,256]{1,0:T(8,128)}, f32[48,256]{1,0:T(8,128)S(1)}, u32[]{:S(2)}, u32[]{:S(2)}) collective-permute-start(f32[48,256]{1,0:T(8,128)} %get-tuple-element.68), channel_id=1, source_target_pairs={{0,96},{32,0},{64,32},{96,64},{1,97},{33,1},{65,33},{97,65},{2,98}... | collective-permute-start | bytes 147464 | tf_op jit(solution)/shard_map/ppermute | solution.py:848
  18.1 20.5 %all-to-all-start.1 = ((f32[128,1,384]{2,1,0:T(1,128)}), f32[128,1,384]{2,1,0:T(1,128)S(1)}, u32[]{:S(2)}, u32[]{:S(2)}) async-start(f32[128,1,384]{2,1,0:T(1,128)} %get-tuple-element.64), calls=%async_computation.1 | async-start | bytes 393216 | tf_op jit(solution)/shard_map/all_to_all | solution.py:899
  29.9 11.4 %collective-permute-start.14 = (f32[168,256]{1,0:T(8,128)}, f32[168,256]{1,0:T(8,128)S(1)}, u32[]{:S(2)}, u32[]{:S(2)}) collective-permute-start(f32[168,256]{1,0:T(8,128)} %get-tuple-element.71), channel_id=1, source_target_pairs={{0,1},{1,2},{2,3},{3,4},{4,5},{5,6},{6,7},{7,8},{8,9},{9,10},{10,1... | collective-permute-start | bytes 516104 | tf_op jit(solution)/shard_map/ppermute | solution.py:848
  31.5 9.8 %collective-permute-start.15 = (f32[168,256]{1,0:T(8,128)}, f32[168,256]{1,0:T(8,128)S(1)}, u32[]{:S(2)}, u32[]{:S(2)}) collective-permute-start(f32[168,256]{1,0:T(8,128)} %get-tuple-element.72), channel_id=1, source_target_pairs={{0,31},{1,0},{2,1},{3,2},{4,3},{5,4},{6,5},{7,6},{8,7},{9,8},{10,9... | collective-permute-start | bytes 516104 | tf_op jit(solution)/shard_map/ppermute | solution.py:848
  46.8 17.3 %all-to-all-start.2 = ((f32[128,1,512]{2,1,0:T(1,128)}), f32[128,1,512]{2,1,0:T(1,128)S(1)}, u32[]{:S(2)}, u32[]{:S(2)}) async-start(f32[128,1,512]{2,1,0:T(1,128)} %get-tuple-element.74), calls=%async_computation.2 | async-start | bytes 524288 | tf_op jit(solution)/shard_map/all_to_all | solution.py:899
